TPU v7x, 32 devices: a whole 2x2x4 slice. The times are simulated.
32 devices in a mesh: rep: 2 (over y), seq: 8 (over z, x), grp: 2 (over core).
Axes of the slice: x: 2, y: 2, z: 4, core: 2. Of those that a mesh axis runs over, the one named last changes fastest.
Arguments:
- hidden: bfloat16 [4352, 8192], P(('rep', 'seq'), 'grp'), parts along dimension 0, may hold values from -6 to 6
- proj: bfloat16 [3, 256, 8192], P(None, 'seq', 'grp'), may hold values from -0.0625 to 0.0625
- short_taps: float32 [3, 3, 256], P(None, None, 'grp'), may hold values from -4 to 4
- filters: float32 [16, 128], P('grp'), may hold values from -0.5 to 0.5
- grad_out: bfloat16 [4352, 256], P(('rep', 'seq'), 'grp'), parts along dimension 0, may hold values from -6 to 6
- var_pos: int32 [256], P(('rep', 'seq')), parts along dimension 0, may hold values from 0 to 2175, as said below
- alt_hidden: bfloat16 [256, 8192], P(('rep', 'seq'), 'grp'), parts along dimension 0, may hold values from -6 to 6
Outputs:
- attribution: float32 [4352], P(('rep', 'seq')), parts along dimension 0
- effect: float32 [256], P(('rep', 'seq')), parts along dimension 0
There are 2 independent parts, one for each index of `rep`. A program takes and returns all parts, laid end to end along the dimension named above; an argument that names none is the same for every part. Nothing has to cross between parts.
Inputs may be any that keep to these rules, and one draw needn't show every extreme that they name: `var_pos`: variants v of block j (j * 16 <= v < (j + 1) * 16) lie in tokens j * 272 to (j + 1) * 272 - 1; each block holds the first and the last of those tokens.
All inputs are finite; a program needn't handle non-finite values.
Results may differ from a plain program's by a relative error of at most 0.0028.
Values may be sent and summed in bfloat16 or wider, within the bound.
No kernel may reach another device: no remote copies, remote signals or barrier semaphores. Data moves between devices by JAX's collectives and lax.ppermute only.
A program may use at most 64 MiB of HBM per device.

v0:
```python
import jax
import jax.numpy as jnp
from jax import lax
from jax.sharding import PartitionSpec as P

D = 8192
GROUP = 16


def shifted(block, axis, distance):
    devices = range(lax.axis_size(axis))
    route = [(i - distance, i) for i in devices if i - distance in devices]
    return lax.ppermute(block, axis, route)


def causal_taps(source, taps, leading):
    tap_count = taps.shape[0]
    row_count = source.shape[0]
    extended = jnp.concatenate([leading, source], 0)
    summed = jnp.zeros(source.shape, jnp.float32)
    for offset in range(tap_count):
        begin = tap_count - 1 - offset
        summed = summed + taps[offset] * extended[begin : begin + row_count]
    return summed


def later_taps(source, taps, trailing):
    tap_count = taps.shape[0]
    row_count = source.shape[0]
    extended = jnp.concatenate([source, trailing], 0)
    summed = jnp.zeros(source.shape, jnp.float32)
    for offset in range(tap_count):
        summed = summed + taps[offset] * extended[offset : offset + row_count]
    return summed


def long_filter(extended, filters, row_count, later):
    filter_span = filters.shape[1]
    per_channel = jnp.repeat(filters, GROUP, axis=0).T

    def accumulate(block, summed):
        for inner in range(8):
            offset = block * 8 + inner
            begin = offset if later else filter_span - 1 - offset
            section = lax.dynamic_slice_in_dim(extended, begin, row_count, 0)
            summed = (
                summed + lax.dynamic_index_in_dim(per_channel, offset, 0, keepdims=False) * section
            )
        return summed

    return lax.fori_loop(
        0, filter_span // 8, accumulate, jnp.zeros((row_count, extended.shape[1]), jnp.float32)
    )


def per_device(hidden, proj, short_taps, filters, grad_out, var_pos, alt_hidden):
    row_count = hidden.shape[0]
    tap_count = short_taps.shape[0]
    filter_span = filters.shape[1]
    partial_feature = jnp.einsum(
        "td,fcd->tfc",
        hidden,
        lax.all_gather(proj, "seq", axis=1, tiled=True),
        preferred_element_type=jnp.float32,
    )
    feature = lax.psum_scatter(partial_feature, "grp", scatter_dimension=2, tiled=True)
    short_rim = shifted(feature[row_count - tap_count + 1 :], "seq", 1)
    mixed = causal_taps(feature, short_taps, short_rim)
    product = mixed[:, 1] * mixed[:, 2]
    prior_product = shifted(product[row_count - filter_span + 1 :], "seq", 1)
    queries = mixed[:, 0]
    filtered = long_filter(jnp.concatenate([prior_product, product], 0), filters, row_count, False)
    upstream = grad_out.astype(jnp.float32)
    back_queries = upstream * filtered
    back_filtered = upstream * queries
    next_filtered = shifted(back_filtered[: filter_span - 1], "seq", -1)
    back_product = long_filter(
        jnp.concatenate([back_filtered, next_filtered], 0), filters, row_count, True
    )
    back_mixed = jnp.stack(
        [back_queries, back_product * mixed[:, 2], back_product * mixed[:, 1]], 1
    )
    next_mixed = shifted(back_mixed[: tap_count - 1], "seq", -1)
    back_feature = later_taps(back_mixed, short_taps, next_mixed).astype(jnp.bfloat16)
    all_channels = lax.all_gather(back_feature, "grp", axis=2, tiled=True)
    panels_again = lax.all_gather(proj, "seq", axis=1, tiled=True)
    back_hidden = jnp.einsum(
        "tfc,fcd->td", all_channels, panels_again, preferred_element_type=jnp.float32
    )
    hidden_float = hidden.astype(jnp.float32)
    attribution_part = jnp.sum(back_hidden * hidden_float, 1)
    local_rows = var_pos - lax.axis_index("seq") * row_count
    picked = jnp.take(back_hidden, local_rows, axis=0)
    present = jnp.take(hidden_float, local_rows, axis=0)
    change = alt_hidden.astype(jnp.float32) - present
    effect_part = jnp.sum(picked * change, 1)
    attribution, effect = lax.psum((attribution_part, effect_part), "grp")
    factor = D ** (-0.5)
    return (attribution * factor, effect * factor)


def solution(mesh):
    in_specs = (
        P(("rep", "seq"), "grp"),
        P(None, "seq", "grp"),
        P(None, None, "grp"),
        P("grp", None),
        P(("rep", "seq"), "grp"),
        P(("rep", "seq")),
        P(("rep", "seq"), "grp"),
    )
    out_specs = (P(("rep", "seq")), P(("rep", "seq")))
    return jax.shard_map(
        per_device, mesh=mesh, in_specs=in_specs, out_specs=out_specs, check_vma=False
    )
```

profile of v0, /device:TPU:23, one launch (start us, length us, event | category | flops | bytes accessed | tf_op | source)
XLA Modules:
  0.0 181.5 jit_solution(11757446988338695483)
XLA Ops:
  7.2 0.0 all-gather.2.cloned.1.call-start
  7.2 0.7 all-gather.2.cloned.1.call-update
  7.9 0.0 copy-start.3
  7.9 0.0 reduce-scatter.2.cloned.1.call-start
  8.0 100.0 %all-gather.2.cloned.1.call-done = bf16[3,256,4096]{2,1,0:T(8,128)(2,1)} async-done(((bf16[3,32,4096]{2,1,0:T(8,128)(2,1)}), bf16[3,256,4096]{2,1,0:T(8,128)(2,1)}) %all-gather.2.cloned.1.call-update) | async-done | bytes 6291472 | tf_op jit(solution)/shard_map/all_gather | solution.py:63
  108.0 6.3 %fusion.30 = f32[272,3,256]{2,0,1:T(8,128)} fusion(bf16[3,256,4096]{2,1,0:T(8,128)(2,1)} %all-gather.2.cloned.1.call-done, bf16[272,4096]{1,0:T(8,128)(2,1)} %param.13), kind=kOutput, calls=%fused_computation.52 | convolution fusion | flops 1711276032 | bytes 9355264 | tf_op jit(solution)/shard_map/td,fcd->tfc/dot_general | solution.py:60
  114.4 0.0 reduce-scatter.2.cloned.1.call-update
  114.4 9.6 %reduce-scatter.2.cloned.1.call-done = f32[272,3,128]{2,0,1:T(8,128)} async-done(((f32[272,3,256]{2,0,1:T(8,128)}), f32[272,3,128]{2,0,1:T(8,128)}) %reduce-scatter.2.cloned.1.call-update) | async-done | bytes 417808 | tf_op jit(solution)/shard_map/reduce_scatter | solution.py:66
  124.0 0.7 slice.65
  124.7 3.1 %collective-permute-start = (f32[2,3,128]{2,0,1:T(2,128)S(1)}, f32[2,3,128]{2,0,1:T(2,128)S(1)}, u32[]{:S(2)}, u32[]{:S(2)}) collective-permute-start(f32[2,3,128]{2,0,1:T(2,128)S(1)} %slice.65), channel_id=1, source_target_pairs={{0,2},{2,4},{4,6},{6,8},{8,10},{10,12},{12,14},{1,3},{3,5},{5,7},{... | collective-permute-start | bytes 9224 | tf_op jit(solution)/shard_map/ppermute | solution.py:13
  127.8 1.2 collective-permute-done
  129.0 1.5 fusion.35
  130.6 3.1 %collective-permute-start.2 = (f32[127,128]{1,0:T(8,128)S(1)}, f32[127,128]{1,0:T(8,128)S(1)}, u32[]{:S(2)}, u32[]{:S(2)}) collective-permute-start(f32[127,128]{1,0:T(8,128)S(1)} %slice.72), channel_id=1, source_target_pairs={{2,0},{4,2},{6,4},{8,6},{10,8},{12,10},{14,12},{3,1},{5,3},{7,5},{... | collective-permute-start | bytes 195080 | tf_op jit(solution)/shard_map/ppermute | solution.py:13
  133.8 0.1 copy.10
  133.9 3.1 %collective-permute-start.1 = (f32[127,128]{1,0:T(8,128)S(1)}, f32[127,128]{1,0:T(8,128)S(1)}, u32[]{:S(2)}, u32[]{:S(2)}) collective-permute-start(f32[127,128]{1,0:T(8,128)S(1)} %slice.70), channel_id=1, source_target_pairs={{0,2},{2,4},{4,6},{6,8},{8,10},{10,12},{12,14},{1,3},{3,5},{5,7},{... | collective-permute-start | bytes 195080 | tf_op jit(solution)/shard_map/ppermute | solution.py:13
  137.0 0.0 collective-permute-done.2
  137.0 5.7 %while.34 = (s32[]{:T(128)}, f32[272,128]{1,0:T(8,128)S(1)}, f32[128,128]{1,0:T(8,128)S(1)}, f32[399,128]{1,0:T(8,128)S(1)}, s32[]{:T(128)}, /*index=5*/s32[]{:T...) while((s32[]{:T(128)}, f32[272,128]{1,0:T(8,128)S(1)}, ...), condition=%wide.region_4.5_spmd.clone, body=%wide.region_3.4_spmd.clone.sunk | while | flops 591923 | bytes 1405823 | solution.py:51
  137.2 0.2 fusion.54
  137.6 0.2 fusion.54
  137.9 0.2 fusion.54
  138.3 0.2 fusion.54
  138.6 0.2 fusion.54
  139.0 0.2 fusion.54
  139.3 0.2 fusion.54
  139.7 0.2 fusion.54
  140.1 0.2 fusion.54
  140.4 0.2 fusion.54
  140.8 0.2 fusion.54
  141.1 0.2 fusion.54
  141.5 0.2 fusion.54
  141.8 0.2 fusion.54
  142.2 0.2 fusion.54
  142.5 0.2 fusion.54
  142.8 0.0 collective-permute-done.1
  142.8 0.0 copy-start
  142.8 5.8 %while.33 = (s32[]{:T(128)}, f32[272,128]{1,0:T(8,128)S(1)}, f32[128,128]{1,0:T(8,128)S(1)}, f32[399,128]{1,0:T(8,128)S(1)}, s32[]{:T(128)}, /*index=5*/s32[]{:T...) while((s32[]{:T(128)}, f32[272,128]{1,0:T(8,128)S(1)}, ...), condition=%wide.region_2.3_spmd.clone, body=%wide.region_1.2_spmd.clone.sunk | while | flops 591939 | bytes 1405943 | solution.py:51
  143.0 0.2 fusion.52
  143.4 0.2 fusion.52
  143.7 0.2 fusion.52
  144.1 0.2 fusion.52
  144.4 0.2 fusion.52
  144.8 0.2 fusion.52
  145.2 0.2 fusion.52
  145.5 0.2 fusion.52
  145.9 0.2 fusion.52
  146.2 0.2 fusion.52
  146.6 0.2 fusion.52
  147.0 0.2 fusion.52
  147.3 0.2 fusion.52
  147.7 0.2 fusion.52
  148.1 0.2 fusion.52
  148.4 0.2 fusion.52
  148.7 2.2 %collective-permute-start.3 = (f32[2,3,128]{2,0,1:T(2,128)S(1)}, f32[2,3,128]{2,0,1:T(2,128)S(1)}, u32[]{:S(2)}, u32[]{:S(2)}) collective-permute-start(f32[2,3,128]{2,0,1:T(2,128)S(1)} %slice.73), channel_id=1, source_target_pairs={{2,0},{4,2},{6,4},{8,6},{10,8},{12,10},{14,12},{3,1},{5,3},{7,5},{... | collective-permute-start | bytes 9224 | tf_op jit(solution)/shard_map/ppermute | solution.py:13
  150.9 2.7 %convert_element_type.14 = f32[272,4096]{1,0:T(8,128)} convert(bf16[272,4096]{1,0:T(8,128)(2,1)S(1)} %copy-done) | non-fusion elementwise | flops 1114112 | bytes 6684672 | tf_op jit(solution)/shard_map/convert_element_type | solution.py:90
  153.6 3.0 %gather_fusion.1 = f32[16,4096]{1,0:T(8,128)S(1)} fusion(f32[272,4096]{1,0:T(8,128)} %convert_element_type.14, s32[1024]{0:T(1024)S(1)} %pad_clamp_fusion), kind=kCustom, calls=%fused_computation.1.clone | custom fusion | bytes 524352 | tf_op jit(solution)/shard_map/jit(_take)/gather | solution.py:94
  156.6 0.0 collective-permute-done.3
  156.6 0.2 fusion.37
  156.8 4.0 %all_gather.8 = bf16[272,3,256]{2,0,1:T(8,128)(2,1)S(1)} all-gather(bf16[272,3,128]{2,0,1:T(8,128)(2,1)S(1)} %fusion.37), channel_id=1, replica_groups=mesh['rep'=2,'seq'=8,'grp'=2] {'grp'}, dimensions={2}, use_global_device_ids=true | all-gather | bytes 626688 | tf_op jit(solution)/shard_map/all_gather | solution.py:85
  160.8 7.0 %multiply_reduce_fusion = (f32[272]{0:T(512)S(1)}, f32[272,4096]{1,0:T(8,128)}) fusion(bf16[272,4096]{1,0:T(8,128)(2,1)S(1)} %copy-done, bf16[272,3,256]{2,0,1:T(8,128)(2,1)S(1)} %all_gather.8, bf16[3,256,4096]{2,1,0:T(8,128)(2,1)} %all-gather.2.cloned.1.call-done), kind=kOutput, calls=%fused_computation.51 | convolution fusion | flops 1714618112 | bytes 13395008 | tf_op jit(solution)/shard_map/tfc,fcd->td/dot_general | solution.py:87
  167.8 3.0 %gather_fusion = f32[16,4096]{1,0:T(8,128)S(1)} fusion(f32[272,4096]{1,0:T(8,128)} %get-tuple-element.361, s32[1024]{0:T(1024)S(1)} %pad_clamp_fusion), kind=kCustom, calls=%fused_computation.clone | custom fusion | bytes 524352 | tf_op jit(solution)/shard_map/jit(_take)/gather | solution.py:93
  170.8 0.2 fusion.41
  171.1 2.5 %all-reduce = (f32[272]{0:T(512)S(1)}, f32[16]{0:T(128)S(1)}) all-reduce(f32[272]{0:T(512)S(1)} %get-tuple-element.360, f32[16]{0:T(128)S(1)} %fusion.41), channel_id=1, replica_groups=mesh['rep'=2,'seq'=8,'grp'=2] {'grp'}, use_global_device_ids=true, to_apply=%region_6.7 | all-reduce | flops 288 | bytes 2304 | tf_op jit(solution)/shard_map/psum | solution.py:97
  173.6 0.6 broadcast_multiply_fusion
  174.1 0.5 broadcast_multiply_fusion.1
  (58 shorter events, 1.2 us)
Async XLA Ops:
  7.2 100.9 %all-gather.2.cloned.1.call-start = ((), (), s32[]{:S(2)}) async-start(), calls=%async_computation.1 | async-start | bytes 7077888 | tf_op jit(solution)/shard_map/all_gather | solution.py:63
  7.9 119.9 %copy-start.3 = (f32[3,3,128]{2,1,0:T(4,128)S(1)}, f32[3,3,128]{2,1,0:T(4,128)}, u32[]{:S(2)}) copy-start(f32[3,3,128]{2,1,0:T(4,128)} %param.15) | copy-start | bytes 13828
  7.9 122.7 %copy-start.1 = (bf16[272,128]{1,0:T(8,128)(2,1)S(1)}, bf16[272,128]{1,0:T(8,128)(2,1)}, u32[]{:S(2)}) copy-start(bf16[272,128]{1,0:T(8,128)(2,1)} %param.17) | copy-start | bytes 208900
  7.9 125.8 %copy-start.5 = (s32[16]{0:T(128)S(1)}, s32[16]{0:T(128)}, u32[]{:S(2)}) copy-start(s32[16]{0:T(128)} %param.18) | copy-start | bytes 196
  7.9 125.8 %copy-start.4 = (f32[8,128]{1,0:T(8,128)S(1)}, f32[8,128]{1,0:T(8,128)}, u32[]{:S(2)}) copy-start(f32[8,128]{1,0:T(8,128)} %param.16) | copy-start | bytes 12292
  7.9 116.0 %reduce-scatter.2.cloned.1.call-start = ((), (), s32[]{:S(2)}) async-start(), calls=%async_computation.2 | async-start | bytes 1253376 | tf_op jit(solution)/shard_map/reduce_scatter | solution.py:66
  124.7 4.3 %collective-permute-start = (f32[2,3,128]{2,0,1:T(2,128)S(1)}, f32[2,3,128]{2,0,1:T(2,128)S(1)}, u32[]{:S(2)}, u32[]{:S(2)}) collective-permute-start(f32[2,3,128]{2,0,1:T(2,128)S(1)} %slice.65), channel_id=1, source_target_pairs={{0,2},{2,4},{4,6},{6,8},{8,10},{10,12},{12,14},{1,3},{3,5},{5,7},{... | collective-permute-start | bytes 9224 | tf_op jit(solution)/shard_map/ppermute | solution.py:13
  130.6 6.4 %collective-permute-start.2 = (f32[127,128]{1,0:T(8,128)S(1)}, f32[127,128]{1,0:T(8,128)S(1)}, u32[]{:S(2)}, u32[]{:S(2)}) collective-permute-start(f32[127,128]{1,0:T(8,128)S(1)} %slice.72), channel_id=1, source_target_pairs={{2,0},{4,2},{6,4},{8,6},{10,8},{12,10},{14,12},{3,1},{5,3},{7,5},{... | collective-permute-start | bytes 195080 | tf_op jit(solution)/shard_map/ppermute | solution.py:13
  133.9 8.9 %collective-permute-start.1 = (f32[127,128]{1,0:T(8,128)S(1)}, f32[127,128]{1,0:T(8,128)S(1)}, u32[]{:S(2)}, u32[]{:S(2)}) collective-permute-start(f32[127,128]{1,0:T(8,128)S(1)} %slice.70), channel_id=1, source_target_pairs={{0,2},{2,4},{4,6},{6,8},{8,10},{10,12},{12,14},{1,3},{3,5},{5,7},{... | collective-permute-start | bytes 195080 | tf_op jit(solution)/shard_map/ppermute | solution.py:13
  142.8 8.1 %copy-start = (bf16[272,4096]{1,0:T(8,128)(2,1)S(1)}, bf16[272,4096]{1,0:T(8,128)(2,1)}, u32[]{:S(2)}) copy-start(bf16[272,4096]{1,0:T(8,128)(2,1)} %param.13) | copy-start | bytes 6684676
  148.7 7.9 %collective-permute-start.3 = (f32[2,3,128]{2,0,1:T(2,128)S(1)}, f32[2,3,128]{2,0,1:T(2,128)S(1)}, u32[]{:S(2)}, u32[]{:S(2)}) collective-permute-start(f32[2,3,128]{2,0,1:T(2,128)S(1)} %slice.73), channel_id=1, source_target_pairs={{2,0},{4,2},{6,4},{8,6},{10,8},{12,10},{14,12},{3,1},{5,3},{7,5},{... | collective-permute-start | bytes 9224 | tf_op jit(solution)/shard_map/ppermute | solution.py:13
  160.8 10.0 %copy-start.2 = (bf16[16,4096]{1,0:T(8,128)(2,1)S(1)}, bf16[16,4096]{1,0:T(8,128)(2,1)}, u32[]{:S(2)}) copy-start(bf16[16,4096]{1,0:T(8,128)(2,1)} %param.19) | copy-start | bytes 393220
Sparse Core Ops, SparseCore 0:
  10.2 97.8 all-gather.1
  114.5 9.4 reduce-scatter.1
where the time goes:
time: 183 us; the launch traced here: 181 us
  waiting for transfers between devices  112 us (61%)
  between operations  14.3 us (8%)
  matrix products  13.3 us (7%)
  other arithmetic  11.7 us (6%)
  starting transfers between devices  11.5 us (6%)
  local copies, waits for them, and re-layouts  7.86 us (4%)
  blocking collectives  6.51 us (4%)
  loops' own time  4.69 us (3%)
    all_gather x1, waiting for transfers between devices, per_device(): lax.all_gather(proj, 'seq', axis=1, tiled=True)  100 us
    ppermute x4, starting transfers between devices, shifted(): return lax.ppermute(block, axis, route)  11.4 us
    reduce_scatter x1, waiting for transfers between devices, per_device(): lax.psum_scatter(partial_feature, 'grp', scatter_dimension=2, tiled=True)  9.6 us
    dot_general x1, matrix products, per_device(): jnp.einsum('tfc,fcd->td', all_channels, panels_again, preferred_element_t...  6.99 us
    dot_general x1, matrix products, per_device(): jnp.einsum('td,fcd->tfc', hidden, lax.all_gather(proj, 'seq', axis=1, til...  6.32 us
    add x32, other arithmetic, accumulate(): summed + lax.dynamic_index_in_dim(per_channel, offset, 0, keepdims=False)...  5.8 us
    another operation x2, loops' own time, long_filter(): lax.fori_loop(0, filter_span // 8, accumulate, jnp.zeros((row_count, exte...  4.69 us
    all_gather x1, blocking collectives, per_device(): all_channels = lax.all_gather(back_feature, 'grp', axis=2, tiled=True)  4.02 us
  transfers between devices with their start and end apart: 6, of which 3 were waited for; matrix products, arithmetic and copies ran while one was open for 5% of the time, Pallas kernels for 0%

commit v1 on v0

v1 whole, which is shorter than its diff:
```python
import jax
import jax.numpy as jnp
from jax import lax
from jax.experimental import pallas as pl
from jax.experimental.pallas import tpu as pltpu
from jax.sharding import PartitionSpec as P

D = 8192
GROUP = 16
EDGE = 8


def shifted(block, axis, distance):
    devices = range(lax.axis_size(axis))
    route = [(i - distance, i) for i in devices if i - distance in devices]
    return lax.ppermute(block, axis, route)


def swapped(block, axis):
    return lax.ppermute(block, axis, [(0, 1), (1, 0)])


def mixer_kernel(
    rows, reach, picks, feature, before, after, grad, grad_after, taps, filters, out,
    query, key, value, product, back_filtered, grads, summed,
):
    span = filters.shape[0]
    variants = picks.shape[0]
    ahead = rows + EDGE
    query[:EDGE] = before[2 * reach :]
    query[EDGE : EDGE + rows] = feature[0, :rows]
    query[EDGE + rows :] = after[:reach]
    for index, extended in ((1, key), (2, value)):
        extended[:reach] = before[(index - 1) * reach : index * reach]
        extended[reach : reach + rows] = feature[index, :rows]
        extended[reach + rows :] = after[reach + (index - 1) * EDGE : reach + index * EDGE]

    def tap(offset, index):
        return taps[offset * 3 + index : offset * 3 + index + 1, :]

    def mixed(extended, index, begin, count):
        total = tap(0, index) * extended[begin : begin + count]
        for offset in (1, 2):
            total = total + tap(offset, index) * extended[begin - offset : begin - offset + count]
        return total

    shift = reach - span
    product[...] = mixed(key, 1, shift, span + ahead) * mixed(value, 2, shift, span + ahead)
    back_filtered[:rows] = grad[...].astype(jnp.float32) * mixed(query, 0, EDGE, rows)
    back_filtered[rows:] = grad_after[...].astype(jnp.float32) * mixed(
        query, 0, EDGE + rows, reach
    )

    def long_filter(source, later):
        def accumulate(block, total):
            for inner in range(8):
                offset = block * 8 + inner
                begin = offset if later else span - offset
                total = total + filters[pl.ds(offset, 1), :] * source[pl.ds(begin, ahead), :]
            return total

        return lax.fori_loop(
            0, span // 8, accumulate, jnp.zeros((ahead, filters.shape[1]), jnp.float32)
        )

    filtered = long_filter(product, False)
    grads[0, :rows] = grad[...].astype(jnp.float32) * filtered[:rows]
    grads[0, rows:] = grad_after[:EDGE].astype(jnp.float32) * filtered[rows:]
    back_product = long_filter(back_filtered, True)
    grads[1] = back_product * mixed(value, 2, reach, ahead)
    grads[2] = back_product * mixed(key, 1, reach, ahead)
    total = jnp.zeros((rows, filters.shape[1]), jnp.float32)
    for index in range(3):
        back = tap(0, index) * grads[index, :rows]
        for offset in (1, 2):
            back = back + tap(offset, index) * grads[index, offset : offset + rows]
        back = back.astype(jnp.bfloat16).astype(jnp.float32)
        grads[index, :rows] = back
        total = total + back * feature[index, :rows]
    summed[:rows] = total
    for variant in range(variants):
        at = picks[variant]
        change = jnp.zeros((1, filters.shape[1]), jnp.float32)
        for index in range(3):
            alternate = feature[index, rows + variant : rows + variant + 1]
            present = feature[index, pl.ds(at, 1)]
            change = change + grads[index, pl.ds(at, 1)] * (alternate - present)
        summed[rows + variant : rows + variant + 1] = change
    out[...] = lax.dot_general(
        jnp.ones((8, filters.shape[1]), jnp.float32),
        summed[...],
        (((1,), (1,)), ((), ())),
        precision=lax.Precision.HIGHEST,
        preferred_element_type=jnp.float32,
    )


def mixer(picks, feature, before, after, grad, grad_after, taps, filters):
    rows, lanes = grad.shape
    reach = grad_after.shape[0]
    span = filters.shape[0]
    count = feature.shape[1]

    def body(*refs):
        mixer_kernel(rows, reach, *refs)

    vmem = pl.BlockSpec(memory_space=pltpu.VMEM)
    return pl.pallas_call(
        body,
        out_shape=jax.ShapeDtypeStruct((8, count), jnp.float32),
        in_specs=[pl.BlockSpec(memory_space=pltpu.SMEM)] + [vmem] * 7,
        out_specs=vmem,
        scratch_shapes=[
            pltpu.VMEM((EDGE + rows + reach, lanes), jnp.float32),
            pltpu.VMEM((reach + rows + EDGE, lanes), jnp.float32),
            pltpu.VMEM((reach + rows + EDGE, lanes), jnp.float32),
            pltpu.VMEM((span + rows + EDGE, lanes), jnp.float32),
            pltpu.VMEM((rows + reach, lanes), jnp.float32),
            pltpu.VMEM((3, rows + EDGE, lanes), jnp.float32),
            pltpu.VMEM((count, lanes), jnp.float32),
        ],
        name="mixer",
    )(picks, feature, before, after, grad, grad_after, taps, filters)


def per_device(hidden, proj, short_taps, filters, grad_out, var_pos, alt_hidden):
    rows = hidden.shape[0]
    lanes = grad_out.shape[1]
    reach = filters.shape[1] + EDGE
    rep, half = lax.axis_index("rep"), lax.axis_index("grp")
    parts = lax.axis_size("rep")
    width = hidden.shape[1] // parts

    tokens = jnp.concatenate([hidden, alt_hidden], 0)
    theirs = swapped(lax.dynamic_slice_in_dim(tokens, (1 - rep) * width, width, 1), "rep")
    panels = lax.all_gather(
        lax.dynamic_slice_in_dim(proj, rep * width, width, 2), "seq", axis=1, tiled=True
    )
    ours = lax.dynamic_slice_in_dim(tokens, rep * width, width, 1)
    grad_after = shifted(grad_out[:reach], "seq", -1)
    per_channel = jnp.repeat(filters, GROUP, axis=0).T
    picks = var_pos - lax.axis_index("seq") * rows

    both = jnp.concatenate([ours, theirs], 0)
    partial = jnp.einsum("td,fcd->ftc", both, panels, preferred_element_type=jnp.float32)
    keep = lax.dynamic_slice_in_dim(partial, half * lanes, lanes, 2)
    give = lax.dynamic_slice_in_dim(partial, (1 - half) * lanes, lanes, 2)
    chip = keep + swapped(give, "grp")
    count = tokens.shape[0]
    feature = chip[:, :count] + swapped(chip[:, count:], "rep")

    before = shifted(
        jnp.concatenate(
            [
                feature[1, rows - reach : rows],
                feature[2, rows - reach : rows],
                feature[0, rows - EDGE : rows],
            ],
            0,
        ),
        "seq",
        1,
    )
    after = shifted(
        jnp.concatenate([feature[0, :reach], feature[1, :EDGE], feature[2, :EDGE]], 0), "seq", -1
    )
    scores = mixer(
        picks, feature, before, after, grad_out, grad_after,
        short_taps.reshape(9, lanes), per_channel,
    )[0]
    scores = lax.psum(scores, "grp") * D ** (-0.5)
    return scores[:rows], scores[rows:]


def solution(mesh):
    in_specs = (
        P(("rep", "seq"), "grp"),
        P(None, "seq", "grp"),
        P(None, None, "grp"),
        P("grp", None),
        P(("rep", "seq"), "grp"),
        P(("rep", "seq")),
        P(("rep", "seq"), "grp"),
    )
    out_specs = (P(("rep", "seq")), P(("rep", "seq")))
    return jax.shard_map(
        per_device, mesh=mesh, in_specs=in_specs, out_specs=out_specs, check_vma=False
    )
```

time: 183 us -> 121 us (0.66)
  waiting for transfers between devices: 112 us -> 68.6 us
  other arithmetic: 11.7 us -> 1.87 us
  matrix products: 13.3 us -> 4.6 us
  Pallas kernels: 0 us -> 6.12 us
  loops' own time: 4.69 us -> 0 us
  blocking collectives: 6.51 us -> 4.49 us
    all_gather x1, waiting for transfers between devices: 100 us -> 30.5 us  [per_device(): lax.all_gather(lax.dynamic_slice_in_dim(proj, rep * width, width, 2), 'se...]
    ppermute x0 -> x3, waiting for transfers between devices: none -> 36.9 us  [swapped(): return lax.ppermute(block, axis, [(0, 1), (1, 0)])]
    reduce_scatter x1 -> x0, waiting for transfers between devices: 9.6 us -> none  [per_device(): lax.psum_scatter(partial_feature, 'grp', scatter_dimension=2, tiled=True)]
    dot_general x2 -> x1, matrix products: 13.3 us -> 4.6 us  [per_device(): jnp.einsum('td,fcd->ftc', both, panels, preferred_element_type=jnp.float32)]
    pallas_call x0 -> x1, Pallas kernels: none -> 6.12 us  [mixer(): pl.pallas_call(body, out_shape=jax.ShapeDtypeStruct((8, count), jnp.float...]
    gather x2 -> x0, local copies, waits for them, and re-layouts: 6.02 us -> none  [the longest x1 3.01 us: per_device(): present = jnp.take(hidden_float, local_rows, axis=0)]
    add x33 -> x2, other arithmetic: 7.34 us -> 1.33 us  [the longest x1 1.28 us: per_device(): chip = keep + swapped(give, 'grp')]
    another operation x2 -> x0, loops' own time: 4.69 us -> none  [long_filter(): lax.fori_loop(0, filter_span // 8, accumulate, jnp.zeros((row_count, exte...]
  transfers between devices with their start and end apart: 6 -> 7, of which waited for: 3 -> 5; matrix products, arithmetic and copies ran while one was open for 5% -> 4% of each run, Pallas kernels for 0% -> 0%
where the time goes in v1:
time: 121 us; the launch traced here: 120 us
  waiting for transfers between devices  68.6 us (57%)
  between operations  14.2 us (12%)
  starting transfers between devices  11.3 us (9%)
  local copies, waits for them, and re-layouts  8.37 us (7%)
  Pallas kernels  6.12 us (5%)
  matrix products  4.6 us (4%)
  blocking collectives  4.49 us (4%)
  other arithmetic  1.87 us (2%)
    ppermute x3, waiting for transfers between devices, swapped(): return lax.ppermute(block, axis, [(0, 1), (1, 0)])  36.9 us
    all_gather x1, waiting for transfers between devices, per_device(): lax.all_gather(lax.dynamic_slice_in_dim(proj, rep * width, width, 2), 'se...  30.5 us
    ppermute x3, starting transfers between devices, shifted(): return lax.ppermute(block, axis, route)  9.28 us
    pallas_call x1, Pallas kernels, mixer(): pl.pallas_call(body, out_shape=jax.ShapeDtypeStruct((8, count), jnp.float...  6.12 us
    dot_general x1, matrix products, per_device(): jnp.einsum('td,fcd->ftc', both, panels, preferred_element_type=jnp.float32)  4.6 us
    psum x1, blocking collectives, per_device(): scores = lax.psum(scores, 'grp') * D ** (-0.5)  4.49 us
    unnamed x23, local copies, waits for them, and re-layouts  3.56 us
  transfers between devices with their start and end apart: 7, of which 5 were waited for; matrix products, arithmetic and copies ran while one was open for 4% of the time, Pallas kernels for 0%

profile of v1, /device:TPU:23, one launch (start us, length us, event | category | flops | bytes accessed | tf_op | source)
XLA Modules:
  0.0 119.5 jit_solution(9218001904727796009)
XLA Ops:
  7.2 0.0 copy-start
  7.2 0.0 all-gather.2.cloned.1.call-start
  7.2 1.1 copy-done
  8.3 0.8 constant_dynamic-slice_fusion.2
  9.1 0.0 copy-start.4
  9.1 0.0 all-gather.2.cloned.1.call-update
  9.1 1.8 %constant_dynamic-update-slice_fusion.1 = bf16[288,4096]{1,0:T(8,128)(2,1)S(1)} fusion(bf16[272,4096]{1,0:T(8,128)(2,1)} %param.7), kind=kLoop, calls=%fused_computation.13 | loop fusion | bytes 4456448
  10.9 0.0 copy-done.4
  10.9 1.3 %constant_dynamic-slice_fusion.1 = (bf16[288,2048]{1,0:T(8,128)(2,1)}, bf16[288,2048]{1,0:T(8,128)(2,1)S(1)}) fusion(bf16[288,4096]{1,0:T(8,128)(2,1)S(1)} %constant_dynamic-update-slice_fusion, s32[]{:T(128)S(6)} %select_n.13, s32[]{:T(128)S(6)} %select_n.14), kind=kLoop, calls=%fused_computation.19 | loop fusion | bytes 4718600 | tf_op jit(solution)/shard_map/dynamic_slice | solution.py:139
  12.2 0.2 collective-permute-start
  12.4 26.7 %collective-permute-done = bf16[288,2048]{1,0:T(8,128)(2,1)} collective-permute-done((bf16[288,2048]{1,0:T(8,128)(2,1)S(1)}, bf16[288,2048]{1,0:T(8,128)(2,1)}, u32[]{:S(2)}, u32[]{:S(2)}) %collective-permute-start) | collective-permute-done | bytes 1179680 | tf_op jit(solution)/shard_map/ppermute | solution.py:20
  39.1 30.5 %all-gather.2.cloned.1.call-done = bf16[3,256,2048]{2,1,0:T(8,128)(2,1)} async-done(((bf16[3,32,2048]{2,1,0:T(8,128)(2,1)}), bf16[3,256,2048]{2,1,0:T(8,128)(2,1)}) %all-gather.2.cloned.1.call-update) | async-done | bytes 3145744 | tf_op jit(solution)/shard_map/all_gather | solution.py:136
  69.7 4.6 %fusion = f32[3,256,576]{1,2,0:T(8,128)S(1)} fusion(bf16[3,256,2048]{2,1,0:T(8,128)(2,1)} %all-gather.2.cloned.1.call-done, bf16[288,2048]{1,0:T(8,128)(2,1)} %collective-permute-done, bf16[288,2048]{1,0:T(8,128)(2,1)} %get-tuple-element.2), kind=kOutput, calls=%fused_computation.1 | convolution fusion | flops 1816657920 | bytes 7274496 | tf_op jit(solution)/shard_map/td,fcd->ftc/dot_general | solution.py:145
  74.3 0.0 copy-start.2
  74.3 0.1 dynamic-slice_bitcast_fusion
  74.4 1.4 %collective-permute-start.1 = (f32[3,576,128]{2,1,0:T(8,128)S(1)}, f32[3,576,128]{2,1,0:T(8,128)}, u32[]{:S(2)}, u32[]{:S(2)}) collective-permute-start(f32[3,576,128]{2,1,0:T(8,128)S(1)} %dynamic-slice_bitcast_fusion), channel_id=1, source_target_pairs={{0,1},{1,0},{2,3},{3,2},{4,5},{5,4},{6,7},{7,6},{8,9},{9,8},{10,11... | collective-permute-start | bytes 2654216 | tf_op jit(solution)/shard_map/ppermute | solution.py:20
  75.8 0.0 copy-start.10
  75.8 0.0 copy-start.8
  75.8 0.0 copy-start.7
  75.8 2.2 %collective-permute-done.1 = f32[3,576,128]{2,1,0:T(8,128)} collective-permute-done((f32[3,576,128]{2,1,0:T(8,128)S(1)}, f32[3,576,128]{2,1,0:T(8,128)}, u32[]{:S(2)}, u32[]{:S(2)}) %collective-permute-start.1) | collective-permute-done | bytes 884768 | tf_op jit(solution)/shard_map/ppermute | solution.py:20
  78.0 1.3 %bitcast_add_fusion = f32[3,576,128]{2,1,0:T(8,128)S(1)} fusion(f32[3,576,128]{2,1,0:T(8,128)} %collective-permute-done.1, f32[3,256,576]{1,2,0:T(8,128)S(1)} %fusion, s32[]{:T(128)S(6)} %select_n.15), kind=kLoop, calls=%fused_computation.4 | loop fusion | flops 221184 | bytes 2654212 | tf_op jit(solution)/shard_map/add | solution.py:148
  79.3 0.3 collective-permute-start.2
  79.6 0.0 copy-done.2
  79.7 3.1 %collective-permute-start.5 = (bf16[136,128]{1,0:T(8,128)(2,1)S(1)}, bf16[136,128]{1,0:T(8,128)(2,1)S(1)}, u32[]{:S(2)}, u32[]{:S(2)}) collective-permute-start(bf16[136,128]{1,0:T(8,128)(2,1)S(1)} %slice.44), channel_id=1, source_target_pairs={{2,0},{4,2},{6,4},{8,6},{10,8},{12,10},{14,12},{3,1},{5,3},{7,5},{... | collective-permute-start | bytes 104456 | tf_op jit(solution)/shard_map/ppermute | solution.py:16
  82.8 8.0 %collective-permute-done.2 = f32[3,288,128]{2,1,0:T(8,128)S(1)} collective-permute-done((f32[3,288,128]{2,1,0:T(8,128)S(1)}, f32[3,288,128]{2,1,0:T(8,128)S(1)}, u32[]{:S(2)}, u32[]{:S(2)}) %collective-permute-start.2) | collective-permute-done | bytes 442400 | tf_op jit(solution)/shard_map/ppermute | solution.py:20
  90.8 0.0 copy-start.1
  90.9 3.1 %collective-permute-start.4 = (f32[152,128]{1,0:T(8,128)S(1)}, f32[152,128]{1,0:T(8,128)S(1)}, u32[]{:S(2)}, u32[]{:S(2)}) collective-permute-start(f32[152,128]{1,0:T(8,128)S(1)} %pad_maximum_fusion.1), channel_id=1, source_target_pairs={{2,0},{4,2},{6,4},{8,6},{10,8},{12,10},{14,12},{3,1},{5,3},{7,5},{... | collective-permute-start | bytes 233480 | tf_op jit(solution)/shard_map/ppermute | solution.py:16
  94.0 3.1 %collective-permute-start.3 = (f32[280,128]{1,0:T(8,128)S(1)}, f32[280,128]{1,0:T(8,128)S(1)}, u32[]{:S(2)}, u32[]{:S(2)}) collective-permute-start(f32[280,128]{1,0:T(8,128)S(1)} %pad_maximum_fusion), channel_id=1, source_target_pairs={{0,2},{2,4},{4,6},{6,8},{8,10},{10,12},{12,14},{1,3},{3,5},{5,7},{... | collective-permute-start | bytes 430088 | tf_op jit(solution)/shard_map/ppermute | solution.py:16
  97.1 0.0 copy-done.10
  97.1 0.5 broadcast_subtract_fusion.refs_0_
  97.6 0.0 copy-done.8
  97.7 0.7 copy.10
  98.4 0.0 copy-done.7
  98.4 0.6 reshape.10.refs_6_
  99.0 0.0 collective-permute-done.5.refs_5_
  99.0 0.0 copy-start.6
  99.0 0.0 collective-permute-done.4.refs_3_
  99.0 0.0 copy-start.5
  99.0 1.1 collective-permute-done.3.refs_2_
  100.1 0.0 copy-start.3
  100.1 0.0 copy-done.1
  100.1 0.0 copy-done.6
  100.1 0.0 copy-done.5
  100.1 0.6 copy-done.3
  100.8 6.1 %mixer.1 = f32[8,288]{1,0:T(8,128)} custom-call(s32[16]{0:T(128)} %broadcast_subtract_fusion.refs_0_, f32[3,288,128]{2,1,0:T(8,128)} %copy-done.1, f32[280,128]{1,0:T(8,128)} %copy-done.3, f32[152,128]{1,0:T(8,128)} %copy-done.5, bf16[272,128]{1,0:T(8,128)(2,1)} %refs_4_.1, bf16[136,128]{1,0:T(8,128)(2,1)} %copy-done.6, f32[9,128]{1,0:T(8,128)} %reshape.10.refs_6_, ...), custom_call_target="tpu_custom_call" | custom-call | tf_op jit(solution)/shard_map/mixer/pallas_call | solution.py:108
  106.9 0.7 slice_reduce_fusion
  107.6 4.5 %psum.7 = f32[288]{0:T(512)S(1)} all-reduce(f32[288]{0:T(512)S(1)} %slice_reduce_fusion), channel_id=1, replica_groups=mesh['rep'=2,'seq'=8,'grp'=2] {'grp'}, use_global_device_ids=true, to_apply=%region_0.0 | all-reduce | flops 288 | bytes 2304 | tf_op jit(solution)/shard_map/psum | solution.py:171
  112.1 0.0 copy-start.9
  112.1 0.6 slice.47
  112.7 0.0 copy-done.9
  (10 shorter events, 0.1 us)
Async XLA Ops:
  7.2 1.1 copy-start
  7.2 62.5 %all-gather.2.cloned.1.call-start = ((), (), s32[]{:S(2)}) async-start(), calls=%async_computation | async-start | bytes 3538944 | tf_op jit(solution)/shard_map/all_gather | solution.py:136
  9.1 1.8 %copy-start.4 = (bf16[16,4096]{1,0:T(8,128)(2,1)S(1)}, bf16[16,4096]{1,0:T(8,128)(2,1)}, u32[]{:S(2)}) copy-start(bf16[16,4096]{1,0:T(8,128)(2,1)} %param.13) | copy-start | bytes 393220
  12.2 26.9 %collective-permute-start = (bf16[288,2048]{1,0:T(8,128)(2,1)S(1)}, bf16[288,2048]{1,0:T(8,128)(2,1)}, u32[]{:S(2)}, u32[]{:S(2)}) collective-permute-start(bf16[288,2048]{1,0:T(8,128)(2,1)S(1)} %get-tuple-element.3), channel_id=1, source_target_pairs={{0,16},{16,0},{1,17},{17,1},{2,18},{18,2},{3,19},{19,3},{4,20},{20... | collective-permute-start | bytes 3538952 | tf_op jit(solution)/shard_map/ppermute | solution.py:20
  74.3 5.4 %copy-start.2 = (bf16[272,128]{1,0:T(8,128)(2,1)S(1)}, bf16[272,128]{1,0:T(8,128)(2,1)}, u32[]{:S(2)}) copy-start(bf16[272,128]{1,0:T(8,128)(2,1)} %refs_4_.1) | copy-start | bytes 208900
  74.4 3.6 %collective-permute-start.1 = (f32[3,576,128]{2,1,0:T(8,128)S(1)}, f32[3,576,128]{2,1,0:T(8,128)}, u32[]{:S(2)}, u32[]{:S(2)}) collective-permute-start(f32[3,576,128]{2,1,0:T(8,128)S(1)} %dynamic-slice_bitcast_fusion), channel_id=1, source_target_pairs={{0,1},{1,0},{2,3},{3,2},{4,5},{5,4},{6,7},{7,6},{8,9},{9,8},{10,11... | collective-permute-start | bytes 2654216 | tf_op jit(solution)/shard_map/ppermute | solution.py:20
  75.8 21.3 %copy-start.10 = (s32[16]{0:T(128)S(1)}, s32[16]{0:T(128)}, u32[]{:S(2)}) copy-start(s32[16]{0:T(128)} %param.12) | copy-start | bytes 196
  75.8 21.8 %copy-start.8 = (f32[8,128]{1,0:T(8,128)S(1)}, f32[8,128]{1,0:T(8,128)}, u32[]{:S(2)}) copy-start(f32[8,128]{1,0:T(8,128)} %param.10) | copy-start | bytes 12292
  75.8 22.6 %copy-start.7 = (f32[3,3,128]{2,1,0:T(4,128)S(1)}, f32[3,3,128]{2,1,0:T(4,128)}, u32[]{:S(2)}) copy-start(f32[3,3,128]{2,1,0:T(4,128)} %param.9) | copy-start | bytes 13828
  79.3 11.5 %collective-permute-start.2 = (f32[3,288,128]{2,1,0:T(8,128)S(1)}, f32[3,288,128]{2,1,0:T(8,128)S(1)}, u32[]{:S(2)}, u32[]{:S(2)}) collective-permute-start(f32[3,288,128]{2,1,0:T(8,128)S(1)} %slice.49), channel_id=1, source_target_pairs={{0,16},{16,0},{1,17},{17,1},{2,18},{18,2},{3,19},{19,3},{4,20},{20... | collective-permute-start | bytes 1327112 | tf_op jit(solution)/shard_map/ppermute | solution.py:20
  79.7 19.3 %collective-permute-start.5 = (bf16[136,128]{1,0:T(8,128)(2,1)S(1)}, bf16[136,128]{1,0:T(8,128)(2,1)S(1)}, u32[]{:S(2)}, u32[]{:S(2)}) collective-permute-start(bf16[136,128]{1,0:T(8,128)(2,1)S(1)} %slice.44), channel_id=1, source_target_pairs={{2,0},{4,2},{6,4},{8,6},{10,8},{12,10},{14,12},{3,1},{5,3},{7,5},{... | collective-permute-start | bytes 104456 | tf_op jit(solution)/shard_map/ppermute | solution.py:16
  90.8 9.3 %copy-start.1 = (f32[3,288,128]{2,1,0:T(8,128)}, f32[3,288,128]{2,1,0:T(8,128)S(1)}, u32[]{:S(2)}) copy-start(f32[3,288,128]{2,1,0:T(8,128)S(1)} %slice_add_fusion.refs_1_) | copy-start | bytes 1327108
  90.9 8.1 %collective-permute-start.4 = (f32[152,128]{1,0:T(8,128)S(1)}, f32[152,128]{1,0:T(8,128)S(1)}, u32[]{:S(2)}, u32[]{:S(2)}) collective-permute-start(f32[152,128]{1,0:T(8,128)S(1)} %pad_maximum_fusion.1), channel_id=1, source_target_pairs={{2,0},{4,2},{6,4},{8,6},{10,8},{12,10},{14,12},{3,1},{5,3},{7,5},{... | collective-permute-start | bytes 233480 | tf_op jit(solution)/shard_map/ppermute | solution.py:16
  94.0 6.1 %collective-permute-start.3 = (f32[280,128]{1,0:T(8,128)S(1)}, f32[280,128]{1,0:T(8,128)S(1)}, u32[]{:S(2)}, u32[]{:S(2)}) collective-permute-start(f32[280,128]{1,0:T(8,128)S(1)} %pad_maximum_fusion), channel_id=1, source_target_pairs={{0,2},{2,4},{4,6},{6,8},{8,10},{10,12},{12,14},{1,3},{3,5},{5,7},{... | collective-permute-start | bytes 430088 | tf_op jit(solution)/shard_map/ppermute | solution.py:16
  99.0 1.1 copy-start.6
  99.0 1.1 copy-start.5
  100.1 0.7 copy-start.3
  112.1 0.6 copy-start.9
Sparse Core Ops, SparseCore 0:
  10.2 59.4 all-gather.1

commit v2 on v1

--- a/solution.py
+++ b/solution.py
@@ -8,6 +8,9 @@
 D = 8192
 GROUP = 16
 EDGE = 8
+AXES = ("rep", "seq", "grp")
+VMEM = pl.BlockSpec(memory_space=pltpu.VMEM)
+SMEM = pl.BlockSpec(memory_space=pltpu.SMEM)
 
 
 def shifted(block, axis, distance):
@@ -16,8 +19,61 @@
     return lax.ppermute(block, axis, route)
 
 
-def swapped(block, axis):
-    return lax.ppermute(block, axis, [(0, 1), (1, 0)])
+def crossed(block, axis, bit):
+    return lax.ppermute(block, axis, [(i, i ^ bit) for i in range(lax.axis_size(axis))])
+
+
+def routed(block, target):
+    parts, members, cores = (lax.axis_size(axis) for axis in AXES)
+    route = []
+    for rep in range(parts):
+        for seq in range(members):
+            for core in range(cores):
+                goal = target(rep, seq, core)
+                if goal is not None:
+                    source = (rep * members + seq) * cores + core
+                    route.append((source, (goal[0] * members + goal[1]) * cores + goal[2]))
+    return lax.ppermute(block, AXES, route)
+
+
+def product_kernel(place, ours, theirs, first, second, third, fourth, out, panel):
+    kinds, height, _ = first.shape
+    lanes = 4 * height
+    count = ours.shape[0]
+    for number, block in enumerate((first, second, third, fourth)):
+        begin = pl.multiple_of((place[0] ^ number) * height, height)
+        for kind in range(kinds):
+            panel[pl.ds(kind * lanes + begin, height), :] = block[kind]
+    for index, tokens in enumerate((ours, theirs)):
+        result = lax.dot_general(
+            tokens[...],
+            panel[...],
+            (((1,), (1,)), ((), ())),
+            preferred_element_type=jnp.float32,
+        )
+        for kind in range(kinds):
+            out[kind, index * count : (index + 1) * count] = result[
+                :, kind * lanes : (kind + 1) * lanes
+            ]
+
+
+def product(place, ours, theirs, blocks):
+    kinds, height, width = blocks[0].shape
+    count = ours.shape[0]
+    return pl.pallas_call(
+        product_kernel,
+        out_shape=jax.ShapeDtypeStruct((kinds, 2 * count, 4 * height), jnp.float32),
+        in_specs=[SMEM] + [VMEM] * 6,
+        out_specs=VMEM,
+        scratch_shapes=[pltpu.VMEM((kinds * 4 * height, width), jnp.bfloat16)],
+        compiler_params=pltpu.CompilerParams(vmem_limit_bytes=24 << 20),
+        cost_estimate=pl.CostEstimate(
+            flops=2 * 2 * count * kinds * 4 * height * width,
+            bytes_accessed=2 * 2 * count * width + 8 * kinds * height * width,
+            transcendentals=0,
+        ),
+        name="product",
+    )(place, ours, theirs, *blocks)
 
 
 def mixer_kernel(
@@ -104,12 +160,11 @@
     def body(*refs):
         mixer_kernel(rows, reach, *refs)
 
-    vmem = pl.BlockSpec(memory_space=pltpu.VMEM)
     return pl.pallas_call(
         body,
         out_shape=jax.ShapeDtypeStruct((8, count), jnp.float32),
-        in_specs=[pl.BlockSpec(memory_space=pltpu.SMEM)] + [vmem] * 7,
-        out_specs=vmem,
+        in_specs=[SMEM] + [VMEM] * 7,
+        out_specs=VMEM,
         scratch_shapes=[
             pltpu.VMEM((EDGE + rows + reach, lanes), jnp.float32),
             pltpu.VMEM((reach + rows + EDGE, lanes), jnp.float32),
@@ -123,32 +178,85 @@
     )(picks, feature, before, after, grad, grad_after, taps, filters)
 
 
+def gathered_features(tokens, proj, lanes):
+    rep, half = lax.axis_index("rep"), lax.axis_index("grp")
+    width = proj.shape[2] // lax.axis_size("rep")
+    count = sum(piece.shape[0] for piece in tokens)
+
+    def columns(side):
+        return jnp.concatenate(
+            [lax.dynamic_slice_in_dim(piece, side * width, width, 1) for piece in tokens], 0
+        )
+
+    theirs = crossed(columns(1 - rep), "rep", 1)
+    panels = lax.all_gather(
+        lax.dynamic_slice_in_dim(proj, rep * width, width, 2), "seq", axis=1, tiled=True
+    )
+    both = jnp.concatenate([columns(rep), theirs], 0)
+    partial = jnp.einsum("td,fcd->ftc", both, panels, preferred_element_type=jnp.float32)
+    keep = lax.dynamic_slice_in_dim(partial, half * lanes, lanes, 2)
+    give = lax.dynamic_slice_in_dim(partial, (1 - half) * lanes, lanes, 2)
+    chip = keep + crossed(give, "grp", 1)
+    return chip[:, :count] + crossed(chip[:, count:], "rep", 1)
+
+
+def cube_features(tokens, proj):
+    rep, seq, half = (lax.axis_index(axis) for axis in AXES)
+    width = proj.shape[2] // lax.axis_size("rep")
+    count = sum(piece.shape[0] for piece in tokens)
+    bar = lax.optimization_barrier
+
+    def columns(side):
+        return jnp.concatenate(
+            [lax.dynamic_slice_in_dim(piece, side * width, width, 1) for piece in tokens], 0
+        )
+
+    own = lax.dynamic_slice_in_dim(proj, rep * width, width, 2)
+    own_2 = crossed(own, "seq", 2)
+    own_4 = crossed(own, "seq", 4)
+    own_1 = crossed(own, "seq", 1)
+    theirs = crossed(columns(1 - rep), "rep", 1)
+    own_2, own_1 = bar((own_2, own_1))
+    own_3 = crossed(own_2, "seq", 1)
+    own_4, own_3 = bar((own_4, own_3))
+    own_6 = crossed(own_4, "seq", 2)
+    own_5 = crossed(own_4, "seq", 1)
+    own_6, own_5 = bar((own_6, own_5))
+    cut = own.shape[1] // 2
+    own_7 = jnp.concatenate(
+        [crossed(own_6[:, :cut], "seq", 1), crossed(own_5[:, cut:], "seq", 2)], 1
+    )
+    ours = columns(rep)
+    place = (seq % 4).reshape(1)
+
+    def chip_sum(partial, near):
+        keeper = lambda seq, core: (core == seq // 4) == near
+        brought = routed(
+            partial, lambda rep, seq, core: None if keeper(seq, core) else (rep, seq, 1 - core)
+        )
+        summed = partial + brought
+        other = routed(
+            summed[:, count:],
+            lambda rep, seq, core: (1 - rep, seq, core) if keeper(seq, core) else None,
+        )
+        return summed[:, :count] + other
+
+    near = chip_sum(product(place, ours, theirs, (own, own_1, own_2, own_3)), True)
+    far = chip_sum(product(place, ours, theirs, (own_4, own_5, own_6, own_7)), False)
+    return jnp.where(half == seq // 4, near, far)
+
+
 def per_device(hidden, proj, short_taps, filters, grad_out, var_pos, alt_hidden):
     rows = hidden.shape[0]
     lanes = grad_out.shape[1]
     reach = filters.shape[1] + EDGE
-    rep, half = lax.axis_index("rep"), lax.axis_index("grp")
-    parts = lax.axis_size("rep")
-    width = hidden.shape[1] // parts
-
-    tokens = jnp.concatenate([hidden, alt_hidden], 0)
-    theirs = swapped(lax.dynamic_slice_in_dim(tokens, (1 - rep) * width, width, 1), "rep")
-    panels = lax.all_gather(
-        lax.dynamic_slice_in_dim(proj, rep * width, width, 2), "seq", axis=1, tiled=True
-    )
-    ours = lax.dynamic_slice_in_dim(tokens, rep * width, width, 1)
     grad_after = shifted(grad_out[:reach], "seq", -1)
     per_channel = jnp.repeat(filters, GROUP, axis=0).T
     picks = var_pos - lax.axis_index("seq") * rows
-
-    both = jnp.concatenate([ours, theirs], 0)
-    partial = jnp.einsum("td,fcd->ftc", both, panels, preferred_element_type=jnp.float32)
-    keep = lax.dynamic_slice_in_dim(partial, half * lanes, lanes, 2)
-    give = lax.dynamic_slice_in_dim(partial, (1 - half) * lanes, lanes, 2)
-    chip = keep + swapped(give, "grp")
-    count = tokens.shape[0]
-    feature = chip[:, :count] + swapped(chip[:, count:], "rep")
-
+    if lax.axis_size("seq") == 8:
+        feature = cube_features((hidden, alt_hidden), proj)
+    else:
+        feature = gathered_features((hidden, alt_hidden), proj, lanes)
     before = shifted(
         jnp.concatenate(
             [

time: 121 us -> 92.2 us (0.76)
  the two profiles are of different devices: /device:TPU:23 before, /device:TPU:9 now
where the time goes in v2:
time: 92.2 us; the launch traced here: 91.6 us
  starting transfers between devices  30.3 us (33%)
  waiting for transfers between devices  30.1 us (33%)
  local copies, waits for them, and re-layouts  14.5 us (16%)
  Pallas kernels  9.11 us (10%)
  other arithmetic  4.11 us (4%)
  blocking collectives  2.48 us (3%)
  between operations  1.03 us (1%)
    ppermute x9, waiting for transfers between devices, crossed(): lax.ppermute(block, axis, [(i, i ^ bit) for i in range(lax.axis_size(axis...  19.7 us
    ppermute x4, starting transfers between devices, routed(): return lax.ppermute(block, AXES, route)  11.6 us
    ppermute x3, starting transfers between devices, shifted(): return lax.ppermute(block, axis, route)  9.66 us
    ppermute x9, starting transfers between devices, crossed(): lax.ppermute(block, axis, [(i, i ^ bit) for i in range(lax.axis_size(axis...  9.06 us
    unnamed x46, local copies, waits for them, and re-layouts  7.83 us
    ppermute x4, waiting for transfers between devices, routed(): return lax.ppermute(block, AXES, route)  6.88 us
    pallas_call x1, Pallas kernels, mixer(): pl.pallas_call(body, out_shape=jax.ShapeDtypeStruct((8, count), jnp.float...  6.13 us
    ppermute x3, waiting for transfers between devices, shifted(): return lax.ppermute(block, axis, route)  3.56 us
  transfers between devices with their start and end apart: 16, of which 8 were waited for; matrix products, arithmetic and copies ran while one was open for 10% of the time, Pallas kernels for 3%

profile of v2, /device:TPU:9, one launch (start us, length us, event | category | flops | bytes accessed | tf_op | source)
XLA Modules:
  0.0 91.6 jit_solution(17039911137229849023)
XLA Ops:
  0.6 0.0 copy-start
  0.7 1.1 %copy-done = bf16[3,32,4096]{2,1,0:T(8,128)(2,1)S(1)} copy-done((bf16[3,32,4096]{2,1,0:T(8,128)(2,1)S(1)}, bf16[3,32,4096]{2,1,0:T(8,128)(2,1)}, u32[]{:S(2)}) %copy-start) | copy-done | bytes 786456
  1.8 0.1 collective-permute-start.1
  1.9 1.4 %collective-permute-start.2 = (bf16[3,32,2048]{2,1,0:T(8,128)(2,1)S(1)}, bf16[3,32,2048]{2,1,0:T(8,128)(2,1)S(1)}, u32[]{:S(2)}, u32[]{:S(2)}) collective-permute-start(bf16[3,32,2048]{2,1,0:T(8,128)(2,1)S(1)} %constant_dynamic-slice_fusion.first), channel_id=1, source_target_pairs={{0,2},{2,0},{4,6},{6,4},{8,10},{10,8},{12,14},{14,12},{1,3},{3,1},... | collective-permute-start | bytes 1179656 | tf_op jit(solution)/shard_map/ppermute | solution.py:23
  3.2 1.8 %constant_dynamic-slice_fusion.2 = (bf16[272,2048]{1,0:T(8,128)(2,1)S(1)}, bf16[272,2048]{1,0:T(8,128)(2,1)S(1)}) fusion(bf16[272,4096]{1,0:T(8,128)(2,1)} %param.7, s32[]{:T(128)S(6)} %select_n.32, s32[]{:T(128)S(6)} %select_n.31), kind=kLoop, calls=%fused_computation.17 | loop fusion | bytes 4456456 | tf_op jit(solution)/shard_map/dynamic_slice | solution.py:211
  5.1 1.1 %pad_maximum_fusion.1 = bf16[288,2048]{1,0:T(8,128)(2,1)} fusion(bf16[16,2048]{1,0:T(8,128)(2,1)S(1)} %get-tuple-element.22, bf16[272,2048]{1,0:T(8,128)(2,1)S(1)} %get-tuple-element.14), kind=kLoop, calls=%fused_computation.1 | loop fusion | flops 2359296 | bytes 2359296 | tf_op jit(solution)/shard_map/concatenate | solution.py:210
  6.2 1.2 %collective-permute-start = (bf16[288,2048]{1,0:T(8,128)(2,1)}, bf16[288,2048]{1,0:T(8,128)(2,1)S(1)}, u32[]{:S(2)}, u32[]{:S(2)}) collective-permute-start(bf16[288,2048]{1,0:T(8,128)(2,1)} %pad_maximum_fusion.1), channel_id=1, source_target_pairs={{0,16},{16,0},{1,17},{17,1},{2,18},{18,2},{3,19},{19,3},{4,20},{20... | collective-permute-start | bytes 3538952 | tf_op jit(solution)/shard_map/ppermute | solution.py:23
  7.4 2.3 %collective-permute-start.3 = (bf16[3,32,2048]{2,1,0:T(8,128)(2,1)S(1)}, bf16[3,32,2048]{2,1,0:T(8,128)(2,1)S(1)}, u32[]{:S(2)}, u32[]{:S(2)}) collective-permute-start(bf16[3,32,2048]{2,1,0:T(8,128)(2,1)S(1)} %constant_dynamic-slice_fusion.first), channel_id=1, source_target_pairs={{0,8},{2,10},{4,12},{6,14},{8,0},{10,2},{12,4},{14,6},{1,9},{3,11}... | collective-permute-start | bytes 1179656 | tf_op jit(solution)/shard_map/ppermute | solution.py:23
  9.7 2.1 %collective-permute-done.1.third = bf16[3,32,2048]{2,1,0:T(8,128)(2,1)S(1)} collective-permute-done((bf16[3,32,2048]{2,1,0:T(8,128)(2,1)S(1)}, bf16[3,32,2048]{2,1,0:T(8,128)(2,1)S(1)}, u32[]{:S(2)}, u32[]{:S(2)}) %collective-permute-start.1) | collective-permute-done | bytes 393248 | tf_op jit(solution)/shard_map/ppermute | solution.py:23
  11.8 0.1 collective-permute-done.2.second
  11.9 0.8 copy-done.7
  12.7 1.9 %collective-permute-start.4 = (bf16[3,32,2048]{2,1,0:T(8,128)(2,1)S(1)}, bf16[3,32,2048]{2,1,0:T(8,128)(2,1)S(1)}, u32[]{:S(2)}, u32[]{:S(2)}) collective-permute-start(bf16[3,32,2048]{2,1,0:T(8,128)(2,1)S(1)} %collective-permute-done.1.third), channel_id=1, source_target_pairs={{0,2},{2,0},{4,6},{6,4},{8,10},{10,8},{12,14},{14,12},{1,3},{3,1},... | collective-permute-start | bytes 1179656 | tf_op jit(solution)/shard_map/ppermute | solution.py:23
  14.6 0.8 copy-done.5
  15.3 10.3 %collective-permute-done.3.first = bf16[3,32,2048]{2,1,0:T(8,128)(2,1)S(1)} collective-permute-done((bf16[3,32,2048]{2,1,0:T(8,128)(2,1)S(1)}, bf16[3,32,2048]{2,1,0:T(8,128)(2,1)S(1)}, u32[]{:S(2)}, u32[]{:S(2)}) %collective-permute-start.3) | collective-permute-done | bytes 393248 | tf_op jit(solution)/shard_map/ppermute | solution.py:23
  25.6 0.0 collective-permute-done.4.fourth
  25.6 0.8 copy-done.11
  26.3 1.8 %collective-permute-start.7 = (bf16[3,32,2048]{2,1,0:T(8,128)(2,1)S(1)}, bf16[3,32,2048]{2,1,0:T(8,128)(2,1)S(1)}, u32[]{:S(2)}, u32[]{:S(2)}) collective-permute-start(bf16[3,32,2048]{2,1,0:T(8,128)(2,1)S(1)} %collective-permute-done.3.first), channel_id=1, source_target_pairs={{0,4},{2,6},{4,0},{6,2},{8,12},{10,14},{12,8},{14,10},{1,5},{3,7},... | collective-permute-start | bytes 1179656 | tf_op jit(solution)/shard_map/ppermute | solution.py:23
  28.1 0.1 collective-permute-start.8
  28.2 0.7 copy-done.9
  29.0 6.3 %collective-permute-done.7.third = bf16[3,32,2048]{2,1,0:T(8,128)(2,1)S(1)} collective-permute-done((bf16[3,32,2048]{2,1,0:T(8,128)(2,1)S(1)}, bf16[3,32,2048]{2,1,0:T(8,128)(2,1)S(1)}, u32[]{:S(2)}, u32[]{:S(2)}) %collective-permute-start.7) | collective-permute-done | bytes 393248 | tf_op jit(solution)/shard_map/ppermute | solution.py:23
  35.3 0.9 collective-permute-done.8.second
  36.2 0.7 slice.51
  36.9 0.3 collective-permute-start.10
  37.2 0.7 slice.50
  37.9 0.0 collective-permute-start.9
  37.9 0.1 pad_maximum_fusion.ours
  38.0 0.0 collective-permute-done.theirs
  38.0 1.0 %copy-done.6 = bf16[3,32,2048]{2,1,0:T(8,128)(2,1)S(1)} copy-done((bf16[3,32,2048]{2,1,0:T(8,128)(2,1)S(1)}, bf16[3,32,2048]{2,1,0:T(8,128)(2,1)}, u32[]{:S(2)}) %copy-start.6) | copy-done | bytes 393240
  39.0 1.0 %copy-done.8 = bf16[3,32,2048]{2,1,0:T(8,128)(2,1)S(1)} copy-done((bf16[3,32,2048]{2,1,0:T(8,128)(2,1)S(1)}, bf16[3,32,2048]{2,1,0:T(8,128)(2,1)}, u32[]{:S(2)}) %copy-start.8) | copy-done | bytes 393240
  40.0 1.0 %copy-done.12 = bf16[3,32,2048]{2,1,0:T(8,128)(2,1)S(1)} copy-done((bf16[3,32,2048]{2,1,0:T(8,128)(2,1)S(1)}, bf16[3,32,2048]{2,1,0:T(8,128)(2,1)}, u32[]{:S(2)}) %copy-start.12) | copy-done | bytes 393240
  41.0 1.5 %product.2 = f32[3,576,128]{2,1,0:T(8,128)S(1)} custom-call(s32[1]{0:T(128)} %bitcast.place, bf16[288,2048]{1,0:T(8,128)(2,1)S(1)} %pad_maximum_fusion.ours, bf16[288,2048]{1,0:T(8,128)(2,1)S(1)} %collective-permute-done.theirs, bf16[3,32,2048]{2,1,0:T(8,128)(2,1)S(1)} %constant_dynamic-slice_fusion.first, bf16[3,32,2048]{2,1,0:T(8,128)(2,1)S(1)} %copy-done.8, ...), custom_call_target="tpu_custom_call" | custom-call | flops 905969664 | bytes 3932160 | tf_op jit(solution)/shard_map/product/pallas_call | solution.py:63
  42.5 5.8 %collective-permute-start.5 = (f32[3,576,128]{2,1,0:T(8,128)S(1)}, f32[3,576,128]{2,1,0:T(8,128)S(1)}, u32[]{:S(2)}, u32[]{:S(2)}) collective-permute-start(f32[3,576,128]{2,1,0:T(8,128)S(1)} %product.2), channel_id=1, source_target_pairs={{1,0},{3,2},{5,4},{7,6},{8,9},{10,11},{12,13},{14,15},{17,16},{19,... | collective-permute-start | bytes 2654216 | tf_op jit(solution)/shard_map/ppermute | solution.py:36
  48.3 0.0 collective-permute-done.10
  48.3 0.0 collective-permute-done.9
  48.4 1.1 %pad_maximum_fusion.2.fourth = bf16[3,32,2048]{2,1,0:T(8,128)(2,1)S(1)} fusion(bf16[3,16,2048]{2,1,0:T(8,128)(2,1)} %collective-permute-done.10, bf16[3,16,2048]{2,1,0:T(8,128)(2,1)} %collective-permute-done.9), kind=kLoop, calls=%fused_computation.5 | loop fusion | flops 786432 | bytes 786432 | tf_op jit(solution)/shard_map/concatenate | solution.py:226
  49.4 1.5 %product.3 = f32[3,576,128]{2,1,0:T(8,128)S(1)} custom-call(s32[1]{0:T(128)} %bitcast.place, bf16[288,2048]{1,0:T(8,128)(2,1)S(1)} %pad_maximum_fusion.ours, bf16[288,2048]{1,0:T(8,128)(2,1)S(1)} %collective-permute-done.theirs, bf16[3,32,2048]{2,1,0:T(8,128)(2,1)S(1)} %copy-done.10, bf16[3,32,2048]{2,1,0:T(8,128)(2,1)S(1)} %copy-done.4, ...), custom_call_target="tpu_custom_call" | custom-call | flops 905969664 | bytes 3932160 | tf_op jit(solution)/shard_map/product/pallas_call | solution.py:63
  50.9 1.3 %collective-permute-start.11 = (f32[3,576,128]{2,1,0:T(8,128)S(1)}, f32[3,576,128]{2,1,0:T(8,128)S(1)}, u32[]{:S(2)}, u32[]{:S(2)}) collective-permute-start(f32[3,576,128]{2,1,0:T(8,128)S(1)} %product.3), channel_id=1, source_target_pairs={{0,1},{2,3},{4,5},{6,7},{9,8},{11,10},{13,12},{15,14},{16,17},{18,... | collective-permute-start | bytes 2654216 | tf_op jit(solution)/shard_map/ppermute | solution.py:36
  52.3 0.1 add.31
  52.4 0.0 copy-start.14
  52.4 0.8 collective-permute-start.6
  53.2 2.0 %collective-permute-done.11 = f32[3,576,128]{2,1,0:T(8,128)S(1)} collective-permute-done((f32[3,576,128]{2,1,0:T(8,128)S(1)}, f32[3,576,128]{2,1,0:T(8,128)S(1)}, u32[]{:S(2)}, u32[]{:S(2)}) %collective-permute-start.11) | collective-permute-done | bytes 884768 | tf_op jit(solution)/shard_map/ppermute | solution.py:36
  55.3 0.1 add.33
  55.4 0.8 slice.67
  56.2 3.6 %collective-permute-start.12 = (f32[3,288,128]{2,1,0:T(8,128)}, f32[3,288,128]{2,1,0:T(8,128)}, u32[]{:S(2)}, u32[]{:S(2)}) collective-permute-start(f32[3,288,128]{2,1,0:T(8,128)} %slice.67), channel_id=1, source_target_pairs={{1,17},{3,19},{5,21},{7,23},{8,24},{10,26},{12,28},{14,30},{17,1},... | collective-permute-start | bytes 1327112 | tf_op jit(solution)/shard_map/ppermute | solution.py:36
  59.8 3.3 %collective-permute-start.15 = (bf16[136,128]{1,0:T(8,128)(2,1)S(1)}, bf16[136,128]{1,0:T(8,128)(2,1)S(1)}, u32[]{:S(2)}, u32[]{:S(2)}) collective-permute-start(bf16[136,128]{1,0:T(8,128)(2,1)S(1)} %slice.60), channel_id=1, source_target_pairs={{2,0},{4,2},{6,4},{8,6},{10,8},{12,10},{14,12},{3,1},{5,3},{7,5},{... | collective-permute-start | bytes 104456 | tf_op jit(solution)/shard_map/ppermute | solution.py:19
  63.2 0.0 copy-start.22
  63.2 0.0 copy-start.20
  63.2 0.0 copy-start.19
  63.2 0.0 collective-permute-done.6
  63.2 4.8 %collective-permute-done.12 = f32[3,288,128]{2,1,0:T(8,128)} collective-permute-done((f32[3,288,128]{2,1,0:T(8,128)}, f32[3,288,128]{2,1,0:T(8,128)}, u32[]{:S(2)}, u32[]{:S(2)}) %collective-permute-start.12) | collective-permute-done | bytes 442400 | tf_op jit(solution)/shard_map/ppermute | solution.py:36
  68.1 1.1 %fusion.refs_1_ = f32[3,288,128]{2,1,0:T(8,128)S(1)} fusion(f32[3,288,128]{2,1,0:T(8,128)} %collective-permute-done.12, f32[3,576,128]{2,1,0:T(8,128)S(1)} %add.33, f32[3,288,128]{2,1,0:T(8,128)S(1)} %collective-permute-done.6, f32[3,576,128]{2,1,0:T(8,128)S(1)} %add.31, pred[]{:T(512)S(6)} %eq.5), kind=kLoop, calls=%fused_computation.3 | loop fusion | flops 331776 | bytes 2211841 | tf_op jit(solution)/shard_map/jit(_where)/select_n | solution.py:246
  69.3 4.4 %collective-permute-start.14 = (f32[152,128]{1,0:T(8,128)S(1)}, f32[152,128]{1,0:T(8,128)S(1)}, u32[]{:S(2)}, u32[]{:S(2)}) collective-permute-start(f32[152,128]{1,0:T(8,128)S(1)} %pad_maximum_fusion.4), channel_id=1, source_target_pairs={{2,0},{4,2},{6,4},{8,6},{10,8},{12,10},{14,12},{3,1},{5,3},{7,5},{... | collective-permute-start | bytes 233480 | tf_op jit(solution)/shard_map/ppermute | solution.py:19
  73.7 1.9 %collective-permute-start.13 = (f32[280,128]{1,0:T(8,128)S(1)}, f32[280,128]{1,0:T(8,128)S(1)}, u32[]{:S(2)}, u32[]{:S(2)}) collective-permute-start(f32[280,128]{1,0:T(8,128)S(1)} %pad_maximum_fusion.3), channel_id=1, source_target_pairs={{0,2},{2,4},{4,6},{6,8},{8,10},{10,12},{12,14},{1,3},{3,5},{5,7},{... | collective-permute-start | bytes 430088 | tf_op jit(solution)/shard_map/ppermute | solution.py:19
  75.6 0.5 broadcast_subtract_fusion.refs_0_
  76.2 0.7 copy.10
  76.9 0.6 reshape.14.refs_6_
  77.5 0.0 collective-permute-done.15.refs_5_
  77.5 0.0 collective-permute-done.14.refs_3_
  77.5 3.6 %collective-permute-done.13.refs_2_ = f32[280,128]{1,0:T(8,128)S(1)} collective-permute-done((f32[280,128]{1,0:T(8,128)S(1)}, f32[280,128]{1,0:T(8,128)S(1)}, u32[]{:S(2)}, u32[]{:S(2)}) %collective-permute-start.13) | collective-permute-done | bytes 143392 | tf_op jit(solution)/shard_map/ppermute | solution.py:19
  81.1 0.6 copy-done.15
  81.7 6.1 %mixer.1 = f32[8,288]{1,0:T(8,128)} custom-call(s32[16]{0:T(128)} %broadcast_subtract_fusion.refs_0_, f32[3,288,128]{2,1,0:T(8,128)} %copy-done.13, f32[280,128]{1,0:T(8,128)} %copy-done.15, f32[152,128]{1,0:T(8,128)} %copy-done.17, bf16[272,128]{1,0:T(8,128)(2,1)} %refs_4_.1, bf16[136,128]{1,0:T(8,128)(2,1)} %copy-done.18, f32[9,128]{1,0:T(8,128)} %reshape.14.refs_6_, ...), custom_call_target="tpu_custom_call" | custom-call | tf_op jit(solution)/shard_map/mixer/pallas_call | solution.py:163
  87.8 0.7 slice_reduce_fusion
  88.6 2.5 %psum.7 = f32[288]{0:T(512)S(1)} all-reduce(f32[288]{0:T(512)S(1)} %slice_reduce_fusion), channel_id=1, replica_groups=mesh['rep'=2,'seq'=8,'grp'=2] {'grp'}, use_global_device_ids=true, to_apply=%region_0.1 | all-reduce | flops 288 | bytes 2304 | tf_op jit(solution)/shard_map/psum | solution.py:279
  91.0 0.6 slice.63
  (43 shorter events, 0.2 us)
Async XLA Ops:
  0.6 1.1 %copy-start = (bf16[3,32,4096]{2,1,0:T(8,128)(2,1)S(1)}, bf16[3,32,4096]{2,1,0:T(8,128)(2,1)}, u32[]{:S(2)}) copy-start(bf16[3,32,4096]{2,1,0:T(8,128)(2,1)} %param.8) | copy-start | bytes 2359300
  1.8 10.0 %collective-permute-start.1 = (bf16[3,32,2048]{2,1,0:T(8,128)(2,1)S(1)}, bf16[3,32,2048]{2,1,0:T(8,128)(2,1)S(1)}, u32[]{:S(2)}, u32[]{:S(2)}) collective-permute-start(bf16[3,32,2048]{2,1,0:T(8,128)(2,1)S(1)} %constant_dynamic-slice_fusion.first), channel_id=1, source_target_pairs={{0,4},{2,6},{4,0},{6,2},{8,12},{10,14},{12,8},{14,10},{1,5},{3,7},... | collective-permute-start | bytes 1179656 | tf_op jit(solution)/shard_map/ppermute | solution.py:23
  1.9 10.0 %collective-permute-start.2 = (bf16[3,32,2048]{2,1,0:T(8,128)(2,1)S(1)}, bf16[3,32,2048]{2,1,0:T(8,128)(2,1)S(1)}, u32[]{:S(2)}, u32[]{:S(2)}) collective-permute-start(bf16[3,32,2048]{2,1,0:T(8,128)(2,1)S(1)} %constant_dynamic-slice_fusion.first), channel_id=1, source_target_pairs={{0,2},{2,0},{4,6},{6,4},{8,10},{10,8},{12,14},{14,12},{1,3},{3,1},... | collective-permute-start | bytes 1179656 | tf_op jit(solution)/shard_map/ppermute | solution.py:23
  3.2 1.8 %copy-start.16 = (bf16[16,4096]{1,0:T(8,128)(2,1)S(1)}, bf16[16,4096]{1,0:T(8,128)(2,1)}, u32[]{:S(2)}) copy-start(bf16[16,4096]{1,0:T(8,128)(2,1)} %param.13) | copy-start | bytes 393220
  6.2 31.8 %collective-permute-start = (bf16[288,2048]{1,0:T(8,128)(2,1)}, bf16[288,2048]{1,0:T(8,128)(2,1)S(1)}, u32[]{:S(2)}, u32[]{:S(2)}) collective-permute-start(bf16[288,2048]{1,0:T(8,128)(2,1)} %pad_maximum_fusion.1), channel_id=1, source_target_pairs={{0,16},{16,0},{1,17},{17,1},{2,18},{18,2},{3,19},{19,3},{4,20},{20... | collective-permute-start | bytes 3538952 | tf_op jit(solution)/shard_map/ppermute | solution.py:23
  7.4 18.2 %collective-permute-start.3 = (bf16[3,32,2048]{2,1,0:T(8,128)(2,1)S(1)}, bf16[3,32,2048]{2,1,0:T(8,128)(2,1)S(1)}, u32[]{:S(2)}, u32[]{:S(2)}) collective-permute-start(bf16[3,32,2048]{2,1,0:T(8,128)(2,1)S(1)} %constant_dynamic-slice_fusion.first), channel_id=1, source_target_pairs={{0,8},{2,10},{4,12},{6,14},{8,0},{10,2},{12,4},{14,6},{1,9},{3,11}... | collective-permute-start | bytes 1179656 | tf_op jit(solution)/shard_map/ppermute | solution.py:23
  11.9 0.8 copy-start.7
  12.7 12.9 %collective-permute-start.4 = (bf16[3,32,2048]{2,1,0:T(8,128)(2,1)S(1)}, bf16[3,32,2048]{2,1,0:T(8,128)(2,1)S(1)}, u32[]{:S(2)}, u32[]{:S(2)}) collective-permute-start(bf16[3,32,2048]{2,1,0:T(8,128)(2,1)S(1)} %collective-permute-done.1.third), channel_id=1, source_target_pairs={{0,2},{2,0},{4,6},{6,4},{8,10},{10,8},{12,14},{14,12},{1,3},{3,1},... | collective-permute-start | bytes 1179656 | tf_op jit(solution)/shard_map/ppermute | solution.py:23
  14.6 0.8 copy-start.5
  25.6 0.8 copy-start.11
  26.3 8.9 %collective-permute-start.7 = (bf16[3,32,2048]{2,1,0:T(8,128)(2,1)S(1)}, bf16[3,32,2048]{2,1,0:T(8,128)(2,1)S(1)}, u32[]{:S(2)}, u32[]{:S(2)}) collective-permute-start(bf16[3,32,2048]{2,1,0:T(8,128)(2,1)S(1)} %collective-permute-done.3.first), channel_id=1, source_target_pairs={{0,4},{2,6},{4,0},{6,2},{8,12},{10,14},{12,8},{14,10},{1,5},{3,7},... | collective-permute-start | bytes 1179656 | tf_op jit(solution)/shard_map/ppermute | solution.py:23
  28.1 8.1 %collective-permute-start.8 = (bf16[3,32,2048]{2,1,0:T(8,128)(2,1)S(1)}, bf16[3,32,2048]{2,1,0:T(8,128)(2,1)S(1)}, u32[]{:S(2)}, u32[]{:S(2)}) collective-permute-start(bf16[3,32,2048]{2,1,0:T(8,128)(2,1)S(1)} %collective-permute-done.3.first), channel_id=1, source_target_pairs={{0,2},{2,0},{4,6},{6,4},{8,10},{10,8},{12,14},{14,12},{1,3},{3,1},... | collective-permute-start | bytes 1179656 | tf_op jit(solution)/shard_map/ppermute | solution.py:23
  28.2 0.7 copy-start.9
  35.3 2.6 %copy-start.1 = (bf16[3,32,2048]{2,1,0:T(8,128)(2,1)}, bf16[3,32,2048]{2,1,0:T(8,128)(2,1)S(1)}, u32[]{:S(2)}) copy-start(bf16[3,32,2048]{2,1,0:T(8,128)(2,1)S(1)} %collective-permute-done.7.third) | copy-start | bytes 1179652
  36.2 1.7 %copy-start.3 = (bf16[3,32,2048]{2,1,0:T(8,128)(2,1)}, bf16[3,32,2048]{2,1,0:T(8,128)(2,1)S(1)}, u32[]{:S(2)}) copy-start(bf16[3,32,2048]{2,1,0:T(8,128)(2,1)S(1)} %collective-permute-done.8.second) | copy-start | bytes 1179652
  36.9 11.5 %collective-permute-start.10 = (bf16[3,16,2048]{2,1,0:T(8,128)(2,1)}, bf16[3,16,2048]{2,1,0:T(8,128)(2,1)}, u32[]{:S(2)}, u32[]{:S(2)}) collective-permute-start(bf16[3,16,2048]{2,1,0:T(8,128)(2,1)} %slice.51), channel_id=1, source_target_pairs={{0,4},{2,6},{4,0},{6,2},{8,12},{10,14},{12,8},{14,10},{1,5},{3,7},... | collective-permute-start | bytes 589832 | tf_op jit(solution)/shard_map/ppermute | solution.py:23
  37.9 10.5 %collective-permute-start.9 = (bf16[3,16,2048]{2,1,0:T(8,128)(2,1)}, bf16[3,16,2048]{2,1,0:T(8,128)(2,1)}, u32[]{:S(2)}, u32[]{:S(2)}) collective-permute-start(bf16[3,16,2048]{2,1,0:T(8,128)(2,1)} %slice.50), channel_id=1, source_target_pairs={{0,2},{2,0},{4,6},{6,4},{8,10},{10,8},{12,14},{14,12},{1,3},{3,1},... | collective-permute-start | bytes 589832 | tf_op jit(solution)/shard_map/ppermute | solution.py:23
  38.0 1.0 %copy-start.6 = (bf16[3,32,2048]{2,1,0:T(8,128)(2,1)S(1)}, bf16[3,32,2048]{2,1,0:T(8,128)(2,1)}, u32[]{:S(2)}) copy-start(bf16[3,32,2048]{2,1,0:T(8,128)(2,1)} %copy-done.5) | copy-start | bytes 1179652
  39.0 1.0 %copy-start.8 = (bf16[3,32,2048]{2,1,0:T(8,128)(2,1)S(1)}, bf16[3,32,2048]{2,1,0:T(8,128)(2,1)}, u32[]{:S(2)}) copy-start(bf16[3,32,2048]{2,1,0:T(8,128)(2,1)} %copy-done.7) | copy-start | bytes 1179652
  40.0 1.0 %copy-start.12 = (bf16[3,32,2048]{2,1,0:T(8,128)(2,1)S(1)}, bf16[3,32,2048]{2,1,0:T(8,128)(2,1)}, u32[]{:S(2)}) copy-start(bf16[3,32,2048]{2,1,0:T(8,128)(2,1)} %copy-done.11) | copy-start | bytes 1179652
  41.0 8.4 %copy-start.2 = (bf16[3,32,2048]{2,1,0:T(8,128)(2,1)S(1)}, bf16[3,32,2048]{2,1,0:T(8,128)(2,1)}, u32[]{:S(2)}) copy-start(bf16[3,32,2048]{2,1,0:T(8,128)(2,1)} %copy-done.1) | copy-start | bytes 1179652
  41.0 8.4 %copy-start.4 = (bf16[3,32,2048]{2,1,0:T(8,128)(2,1)S(1)}, bf16[3,32,2048]{2,1,0:T(8,128)(2,1)}, u32[]{:S(2)}) copy-start(bf16[3,32,2048]{2,1,0:T(8,128)(2,1)} %copy-done.3) | copy-start | bytes 1179652
  41.0 8.4 %copy-start.10 = (bf16[3,32,2048]{2,1,0:T(8,128)(2,1)S(1)}, bf16[3,32,2048]{2,1,0:T(8,128)(2,1)}, u32[]{:S(2)}) copy-start(bf16[3,32,2048]{2,1,0:T(8,128)(2,1)} %copy-done.9) | copy-start | bytes 1179652
  42.5 9.8 %collective-permute-start.5 = (f32[3,576,128]{2,1,0:T(8,128)S(1)}, f32[3,576,128]{2,1,0:T(8,128)S(1)}, u32[]{:S(2)}, u32[]{:S(2)}) collective-permute-start(f32[3,576,128]{2,1,0:T(8,128)S(1)} %product.2), channel_id=1, source_target_pairs={{1,0},{3,2},{5,4},{7,6},{8,9},{10,11},{12,13},{14,15},{17,16},{19,... | collective-permute-start | bytes 2654216 | tf_op jit(solution)/shard_map/ppermute | solution.py:36
  50.9 4.3 %collective-permute-start.11 = (f32[3,576,128]{2,1,0:T(8,128)S(1)}, f32[3,576,128]{2,1,0:T(8,128)S(1)}, u32[]{:S(2)}, u32[]{:S(2)}) collective-permute-start(f32[3,576,128]{2,1,0:T(8,128)S(1)} %product.3), channel_id=1, source_target_pairs={{0,1},{2,3},{4,5},{6,7},{9,8},{11,10},{13,12},{15,14},{16,17},{18,... | collective-permute-start | bytes 2654216 | tf_op jit(solution)/shard_map/ppermute | solution.py:36
  52.4 7.4 %copy-start.14 = (bf16[272,128]{1,0:T(8,128)(2,1)S(1)}, bf16[272,128]{1,0:T(8,128)(2,1)}, u32[]{:S(2)}) copy-start(bf16[272,128]{1,0:T(8,128)(2,1)} %refs_4_.1) | copy-start | bytes 208900
  52.4 10.8 %collective-permute-start.6 = (f32[3,288,128]{2,1,0:T(8,128)S(1)}, f32[3,288,128]{2,1,0:T(8,128)S(1)}, u32[]{:S(2)}, u32[]{:S(2)}) collective-permute-start(f32[3,288,128]{2,1,0:T(8,128)S(1)} %slice.65), channel_id=1, source_target_pairs={{0,16},{2,18},{4,20},{6,22},{9,25},{11,27},{13,29},{15,31},{16,0},... | collective-permute-start | bytes 1327112 | tf_op jit(solution)/shard_map/ppermute | solution.py:36
  56.2 11.9 %collective-permute-start.12 = (f32[3,288,128]{2,1,0:T(8,128)}, f32[3,288,128]{2,1,0:T(8,128)}, u32[]{:S(2)}, u32[]{:S(2)}) collective-permute-start(f32[3,288,128]{2,1,0:T(8,128)} %slice.67), channel_id=1, source_target_pairs={{1,17},{3,19},{5,21},{7,23},{8,24},{10,26},{12,28},{14,30},{17,1},... | collective-permute-start | bytes 1327112 | tf_op jit(solution)/shard_map/ppermute | solution.py:36
  59.8 17.7 %collective-permute-start.15 = (bf16[136,128]{1,0:T(8,128)(2,1)S(1)}, bf16[136,128]{1,0:T(8,128)(2,1)S(1)}, u32[]{:S(2)}, u32[]{:S(2)}) collective-permute-start(bf16[136,128]{1,0:T(8,128)(2,1)S(1)} %slice.60), channel_id=1, source_target_pairs={{2,0},{4,2},{6,4},{8,6},{10,8},{12,10},{14,12},{3,1},{5,3},{7,5},{... | collective-permute-start | bytes 104456 | tf_op jit(solution)/shard_map/ppermute | solution.py:19
  63.2 12.4 %copy-start.22 = (s32[16]{0:T(128)S(1)}, s32[16]{0:T(128)}, u32[]{:S(2)}) copy-start(s32[16]{0:T(128)} %param.12) | copy-start | bytes 196
  63.2 13.0 %copy-start.20 = (f32[8,128]{1,0:T(8,128)S(1)}, f32[8,128]{1,0:T(8,128)}, u32[]{:S(2)}) copy-start(f32[8,128]{1,0:T(8,128)} %param.10) | copy-start | bytes 12292
  63.2 13.7 %copy-start.19 = (f32[3,3,128]{2,1,0:T(4,128)S(1)}, f32[3,3,128]{2,1,0:T(4,128)}, u32[]{:S(2)}) copy-start(f32[3,3,128]{2,1,0:T(4,128)} %param.9) | copy-start | bytes 13828
  69.2 11.8 %copy-start.13 = (f32[3,288,128]{2,1,0:T(8,128)}, f32[3,288,128]{2,1,0:T(8,128)S(1)}, u32[]{:S(2)}) copy-start(f32[3,288,128]{2,1,0:T(8,128)S(1)} %fusion.refs_1_) | copy-start | bytes 1327108
  69.3 8.2 %collective-permute-start.14 = (f32[152,128]{1,0:T(8,128)S(1)}, f32[152,128]{1,0:T(8,128)S(1)}, u32[]{:S(2)}, u32[]{:S(2)}) collective-permute-start(f32[152,128]{1,0:T(8,128)S(1)} %pad_maximum_fusion.4), channel_id=1, source_target_pairs={{2,0},{4,2},{6,4},{8,6},{10,8},{12,10},{14,12},{3,1},{5,3},{7,5},{... | collective-permute-start | bytes 233480 | tf_op jit(solution)/shard_map/ppermute | solution.py:19
  73.7 7.4 %collective-permute-start.13 = (f32[280,128]{1,0:T(8,128)S(1)}, f32[280,128]{1,0:T(8,128)S(1)}, u32[]{:S(2)}, u32[]{:S(2)}) collective-permute-start(f32[280,128]{1,0:T(8,128)S(1)} %pad_maximum_fusion.3), channel_id=1, source_target_pairs={{0,2},{2,4},{4,6},{6,8},{8,10},{10,12},{12,14},{1,3},{3,5},{5,7},{... | collective-permute-start | bytes 430088 | tf_op jit(solution)/shard_map/ppermute | solution.py:19
  77.5 3.6 %copy-start.18 = (bf16[136,128]{1,0:T(8,128)(2,1)}, bf16[136,128]{1,0:T(8,128)(2,1)S(1)}, u32[]{:S(2)}) copy-start(bf16[136,128]{1,0:T(8,128)(2,1)S(1)} %collective-permute-done.15.refs_5_) | copy-start | bytes 104452
  77.5 3.6 %copy-start.17 = (f32[152,128]{1,0:T(8,128)}, f32[152,128]{1,0:T(8,128)S(1)}, u32[]{:S(2)}) copy-start(f32[152,128]{1,0:T(8,128)S(1)} %collective-permute-done.14.refs_3_) | copy-start | bytes 233476
  81.0 0.7 copy-start.15
  91.0 0.6 copy-start.21

commit v3 on v1

v3 whole, which is shorter than its diff:
```python
import jax
import jax.numpy as jnp
from jax import lax
from jax.experimental import pallas as pl
from jax.experimental.pallas import tpu as pltpu
from jax.sharding import PartitionSpec as P

D = 8192
GROUP = 16
EDGE = 8
PIECES = 2
AXES = ("rep", "seq", "grp")
VMEM = pl.BlockSpec(memory_space=pltpu.VMEM)
ANY = pl.BlockSpec(memory_space=pl.ANY)
HBM = pl.BlockSpec(memory_space=pltpu.HBM)
SMEM = pl.BlockSpec(memory_space=pltpu.SMEM)


def shifted(block, axis, distance):
    devices = range(lax.axis_size(axis))
    route = [(i - distance, i) for i in devices if i - distance in devices]
    return lax.ppermute(block, axis, route)


def crossed(block, axis, bit):
    return lax.ppermute(block, axis, [(i, i ^ bit) for i in range(lax.axis_size(axis))])


def moved(pairs, sems):
    copies = [
        pltpu.make_async_copy(source, target, sems.at[index])
        for index, (source, target) in enumerate(pairs)
    ]
    for copy in copies:
        copy.start()
    return copies


def part(side, width):
    return pl.ds(pl.multiple_of(side * width, width), width)


def prepare_kernel(proj, tokens, alternates, own, first, second, theirs, sems):
    width = own.shape[2]
    cut = first.shape[1]
    rows = tokens.shape[0]
    rep = lax.axis_index("rep")
    home, away = part(rep, width), part(1 - rep, width)
    step = rows // PIECES
    copies = moved(
        [
            (proj.at[:, :, home], own),
            (proj.at[:, :cut, home], first),
            (proj.at[:, cut:, home], second),
            (alternates.at[:, away], theirs.at[rows:]),
        ]
        + [
            (tokens.at[begin : begin + step, away], theirs.at[begin : begin + step])
            for begin in range(0, rows, step)
        ],
        sems,
    )
    for copy in copies:
        copy.wait()


def prepare(proj, tokens, alternates, width):
    kinds, height, _ = proj.shape
    count = tokens.shape[0] + alternates.shape[0]
    shapes = [(kinds, height, width)] + [(kinds, height // 2, width)] * 2
    shapes += [(count, width)]
    return pl.pallas_call(
        prepare_kernel,
        out_shape=[jax.ShapeDtypeStruct(shape, proj.dtype) for shape in shapes],
        in_specs=[ANY] * 3,
        out_specs=[VMEM] * 4,
        scratch_shapes=[pltpu.SemaphoreType.DMA((4 + PIECES,))],
        compiler_params=pltpu.CompilerParams(vmem_limit_bytes=60 << 20),
        name="prepare",
    )(proj, tokens, alternates)


def dots(tokens, panel, give, keep):
    kinds, _, lanes = give.shape
    size = kinds * lanes
    for begin, out in ((size, give), (0, keep)):
        result = lax.dot_general(
            tokens[...],
            panel[begin : begin + size],
            (((1,), (1,)), ((), ())),
            preferred_element_type=jnp.float32,
        )
        for kind in range(kinds):
            out[kind] = result[:, kind * lanes : (kind + 1) * lanes]


def theirs_kernel(theirs, *refs):
    blocks, (give, keep, panel) = refs[:-3], refs[-3:]
    kinds, _, lanes = give.shape
    quarter = lanes // 4
    seq = lax.axis_index("seq")
    swap = lax.axis_index("grp") ^ (seq // 4)
    done = 0
    for block in blocks:
        height = block.shape[1]
        order = done // quarter
        side = ((order // 4) ^ swap) * kinds * lanes
        at = ((seq % 4) ^ (order % 4)) * quarter + done % quarter
        for kind in range(kinds):
            panel[pl.ds(pl.multiple_of(side + kind * lanes + at, 16), height), :] = block[kind]
        done += height
    dots(theirs, panel, give, keep)


def ours_kernel(tokens, alternates, panel, give, keep, ours, sems):
    rows = tokens.shape[0]
    home = part(lax.axis_index("rep"), ours.shape[1])
    copies = moved(
        [(tokens.at[:, home], ours.at[:rows]), (alternates.at[:, home], ours.at[rows:])], sems
    )
    for copy in copies:
        copy.wait()
    dots(ours, panel, give, keep)


def products(tokens, alternates, theirs, blocks):
    count, width = theirs.shape
    kinds = blocks[0].shape[0]
    lanes = sum(block.shape[1] for block in blocks) // 2
    half = jax.ShapeDtypeStruct((kinds, count, lanes), jnp.float32)
    params = pltpu.CompilerParams(vmem_limit_bytes=10 << 20)
    cost = pl.CostEstimate(
        flops=4 * count * kinds * lanes * width,
        bytes_accessed=2 * width * (count + 2 * kinds * lanes) + 8 * kinds * count * lanes,
        transcendentals=0,
    )
    give_other, keep_other, panel = pl.pallas_call(
        theirs_kernel,
        out_shape=[half, half, jax.ShapeDtypeStruct((2 * kinds * lanes, width), theirs.dtype)],
        in_specs=[VMEM] * (1 + len(blocks)),
        out_specs=[VMEM] * 3,
        compiler_params=params,
        cost_estimate=cost,
        name="theirs",
    )(theirs, *blocks)
    give_mine, keep_mine = pl.pallas_call(
        ours_kernel,
        out_shape=[half, half],
        in_specs=[ANY, ANY, VMEM],
        out_specs=[VMEM] * 2,
        scratch_shapes=[pltpu.VMEM((count, width), theirs.dtype), pltpu.SemaphoreType.DMA((2,))],
        compiler_params=params,
        cost_estimate=cost,
        name="ours",
    )(tokens, alternates, panel)
    return give_other, keep_other, give_mine, keep_mine


def spread_kernel(filters, out):
    groups, lanes = filters.shape[0], out.shape[1]
    row = lax.broadcasted_iota(jnp.int32, (groups, lanes), 0)
    lane = lax.broadcasted_iota(jnp.int32, (groups, lanes), 1)
    out[...] = lax.dot_general(
        filters[...],
        jnp.where(lane // GROUP == row, 1.0, 0.0),
        (((0,), (0,)), ((), ())),
        precision=lax.Precision.HIGHEST,
        preferred_element_type=jnp.float32,
    )


def spread(filters):
    groups, span = filters.shape
    return pl.pallas_call(
        spread_kernel,
        out_shape=jax.ShapeDtypeStruct((span, groups * GROUP), jnp.float32),
        in_specs=[VMEM],
        out_specs=VMEM,
        compiler_params=pltpu.CompilerParams(vmem_limit_bytes=2 << 20),
        name="spread",
    )(filters)


def mixer_kernel(
    rows, reach, picks, feature, before, after, grad, taps, filters, out, effects,
    query, key, value, product, back_filtered, grads, summed,
):
    span = filters.shape[0]
    variants = picks.shape[0]
    first = lax.axis_index("seq") * rows
    ahead = rows + EDGE
    query[:EDGE] = before[2 * reach :]
    query[EDGE : EDGE + rows] = feature[0, :rows]
    query[EDGE + rows :] = after[:reach]
    for index, extended in ((1, key), (2, value)):
        extended[:reach] = before[(index - 1) * reach : index * reach]
        extended[reach : reach + rows] = feature[index, :rows]
        extended[reach + rows :] = after[reach + (index - 1) * EDGE : reach + index * EDGE]

    def tap(offset, index):
        return taps[offset, index : index + 1, :]

    def mixed(extended, index, begin, count):
        total = tap(0, index) * extended[begin : begin + count]
        for offset in (1, 2):
            total = total + tap(offset, index) * extended[begin - offset : begin - offset + count]
        return total

    shift = reach - span
    product[...] = mixed(key, 1, shift, span + ahead) * mixed(value, 2, shift, span + ahead)
    back_filtered[:rows] = grad[...].astype(jnp.float32) * mixed(query, 0, EDGE, rows)
    back_filtered[rows:] = after[reach + 2 * EDGE :] * mixed(query, 0, EDGE + rows, reach)

    def long_filter(source, later):
        def accumulate(block, total):
            for inner in range(8):
                offset = block * 8 + inner
                begin = offset if later else span - offset
                total = total + filters[pl.ds(offset, 1), :] * source[pl.ds(begin, ahead), :]
            return total

        return lax.fori_loop(
            0, span // 8, accumulate, jnp.zeros((ahead, filters.shape[1]), jnp.float32)
        )

    filtered = long_filter(product, False)
    grads[0, :rows] = grad[...].astype(jnp.float32) * filtered[:rows]
    grads[0, rows:] = after[reach + 2 * EDGE : reach + 3 * EDGE] * filtered[rows:]
    back_product = long_filter(back_filtered, True)
    grads[1] = back_product * mixed(value, 2, reach, ahead)
    grads[2] = back_product * mixed(key, 1, reach, ahead)
    total = jnp.zeros((rows, filters.shape[1]), jnp.float32)
    for index in range(3):
        back = tap(0, index) * grads[index, :rows]
        for offset in (1, 2):
            back = back + tap(offset, index) * grads[index, offset : offset + rows]
        back = back.astype(jnp.bfloat16).astype(jnp.float32)
        grads[index, :rows] = back
        total = total + back * feature[index, :rows]
    summed[:rows] = total
    for variant in range(variants):
        at = picks[variant] - first
        change = jnp.zeros((1, filters.shape[1]), jnp.float32)
        for index in range(3):
            alternate = feature[index, rows + variant : rows + variant + 1]
            present = feature[index, pl.ds(at, 1)]
            change = change + grads[index, pl.ds(at, 1)] * (alternate - present)
        summed[rows + variant : rows + variant + 1] = change
    scores = lax.dot_general(
        jnp.full((8, filters.shape[1]), 1.0, jnp.float32),
        summed[...],
        (((1,), (1,)), ((), ())),
        precision=lax.Precision.HIGHEST,
        preferred_element_type=jnp.float32,
    )
    scores = scores * D ** (-0.5)
    out[...] = scores[0, :rows]
    effects[...] = scores[0, rows:]


def mixer(picks, feature, before, after, grad, taps, filters):
    rows, lanes = grad.shape
    span = filters.shape[0]
    reach = span + EDGE
    count = feature.shape[1]

    def body(*refs):
        mixer_kernel(rows, reach, *refs)

    return pl.pallas_call(
        body,
        out_shape=[
            jax.ShapeDtypeStruct((rows,), jnp.float32),
            jax.ShapeDtypeStruct((count - rows,), jnp.float32),
        ],
        in_specs=[SMEM] + [VMEM] * 6,
        out_specs=[VMEM, VMEM],
        scratch_shapes=[
            pltpu.VMEM((EDGE + rows + reach, lanes), jnp.float32),
            pltpu.VMEM((reach + rows + EDGE, lanes), jnp.float32),
            pltpu.VMEM((reach + rows + EDGE, lanes), jnp.float32),
            pltpu.VMEM((span + rows + EDGE, lanes), jnp.float32),
            pltpu.VMEM((rows + reach, lanes), jnp.float32),
            pltpu.VMEM((3, rows + EDGE, lanes), jnp.float32),
            pltpu.VMEM((count, lanes), jnp.float32),
        ],
        compiler_params=pltpu.CompilerParams(vmem_limit_bytes=8 << 20),
        name="mixer",
    )(picks, feature, before, after, grad, taps, filters)


def gathered_features(tokens, proj, lanes):
    rep, half = lax.axis_index("rep"), lax.axis_index("grp")
    width = proj.shape[2] // lax.axis_size("rep")
    count = sum(piece.shape[0] for piece in tokens)

    def columns(side):
        return jnp.concatenate(
            [lax.dynamic_slice_in_dim(piece, side * width, width, 1) for piece in tokens], 0
        )

    theirs = crossed(columns(1 - rep), "rep", 1)
    panels = lax.all_gather(
        lax.dynamic_slice_in_dim(proj, rep * width, width, 2), "seq", axis=1, tiled=True
    )
    both = jnp.concatenate([columns(rep), theirs], 0)
    partial = jnp.einsum("td,fcd->ftc", both, panels, preferred_element_type=jnp.float32)
    keep = lax.dynamic_slice_in_dim(partial, half * lanes, lanes, 2)
    give = lax.dynamic_slice_in_dim(partial, (1 - half) * lanes, lanes, 2)
    chip = keep + crossed(give, "grp", 1)
    return chip[:, :count] + crossed(chip[:, count:], "rep", 1)


def cube_features(tokens, alternates, proj, early):
    width = proj.shape[2] // lax.axis_size("rep")
    bar = lax.optimization_barrier

    own, own_a, own_b, theirs = prepare(proj, tokens, alternates, width)
    own_4a = crossed(own_a, "seq", 4)
    own_4b = crossed(own_b, "seq", 4)
    own_2 = crossed(own, "seq", 2)
    own_1 = crossed(own, "seq", 1)
    theirs = crossed(theirs, "rep", 1)
    own_2, own_1, own_4a = bar((own_2, own_1, own_4a))
    own_3 = crossed(own_2, "seq", 1)
    own_4a, own_4b, own_3, early = bar((own_4a, own_4b, own_3, early))
    own_6a = crossed(own_4a, "seq", 2)
    own_6b = crossed(own_4b, "seq", 2)
    own_5b = crossed(own_4b, "seq", 1)
    own_5a = crossed(own_4a, "seq", 1)
    own_6a, own_6b, own_5a, own_5b = bar((own_6a, own_6b, own_5a, own_5b))
    own_7a = crossed(own_6a, "seq", 1)
    own_7b = crossed(own_5b, "seq", 2)

    near = own, own_1, own_2, own_3
    far = own_4a, own_4b, own_5a, own_5b, own_6a, own_6b, own_7a, own_7b
    give_other, keep_other, give_mine, keep_mine = products(tokens, alternates, theirs, near + far)
    other = crossed(keep_other + crossed(give_other, "grp", 1), "rep", 1)
    return keep_mine + crossed(give_mine, "grp", 1) + other, early


def per_device(hidden, proj, short_taps, filters, grad_out, var_pos, alt_hidden):
    rows = hidden.shape[0]
    lanes = grad_out.shape[1]
    reach = filters.shape[1] + EDGE
    early = spread(filters), short_taps, var_pos
    if lax.axis_size("seq") == 8:
        feature, early = cube_features(hidden, alt_hidden, proj, early)
    else:
        feature = gathered_features((hidden, alt_hidden), proj, lanes)
    per_channel, short_taps, picks = early
    before = shifted(
        jnp.concatenate(
            [
                feature[1, rows - reach : rows],
                feature[2, rows - reach : rows],
                feature[0, rows - EDGE : rows],
            ],
            0,
        ),
        "seq",
        1,
    )
    after = shifted(
        jnp.concatenate(
            [
                feature[0, :reach],
                feature[1, :EDGE],
                feature[2, :EDGE],
                grad_out[:reach].astype(jnp.float32),
            ],
            0,
        ), "seq", -1
    )
    scores = mixer(
        picks, feature, before, after, grad_out, short_taps, per_channel
    )
    return tuple(lax.psum(tuple(scores), "grp"))


def solution(mesh):
    in_specs = (
        P(("rep", "seq"), "grp"),
        P(None, "seq", "grp"),
        P(None, None, "grp"),
        P("grp", None),
        P(("rep", "seq"), "grp"),
        P(("rep", "seq")),
        P(("rep", "seq"), "grp"),
    )
    out_specs = (P(("rep", "seq")), P(("rep", "seq")))
    return jax.shard_map(
        per_device, mesh=mesh, in_specs=in_specs, out_specs=out_specs, check_vma=False
    )
```

time: 121 us -> 86.7 us (0.72)
  waiting for transfers between devices: 68.6 us -> 49.2 us
  between operations: 14.2 us -> 0.78 us
  starting transfers between devices: 11.3 us -> 20.2 us
  local copies, waits for them, and re-layouts: 8.37 us -> 1.05 us
  Pallas kernels: 6.12 us -> 11.4 us
  matrix products: 4.6 us -> 0 us
  other arithmetic: 1.87 us -> 0.14 us
    all_gather x1 -> x0, waiting for transfers between devices: 30.5 us -> none  [per_device(): lax.all_gather(lax.dynamic_slice_in_dim(proj, rep * width, width, 2), 'se...]
    ppermute x3 -> x15, starting transfers between devices: 2 us -> 14 us  [crossed(): lax.ppermute(block, axis, [(i, i ^ bit) for i in range(lax.axis_size(axis...]
    ppermute x3 -> x15, waiting for transfers between devices: 36.9 us -> 43.9 us  [crossed(): lax.ppermute(block, axis, [(i, i ^ bit) for i in range(lax.axis_size(axis...]
    pallas_call x1 -> x5, Pallas kernels: 6.12 us -> 11.4 us  [the longest x1 5.1 us: mixer(): pl.pallas_call(body, out_shape=[jax.ShapeDtypeStruct((rows,), jnp.float32...]
    dot_general x1 -> x0, matrix products: 4.6 us -> none  [per_device(): jnp.einsum('td,fcd->ftc', both, panels, preferred_element_type=jnp.float32)]
    ppermute x3 -> x2, waiting for transfers between devices: 1.1 us -> 5.28 us  [shifted(): return lax.ppermute(block, axis, route)]
    ppermute x3 -> x2, starting transfers between devices: 9.28 us -> 6.18 us  [shifted(): return lax.ppermute(block, axis, route)]
    unnamed x23 -> x14, local copies, waits for them, and re-layouts: 3.56 us -> 1.03 us
  transfers between devices with their start and end apart: 7 -> 17, of which waited for: 5 -> 11; matrix products, arithmetic and copies ran while one was open for 4% -> 0% of each run, Pallas kernels for 0% -> 2%
where the time goes in v3:
time: 86.7 us; the launch traced here: 86.1 us
  waiting for transfers between devices  49.2 us (57%)
  starting transfers between devices  20.2 us (23%)
  Pallas kernels  11.4 us (13%)
  blocking collectives  3.36 us (4%)
  local copies, waits for them, and re-layouts  1.05 us (1%)
    ppermute x15, waiting for transfers between devices, crossed(): lax.ppermute(block, axis, [(i, i ^ bit) for i in range(lax.axis_size(axis...  43.9 us
    ppermute x15, starting transfers between devices, crossed(): lax.ppermute(block, axis, [(i, i ^ bit) for i in range(lax.axis_size(axis...  14 us
    ppermute x2, starting transfers between devices, shifted(): return lax.ppermute(block, axis, route)  6.18 us
    ppermute x2, waiting for transfers between devices, shifted(): return lax.ppermute(block, axis, route)  5.28 us
    pallas_call x1, Pallas kernels, mixer(): pl.pallas_call(body, out_shape=[jax.ShapeDtypeStruct((rows,), jnp.float32...  5.1 us
    psum x1, blocking collectives, per_device(): return tuple(lax.psum(tuple(scores), 'grp'))  3.36 us
    pallas_call x1, Pallas kernels, prepare(): pl.pallas_call(prepare_kernel, out_shape=[jax.ShapeDtypeStruct(shape, pro...  2.9 us
  transfers between devices with their start and end apart: 17, of which 11 were waited for; matrix products, arithmetic and copies ran while one was open for 0% of the time, Pallas kernels for 2%

profile of v3, /device:TPU:23, one launch (start us, length us, event | category | flops | bytes accessed | tf_op | source)
XLA Modules:
  0.0 86.1 jit_solution(13885431338249344789)
XLA Ops:
  0.6 0.0 copy-start.5
  0.6 2.9 %prepare.1 = (bf16[3,32,2048]{2,1,0:T(8,128)(2,1)}, bf16[3,16,2048]{2,1,0:T(8,128)(2,1)}, bf16[3,16,2048]{2,1,0:T(8,128)(2,1)}, bf16[288,2048]{1,0:T(8,128)(2,1)}) custom-call(bf16[3,32,4096]{2,1,0:T(8,128)(2,1)} %proj.1, bf16[272,4096]{1,0:T(8,128)(2,1)} %tokens.3, bf16[16,4096]{1,0:T(8,128)(2,1)} %alternates.3), custom_call_target="tpu_custom_call" | custom-call | tf_op jit(solution)/shard_map/prepare/pallas_call | solution.py:72
  3.5 0.0 copy-start
  3.6 0.0 copy-start.1
  3.6 1.4 %collective-permute-start = (bf16[3,32,2048]{2,1,0:T(8,128)(2,1)}, bf16[3,32,2048]{2,1,0:T(8,128)(2,1)S(1)}, u32[]{:S(2)}, u32[]{:S(2)}) collective-permute-start(bf16[3,32,2048]{2,1,0:T(8,128)(2,1)} %get-tuple-element.26.refs_0_), channel_id=1, source_target_pairs={{0,4},{2,6},{4,0},{6,2},{8,12},{10,14},{12,8},{14,10},{1,5},{3,7},... | collective-permute-start | bytes 1179656 | tf_op jit(solution)/shard_map/ppermute | solution.py:26
  4.9 0.3 collective-permute-start.1
  5.2 0.2 collective-permute-start.5
  5.4 0.1 collective-permute-start.2
  5.5 12.5 %collective-permute-done.2.refs_4_ = bf16[3,16,2048]{2,1,0:T(8,128)(2,1)S(1)} collective-permute-done((bf16[3,16,2048]{2,1,0:T(8,128)(2,1)}, bf16[3,16,2048]{2,1,0:T(8,128)(2,1)S(1)}, u32[]{:S(2)}, u32[]{:S(2)}) %collective-permute-start.2) | collective-permute-done | bytes 196640 | tf_op jit(solution)/shard_map/ppermute | solution.py:26
  17.9 0.0 collective-permute-done.refs_2_
  17.9 0.0 collective-permute-done.1.refs_1_
  17.9 0.3 collective-permute-start.4
  18.2 0.2 collective-permute-start.3
  18.4 0.0 copy-done.5
  18.4 0.3 spread.1.refs_6_
  18.6 5.3 %collective-permute-done.3.refs_5_ = bf16[3,16,2048]{2,1,0:T(8,128)(2,1)S(1)} collective-permute-done((bf16[3,16,2048]{2,1,0:T(8,128)(2,1)}, bf16[3,16,2048]{2,1,0:T(8,128)(2,1)S(1)}, u32[]{:S(2)}, u32[]{:S(2)}) %collective-permute-start.3) | collective-permute-done | bytes 196640 | tf_op jit(solution)/shard_map/ppermute | solution.py:26
  23.9 3.1 %collective-permute-done.4.refs_3_ = bf16[3,32,2048]{2,1,0:T(8,128)(2,1)S(1)} collective-permute-done((bf16[3,32,2048]{2,1,0:T(8,128)(2,1)S(1)}, bf16[3,32,2048]{2,1,0:T(8,128)(2,1)S(1)}, u32[]{:S(2)}, u32[]{:S(2)}) %collective-permute-start.4) | collective-permute-done | bytes 393248 | tf_op jit(solution)/shard_map/ppermute | solution.py:26
  27.0 4.4 %collective-permute-start.6 = (bf16[3,16,2048]{2,1,0:T(8,128)(2,1)S(1)}, bf16[3,16,2048]{2,1,0:T(8,128)(2,1)S(1)}, u32[]{:S(2)}, u32[]{:S(2)}) collective-permute-start(bf16[3,16,2048]{2,1,0:T(8,128)(2,1)S(1)} %collective-permute-done.2.refs_4_), channel_id=1, source_target_pairs={{0,4},{2,6},{4,0},{6,2},{8,12},{10,14},{12,8},{14,10},{1,5},{3,7},... | collective-permute-start | bytes 589832 | tf_op jit(solution)/shard_map/ppermute | solution.py:26
  31.4 0.0 collective-permute-start.7
  31.5 1.2 %collective-permute-start.8 = (bf16[3,16,2048]{2,1,0:T(8,128)(2,1)S(1)}, bf16[3,16,2048]{2,1,0:T(8,128)(2,1)S(1)}, u32[]{:S(2)}, u32[]{:S(2)}) collective-permute-start(bf16[3,16,2048]{2,1,0:T(8,128)(2,1)S(1)} %collective-permute-done.2.refs_4_), channel_id=1, source_target_pairs={{0,2},{2,0},{4,6},{6,4},{8,10},{10,8},{12,14},{14,12},{1,3},{3,1},... | collective-permute-start | bytes 589832 | tf_op jit(solution)/shard_map/ppermute | solution.py:26
  32.7 0.3 collective-permute-start.9
  32.9 3.2 %collective-permute-done.6.refs_8_ = bf16[3,16,2048]{2,1,0:T(8,128)(2,1)S(1)} collective-permute-done((bf16[3,16,2048]{2,1,0:T(8,128)(2,1)S(1)}, bf16[3,16,2048]{2,1,0:T(8,128)(2,1)S(1)}, u32[]{:S(2)}, u32[]{:S(2)}) %collective-permute-start.6) | collective-permute-done | bytes 196640 | tf_op jit(solution)/shard_map/ppermute | solution.py:26
  36.2 4.2 %collective-permute-done.7.refs_9_ = bf16[3,16,2048]{2,1,0:T(8,128)(2,1)S(1)} collective-permute-done((bf16[3,16,2048]{2,1,0:T(8,128)(2,1)S(1)}, bf16[3,16,2048]{2,1,0:T(8,128)(2,1)S(1)}, u32[]{:S(2)}, u32[]{:S(2)}) %collective-permute-start.7) | collective-permute-done | bytes 196640 | tf_op jit(solution)/shard_map/ppermute | solution.py:26
  40.4 0.0 collective-permute-done.8.refs_6_
  40.4 0.9 collective-permute-done.9.refs_7_
  41.3 1.2 %collective-permute-start.10 = (bf16[3,16,2048]{2,1,0:T(8,128)(2,1)S(1)}, bf16[3,16,2048]{2,1,0:T(8,128)(2,1)S(1)}, u32[]{:S(2)}, u32[]{:S(2)}) collective-permute-start(bf16[3,16,2048]{2,1,0:T(8,128)(2,1)S(1)} %collective-permute-done.6.refs_8_), channel_id=1, source_target_pairs={{0,2},{2,0},{4,6},{6,4},{8,10},{10,8},{12,14},{14,12},{1,3},{3,1},... | collective-permute-start | bytes 589832 | tf_op jit(solution)/shard_map/ppermute | solution.py:26
  42.5 1.1 %collective-permute-start.11 = (bf16[3,16,2048]{2,1,0:T(8,128)(2,1)S(1)}, bf16[3,16,2048]{2,1,0:T(8,128)(2,1)S(1)}, u32[]{:S(2)}, u32[]{:S(2)}) collective-permute-start(bf16[3,16,2048]{2,1,0:T(8,128)(2,1)S(1)} %collective-permute-done.9.refs_7_), channel_id=1, source_target_pairs={{0,4},{2,6},{4,0},{6,2},{8,12},{10,14},{12,8},{14,10},{1,5},{3,7},... | collective-permute-start | bytes 589832 | tf_op jit(solution)/shard_map/ppermute | solution.py:26
  43.6 2.2 %collective-permute-done.10.refs_10_ = bf16[3,16,2048]{2,1,0:T(8,128)(2,1)S(1)} collective-permute-done((bf16[3,16,2048]{2,1,0:T(8,128)(2,1)S(1)}, bf16[3,16,2048]{2,1,0:T(8,128)(2,1)S(1)}, u32[]{:S(2)}, u32[]{:S(2)}) %collective-permute-start.10) | collective-permute-done | bytes 196640 | tf_op jit(solution)/shard_map/ppermute | solution.py:26
  45.8 1.5 %collective-permute-done.11.refs_11_ = bf16[3,16,2048]{2,1,0:T(8,128)(2,1)S(1)} collective-permute-done((bf16[3,16,2048]{2,1,0:T(8,128)(2,1)S(1)}, bf16[3,16,2048]{2,1,0:T(8,128)(2,1)S(1)}, u32[]{:S(2)}, u32[]{:S(2)}) %collective-permute-start.11) | collective-permute-done | bytes 196640 | tf_op jit(solution)/shard_map/ppermute | solution.py:26
  47.3 0.0 collective-permute-done.5.theirs
  47.3 0.0 copy-start.2
  47.3 1.0 %copy-done.2 = bf16[3,32,2048]{2,1,0:T(8,128)(2,1)S(1)} copy-done((bf16[3,32,2048]{2,1,0:T(8,128)(2,1)S(1)}, bf16[3,32,2048]{2,1,0:T(8,128)(2,1)}, u32[]{:S(2)}) %copy-start.2) | copy-done | bytes 393240
  48.3 1.6 %theirs.1 = (f32[3,288,128]{2,1,0:T(8,128)S(1)}, f32[3,288,128]{2,1,0:T(8,128)S(1)}, bf16[768,2048]{1,0:T(8,128)(2,1)S(1)}) custom-call(bf16[288,2048]{1,0:T(8,128)(2,1)S(1)} %collective-permute-done.5.theirs, bf16[3,32,2048]{2,1,0:T(8,128)(2,1)S(1)} %copy-done.2, bf16[3,32,2048]{2,1,0:T(8,128)(2,1)S(1)} %collective-permute-done.1.refs_1_, ...), custom_call_target="tpu_custom_call" | custom-call | flops 905969664 | bytes 5210112 | tf_op jit(solution)/shard_map/theirs/pallas_call | solution.py:137
  49.9 3.0 %collective-permute-start.13 = (f32[3,288,128]{2,1,0:T(8,128)S(1)}, f32[3,288,128]{2,1,0:T(8,128)S(1)}, u32[]{:S(2)}, u32[]{:S(2)}) collective-permute-start(f32[3,288,128]{2,1,0:T(8,128)S(1)} %get-tuple-element.45), channel_id=1, source_target_pairs={{0,1},{1,0},{2,3},{3,2},{4,5},{5,4},{6,7},{7,6},{8,9},{9,8},{10,11... | collective-permute-start | bytes 1327112 | tf_op jit(solution)/shard_map/ppermute | solution.py:26
  52.9 0.0 copy-done
  52.9 0.0 copy-done.1
  52.9 0.0 copy-start.3
  52.9 1.6 %ours.1 = (f32[3,288,128]{2,1,0:T(8,128)S(1)}, f32[3,288,128]{2,1,0:T(8,128)S(1)}) custom-call(bf16[272,4096]{1,0:T(8,128)(2,1)S(1)} %copy-done, bf16[16,4096]{1,0:T(8,128)(2,1)S(1)} %copy-done.1, bf16[768,2048]{1,0:T(8,128)(2,1)S(1)} %get-tuple-element.41.panel), custom_call_target="tpu_custom_call" | custom-call | flops 905969664 | bytes 5210112 | tf_op jit(solution)/shard_map/ours/pallas_call | solution.py:146
  54.4 0.0 copy-start.4
  54.4 0.0 copy-start.6
  54.5 0.1 collective-permute-start.12
  54.6 0.0 collective-permute-done.13
  54.6 0.3 collective-permute-start.14
  54.9 0.0 copy-done.3
  54.9 1.4 %collective-permute-done.12 = f32[3,288,128]{2,1,0:T(8,128)S(1)} collective-permute-done((f32[3,288,128]{2,1,0:T(8,128)S(1)}, f32[3,288,128]{2,1,0:T(8,128)S(1)}, u32[]{:S(2)}, u32[]{:S(2)}) %collective-permute-start.12) | collective-permute-done | bytes 442400 | tf_op jit(solution)/shard_map/ppermute | solution.py:26
  56.3 9.7 %collective-permute-done.14 = f32[3,288,128]{2,1,0:T(8,128)S(1)} collective-permute-done((f32[3,288,128]{2,1,0:T(8,128)S(1)}, f32[3,288,128]{2,1,0:T(8,128)S(1)}, u32[]{:S(2)}, u32[]{:S(2)}) %collective-permute-start.14) | collective-permute-done | bytes 442400 | tf_op jit(solution)/shard_map/ppermute | solution.py:26
  66.0 0.1 add_add_fusion.refs_1_
  66.1 2.2 %collective-permute-start.16 = (f32[288,128]{1,0:T(8,128)S(1)}, f32[288,128]{1,0:T(8,128)S(1)}, u32[]{:S(2)}, u32[]{:S(2)}) collective-permute-start(f32[288,128]{1,0:T(8,128)S(1)} %pad_maximum_fusion), channel_id=1, source_target_pairs={{2,0},{4,2},{6,4},{8,6},{10,8},{12,10},{14,12},{3,1},{5,3},{7,5},{... | collective-permute-start | bytes 442376 | tf_op jit(solution)/shard_map/ppermute | solution.py:22
  68.3 4.0 %collective-permute-start.15 = (f32[280,128]{1,0:T(8,128)S(1)}, f32[280,128]{1,0:T(8,128)S(1)}, u32[]{:S(2)}, u32[]{:S(2)}) collective-permute-start(f32[280,128]{1,0:T(8,128)S(1)} %pad_maximum_fusion.1), channel_id=1, source_target_pairs={{0,2},{2,4},{4,6},{6,8},{8,10},{10,12},{12,14},{1,3},{3,5},{5,7},{... | collective-permute-start | bytes 430088 | tf_op jit(solution)/shard_map/ppermute | solution.py:22
  72.3 5.3 %collective-permute-done.15.refs_2_ = f32[280,128]{1,0:T(8,128)S(1)} collective-permute-done((f32[280,128]{1,0:T(8,128)S(1)}, f32[280,128]{1,0:T(8,128)S(1)}, u32[]{:S(2)}, u32[]{:S(2)}) %collective-permute-start.15) | collective-permute-done | bytes 143392 | tf_op jit(solution)/shard_map/ppermute | solution.py:22
  77.6 0.0 collective-permute-done.16.refs_3_
  77.6 0.0 copy-done.4
  77.6 0.0 copy-done.6
  77.6 5.1 %mixer.1 = (f32[272]{0:T(512)S(1)}, f32[16]{0:T(128)S(1)}) custom-call(s32[16]{0:T(128)S(1)} %copy-done.6, f32[3,288,128]{2,1,0:T(8,128)S(1)} %add_add_fusion.refs_1_, f32[280,128]{1,0:T(8,128)S(1)} %collective-permute-done.15.refs_2_, f32[288,128]{1,0:T(8,128)S(1)} %collective-permute-done.16.refs_3_, bf16[272,128]{1,0:T(8,128)(2,1)S(1)} %copy-done.3, ...), custom_call_target="tpu_custom_call" | custom-call | tf_op jit(solution)/shard_map/mixer/pallas_call | solution.py:270
  82.7 3.4 %all-reduce = (f32[272]{0:T(512)}, f32[16]{0:T(128)}) all-reduce(f32[272]{0:T(512)S(1)} %get-tuple-element.48, f32[16]{0:T(128)S(1)} %get-tuple-element.49), channel_id=1, replica_groups=mesh['rep'=2,'seq'=8,'grp'=2] {'grp'}, use_global_device_ids=true, to_apply=%region_0.0 | all-reduce | flops 288 | bytes 2304 | tf_op jit(solution)/shard_map/psum | solution.py:378
  (6 shorter events, 0.1 us)
Async XLA Ops:
  0.6 17.7 %copy-start.5 = (f32[8,128]{1,0:T(8,128)S(1)}, f32[8,128]{1,0:T(8,128)}, u32[]{:S(2)}) copy-start(f32[8,128]{1,0:T(8,128)} %filters.1) | copy-start | bytes 12292
  3.5 49.3 %copy-start = (bf16[272,4096]{1,0:T(8,128)(2,1)S(1)}, bf16[272,4096]{1,0:T(8,128)(2,1)}, u32[]{:S(2)}) copy-start(bf16[272,4096]{1,0:T(8,128)(2,1)} %tokens.3) | copy-start | bytes 6684676
  3.6 49.3 %copy-start.1 = (bf16[16,4096]{1,0:T(8,128)(2,1)S(1)}, bf16[16,4096]{1,0:T(8,128)(2,1)}, u32[]{:S(2)}) copy-start(bf16[16,4096]{1,0:T(8,128)(2,1)} %alternates.3) | copy-start | bytes 393220
  3.6 14.4 %collective-permute-start = (bf16[3,32,2048]{2,1,0:T(8,128)(2,1)}, bf16[3,32,2048]{2,1,0:T(8,128)(2,1)S(1)}, u32[]{:S(2)}, u32[]{:S(2)}) collective-permute-start(bf16[3,32,2048]{2,1,0:T(8,128)(2,1)} %get-tuple-element.26.refs_0_), channel_id=1, source_target_pairs={{0,4},{2,6},{4,0},{6,2},{8,12},{10,14},{12,8},{14,10},{1,5},{3,7},... | collective-permute-start | bytes 1179656 | tf_op jit(solution)/shard_map/ppermute | solution.py:26
  4.9 13.0 %collective-permute-start.1 = (bf16[3,32,2048]{2,1,0:T(8,128)(2,1)}, bf16[3,32,2048]{2,1,0:T(8,128)(2,1)S(1)}, u32[]{:S(2)}, u32[]{:S(2)}) collective-permute-start(bf16[3,32,2048]{2,1,0:T(8,128)(2,1)} %get-tuple-element.26.refs_0_), channel_id=1, source_target_pairs={{0,2},{2,0},{4,6},{6,4},{8,10},{10,8},{12,14},{14,12},{1,3},{3,1},... | collective-permute-start | bytes 1179656 | tf_op jit(solution)/shard_map/ppermute | solution.py:26
  5.2 42.1 %collective-permute-start.5 = (bf16[288,2048]{1,0:T(8,128)(2,1)}, bf16[288,2048]{1,0:T(8,128)(2,1)S(1)}, u32[]{:S(2)}, u32[]{:S(2)}) collective-permute-start(bf16[288,2048]{1,0:T(8,128)(2,1)} %get-tuple-element.32), channel_id=1, source_target_pairs={{0,16},{16,0},{1,17},{17,1},{2,18},{18,2},{3,19},{19,3},{4,20},{20... | collective-permute-start | bytes 3538952 | tf_op jit(solution)/shard_map/ppermute | solution.py:26
  5.4 12.5 %collective-permute-start.2 = (bf16[3,16,2048]{2,1,0:T(8,128)(2,1)}, bf16[3,16,2048]{2,1,0:T(8,128)(2,1)S(1)}, u32[]{:S(2)}, u32[]{:S(2)}) collective-permute-start(bf16[3,16,2048]{2,1,0:T(8,128)(2,1)} %get-tuple-element.27), channel_id=1, source_target_pairs={{0,8},{2,10},{4,12},{6,14},{8,0},{10,2},{12,4},{14,6},{1,9},{3,11}... | collective-permute-start | bytes 589832 | tf_op jit(solution)/shard_map/ppermute | solution.py:26
  17.9 9.1 %collective-permute-start.4 = (bf16[3,32,2048]{2,1,0:T(8,128)(2,1)S(1)}, bf16[3,32,2048]{2,1,0:T(8,128)(2,1)S(1)}, u32[]{:S(2)}, u32[]{:S(2)}) collective-permute-start(bf16[3,32,2048]{2,1,0:T(8,128)(2,1)S(1)} %collective-permute-done.refs_2_), channel_id=1, source_target_pairs={{0,2},{2,0},{4,6},{6,4},{8,10},{10,8},{12,14},{14,12},{1,3},{3,1},... | collective-permute-start | bytes 1179656 | tf_op jit(solution)/shard_map/ppermute | solution.py:26
  18.2 5.7 %collective-permute-start.3 = (bf16[3,16,2048]{2,1,0:T(8,128)(2,1)}, bf16[3,16,2048]{2,1,0:T(8,128)(2,1)S(1)}, u32[]{:S(2)}, u32[]{:S(2)}) collective-permute-start(bf16[3,16,2048]{2,1,0:T(8,128)(2,1)} %get-tuple-element.29), channel_id=1, source_target_pairs={{0,8},{2,10},{4,12},{6,14},{8,0},{10,2},{12,4},{14,6},{1,9},{3,11}... | collective-permute-start | bytes 589832 | tf_op jit(solution)/shard_map/ppermute | solution.py:26
  27.0 9.2 %collective-permute-start.6 = (bf16[3,16,2048]{2,1,0:T(8,128)(2,1)S(1)}, bf16[3,16,2048]{2,1,0:T(8,128)(2,1)S(1)}, u32[]{:S(2)}, u32[]{:S(2)}) collective-permute-start(bf16[3,16,2048]{2,1,0:T(8,128)(2,1)S(1)} %collective-permute-done.2.refs_4_), channel_id=1, source_target_pairs={{0,4},{2,6},{4,0},{6,2},{8,12},{10,14},{12,8},{14,10},{1,5},{3,7},... | collective-permute-start | bytes 589832 | tf_op jit(solution)/shard_map/ppermute | solution.py:26
  31.4 9.0 %collective-permute-start.7 = (bf16[3,16,2048]{2,1,0:T(8,128)(2,1)S(1)}, bf16[3,16,2048]{2,1,0:T(8,128)(2,1)S(1)}, u32[]{:S(2)}, u32[]{:S(2)}) collective-permute-start(bf16[3,16,2048]{2,1,0:T(8,128)(2,1)S(1)} %collective-permute-done.3.refs_5_), channel_id=1, source_target_pairs={{0,4},{2,6},{4,0},{6,2},{8,12},{10,14},{12,8},{14,10},{1,5},{3,7},... | collective-permute-start | bytes 589832 | tf_op jit(solution)/shard_map/ppermute | solution.py:26
  31.5 8.9 %collective-permute-start.8 = (bf16[3,16,2048]{2,1,0:T(8,128)(2,1)S(1)}, bf16[3,16,2048]{2,1,0:T(8,128)(2,1)S(1)}, u32[]{:S(2)}, u32[]{:S(2)}) collective-permute-start(bf16[3,16,2048]{2,1,0:T(8,128)(2,1)S(1)} %collective-permute-done.2.refs_4_), channel_id=1, source_target_pairs={{0,2},{2,0},{4,6},{6,4},{8,10},{10,8},{12,14},{14,12},{1,3},{3,1},... | collective-permute-start | bytes 589832 | tf_op jit(solution)/shard_map/ppermute | solution.py:26
  32.7 8.6 %collective-permute-start.9 = (bf16[3,16,2048]{2,1,0:T(8,128)(2,1)S(1)}, bf16[3,16,2048]{2,1,0:T(8,128)(2,1)S(1)}, u32[]{:S(2)}, u32[]{:S(2)}) collective-permute-start(bf16[3,16,2048]{2,1,0:T(8,128)(2,1)S(1)} %collective-permute-done.3.refs_5_), channel_id=1, source_target_pairs={{0,2},{2,0},{4,6},{6,4},{8,10},{10,8},{12,14},{14,12},{1,3},{3,1},... | collective-permute-start | bytes 589832 | tf_op jit(solution)/shard_map/ppermute | solution.py:26
  41.3 4.5 %collective-permute-start.10 = (bf16[3,16,2048]{2,1,0:T(8,128)(2,1)S(1)}, bf16[3,16,2048]{2,1,0:T(8,128)(2,1)S(1)}, u32[]{:S(2)}, u32[]{:S(2)}) collective-permute-start(bf16[3,16,2048]{2,1,0:T(8,128)(2,1)S(1)} %collective-permute-done.6.refs_8_), channel_id=1, source_target_pairs={{0,2},{2,0},{4,6},{6,4},{8,10},{10,8},{12,14},{14,12},{1,3},{3,1},... | collective-permute-start | bytes 589832 | tf_op jit(solution)/shard_map/ppermute | solution.py:26
  42.5 4.8 %collective-permute-start.11 = (bf16[3,16,2048]{2,1,0:T(8,128)(2,1)S(1)}, bf16[3,16,2048]{2,1,0:T(8,128)(2,1)S(1)}, u32[]{:S(2)}, u32[]{:S(2)}) collective-permute-start(bf16[3,16,2048]{2,1,0:T(8,128)(2,1)S(1)} %collective-permute-done.9.refs_7_), channel_id=1, source_target_pairs={{0,4},{2,6},{4,0},{6,2},{8,12},{10,14},{12,8},{14,10},{1,5},{3,7},... | collective-permute-start | bytes 589832 | tf_op jit(solution)/shard_map/ppermute | solution.py:26
  47.3 1.0 %copy-start.2 = (bf16[3,32,2048]{2,1,0:T(8,128)(2,1)S(1)}, bf16[3,32,2048]{2,1,0:T(8,128)(2,1)}, u32[]{:S(2)}) copy-start(bf16[3,32,2048]{2,1,0:T(8,128)(2,1)} %get-tuple-element.26.refs_0_) | copy-start | bytes 1179652
  49.9 4.7 %collective-permute-start.13 = (f32[3,288,128]{2,1,0:T(8,128)S(1)}, f32[3,288,128]{2,1,0:T(8,128)S(1)}, u32[]{:S(2)}, u32[]{:S(2)}) collective-permute-start(f32[3,288,128]{2,1,0:T(8,128)S(1)} %get-tuple-element.45), channel_id=1, source_target_pairs={{0,1},{1,0},{2,3},{3,2},{4,5},{5,4},{6,7},{7,6},{8,9},{9,8},{10,11... | collective-permute-start | bytes 1327112 | tf_op jit(solution)/shard_map/ppermute | solution.py:26
  52.9 2.1 %copy-start.3 = (bf16[272,128]{1,0:T(8,128)(2,1)S(1)}, bf16[272,128]{1,0:T(8,128)(2,1)}, u32[]{:S(2)}) copy-start(bf16[272,128]{1,0:T(8,128)(2,1)} %refs_4_.1) | copy-start | bytes 208900
  54.4 23.2 %copy-start.4 = (f32[3,3,128]{2,1,0:T(4,128)S(1)}, f32[3,3,128]{2,1,0:T(4,128)}, u32[]{:S(2)}) copy-start(f32[3,3,128]{2,1,0:T(4,128)} %refs_5_) | copy-start | bytes 13828
  54.4 23.2 %copy-start.6 = (s32[16]{0:T(128)S(1)}, s32[16]{0:T(128)}, u32[]{:S(2)}) copy-start(s32[16]{0:T(128)} %refs_0_) | copy-start | bytes 196
  54.5 1.9 %collective-permute-start.12 = (f32[3,288,128]{2,1,0:T(8,128)S(1)}, f32[3,288,128]{2,1,0:T(8,128)S(1)}, u32[]{:S(2)}, u32[]{:S(2)}) collective-permute-start(f32[3,288,128]{2,1,0:T(8,128)S(1)} %get-tuple-element.43), channel_id=1, source_target_pairs={{0,1},{1,0},{2,3},{3,2},{4,5},{5,4},{6,7},{7,6},{8,9},{9,8},{10,11... | collective-permute-start | bytes 1327112 | tf_op jit(solution)/shard_map/ppermute | solution.py:26
  54.6 11.3 %collective-permute-start.14 = (f32[3,288,128]{2,1,0:T(8,128)S(1)}, f32[3,288,128]{2,1,0:T(8,128)S(1)}, u32[]{:S(2)}, u32[]{:S(2)}) collective-permute-start(f32[3,288,128]{2,1,0:T(8,128)S(1)} %add.14), channel_id=1, source_target_pairs={{0,16},{16,0},{1,17},{17,1},{2,18},{18,2},{3,19},{19,3},{4,20},{20... | collective-permute-start | bytes 1327112 | tf_op jit(solution)/shard_map/ppermute | solution.py:26
  66.1 11.5 %collective-permute-start.16 = (f32[288,128]{1,0:T(8,128)S(1)}, f32[288,128]{1,0:T(8,128)S(1)}, u32[]{:S(2)}, u32[]{:S(2)}) collective-permute-start(f32[288,128]{1,0:T(8,128)S(1)} %pad_maximum_fusion), channel_id=1, source_target_pairs={{2,0},{4,2},{6,4},{8,6},{10,8},{12,10},{14,12},{3,1},{5,3},{7,5},{... | collective-permute-start | bytes 442376 | tf_op jit(solution)/shard_map/ppermute | solution.py:22
  68.3 9.3 %collective-permute-start.15 = (f32[280,128]{1,0:T(8,128)S(1)}, f32[280,128]{1,0:T(8,128)S(1)}, u32[]{:S(2)}, u32[]{:S(2)}) collective-permute-start(f32[280,128]{1,0:T(8,128)S(1)} %pad_maximum_fusion.1), channel_id=1, source_target_pairs={{0,2},{2,4},{4,6},{6,8},{8,10},{10,12},{12,14},{1,3},{3,5},{5,7},{... | collective-permute-start | bytes 430088 | tf_op jit(solution)/shard_map/ppermute | solution.py:22

commit v4 on v3

--- a/solution.py
+++ b/solution.py
@@ -1,3 +1,5 @@
+import functools
+
 import jax
 import jax.numpy as jnp
 from jax import lax
@@ -16,9 +18,10 @@
 SMEM = pl.BlockSpec(memory_space=pltpu.SMEM)
 
 
-def shifted(block, axis, distance):
-    devices = range(lax.axis_size(axis))
-    route = [(i - distance, i) for i in devices if i - distance in devices]
+def paired(block, axis, first):
+    route = []
+    for left in range(first, lax.axis_size(axis) - 1, 2):
+        route += [(left, left + 1), (left + 1, left)]
     return lax.ppermute(block, axis, route)
 
 
@@ -40,20 +43,42 @@
     return pl.ds(pl.multiple_of(side * width, width), width)
 
 
-def prepare_kernel(proj, tokens, alternates, own, first, second, theirs, sems):
+def panels_kernel(proj, own, first, second, sems):
     width = own.shape[2]
     cut = first.shape[1]
-    rows = tokens.shape[0]
-    rep = lax.axis_index("rep")
-    home, away = part(rep, width), part(1 - rep, width)
-    step = rows // PIECES
+    home = part(lax.axis_index("rep"), width)
     copies = moved(
         [
             (proj.at[:, :, home], own),
             (proj.at[:, :cut, home], first),
             (proj.at[:, cut:, home], second),
-            (alternates.at[:, away], theirs.at[rows:]),
-        ]
+        ],
+        sems,
+    )
+    for copy in copies:
+        copy.wait()
+
+
+def panels(proj, width):
+    kinds, height, _ = proj.shape
+    shapes = [(kinds, height, width)] + [(kinds, height // 2, width)] * 2
+    return pl.pallas_call(
+        panels_kernel,
+        out_shape=[jax.ShapeDtypeStruct(shape, proj.dtype) for shape in shapes],
+        in_specs=[ANY],
+        out_specs=[VMEM] * 3,
+        scratch_shapes=[pltpu.SemaphoreType.DMA((3,))],
+        compiler_params=pltpu.CompilerParams(vmem_limit_bytes=2 << 20),
+        name="panels",
+    )(proj)
+
+
+def columns_kernel(tokens, alternates, theirs, sems):
+    rows = tokens.shape[0]
+    away = part(1 - lax.axis_index("rep"), theirs.shape[1])
+    step = rows // PIECES
+    copies = moved(
+        [(alternates.at[:, away], theirs.at[rows:])]
         + [
             (tokens.at[begin : begin + step, away], theirs.at[begin : begin + step])
             for begin in range(0, rows, step)
@@ -64,20 +89,17 @@
         copy.wait()
 
 
-def prepare(proj, tokens, alternates, width):
-    kinds, height, _ = proj.shape
+def columns(tokens, alternates, width):
     count = tokens.shape[0] + alternates.shape[0]
-    shapes = [(kinds, height, width)] + [(kinds, height // 2, width)] * 2
-    shapes += [(count, width)]
     return pl.pallas_call(
-        prepare_kernel,
-        out_shape=[jax.ShapeDtypeStruct(shape, proj.dtype) for shape in shapes],
-        in_specs=[ANY] * 3,
-        out_specs=[VMEM] * 4,
-        scratch_shapes=[pltpu.SemaphoreType.DMA((4 + PIECES,))],
-        compiler_params=pltpu.CompilerParams(vmem_limit_bytes=60 << 20),
-        name="prepare",
-    )(proj, tokens, alternates)
+        columns_kernel,
+        out_shape=jax.ShapeDtypeStruct((count, width), tokens.dtype),
+        in_specs=[ANY] * 2,
+        out_specs=VMEM,
+        scratch_shapes=[pltpu.SemaphoreType.DMA((1 + PIECES,))],
+        compiler_params=pltpu.CompilerParams(vmem_limit_bytes=3 << 20),
+        name="columns",
+    )(tokens, alternates)
 
 
 def dots(tokens, panel, give, keep):
@@ -181,73 +203,131 @@
     )(filters)
 
 
+def tap(taps, offset, index):
+    return taps[offset, index : index + 1, :]
+
+
+def mixed(taps, index, extended, begin, count):
+    total = tap(taps, 0, index) * extended[begin : begin + count]
+    for offset in (1, 2):
+        total = total + tap(taps, offset, index) * extended[begin - offset : begin - offset + count]
+    return total
+
+
+def edges_kernel(span, rows, grad, taps, *refs):
+    terms, (feature, within, across, before, after, head) = refs[:-6], refs[-6:]
+    for kind in range(3):
+        total = terms[0][kind]
+        for term in terms[1:]:
+            total = total + term[kind]
+        feature[kind] = total
+    begin = rows - span
+    before[:span] = mixed(taps, 1, feature.at[1], begin, span) * mixed(
+        taps, 2, feature.at[2], begin, span
+    )
+    for place, kind in enumerate((1, 2, 0)):
+        at = span + place * EDGE
+        before[at : at + EDGE] = feature[kind, rows - EDGE : rows]
+    before[span + 3 * EDGE :] = jnp.zeros((2 * EDGE, head.shape[1]), jnp.float32)
+    reach = span + EDGE
+    head[:EDGE] = jnp.zeros((EDGE, head.shape[1]), jnp.float32)
+    head[EDGE:] = feature[0, :reach]
+    slope = grad[:reach].astype(jnp.float32)
+    after[:reach] = slope * mixed(taps, 0, head, EDGE, reach)
+    for kind in range(3):
+        at = reach + kind * EDGE
+        after[at : at + EDGE] = feature[kind, :EDGE]
+    after[reach + 3 * EDGE :] = slope[:EDGE]
+    even = lax.axis_index("seq") % 2 == 0
+    within[...] = jnp.where(even, before[...], after[...])
+    across[...] = jnp.where(even, after[...], before[...])
+
+
+def edges(grad, taps, span, terms):
+    rows, lanes = grad.shape
+    size = span + 5 * EDGE
+    return pl.pallas_call(
+        functools.partial(edges_kernel, span, rows),
+        out_shape=[jax.ShapeDtypeStruct(terms[0].shape, jnp.float32)]
+        + [jax.ShapeDtypeStruct((size, lanes), jnp.float32)] * 2,
+        in_specs=[VMEM] * (2 + len(terms)),
+        out_specs=[VMEM] * 3,
+        scratch_shapes=[pltpu.VMEM((size, lanes), jnp.float32)] * 2
+        + [pltpu.VMEM((span + 2 * EDGE, lanes), jnp.float32)],
+        compiler_params=pltpu.CompilerParams(vmem_limit_bytes=6 << 20),
+        name="edges",
+    )(grad, taps, *terms)
+
+
 def mixer_kernel(
-    rows, reach, picks, feature, before, after, grad, taps, filters, out, effects,
-    query, key, value, product, back_filtered, grads, summed,
+    rows, picks, feature, within, across, grad, taps, filters, out, effects,
+    before, after, query, key, value, product, back_filtered, shifts, grads, summed,
 ):
-    span = filters.shape[0]
+    span, lanes = filters.shape
     variants = picks.shape[0]
     first = lax.axis_index("seq") * rows
     ahead = rows + EDGE
-    query[:EDGE] = before[2 * reach :]
-    query[EDGE : EDGE + rows] = feature[0, :rows]
-    query[EDGE + rows :] = after[:reach]
-    for index, extended in ((1, key), (2, value)):
-        extended[:reach] = before[(index - 1) * reach : index * reach]
-        extended[reach : reach + rows] = feature[index, :rows]
-        extended[reach + rows :] = after[reach + (index - 1) * EDGE : reach + index * EDGE]
-
-    def tap(offset, index):
-        return taps[offset, index : index + 1, :]
-
-    def mixed(extended, index, begin, count):
-        total = tap(0, index) * extended[begin : begin + count]
-        for offset in (1, 2):
-            total = total + tap(offset, index) * extended[begin - offset : begin - offset + count]
-        return total
-
-    shift = reach - span
-    product[...] = mixed(key, 1, shift, span + ahead) * mixed(value, 2, shift, span + ahead)
-    back_filtered[:rows] = grad[...].astype(jnp.float32) * mixed(query, 0, EDGE, rows)
-    back_filtered[rows:] = after[reach + 2 * EDGE :] * mixed(query, 0, EDGE + rows, reach)
+    reach = span + EDGE
+    even = lax.axis_index("seq") % 2 == 0
+    before[...] = jnp.where(even, across[...], within[...])
+    after[...] = jnp.where(even, within[...], across[...])
+    for kind, place, extended in ((1, 0, key), (2, 1, value), (0, 2, query)):
+        extended[:EDGE] = before[span + place * EDGE : span + (place + 1) * EDGE]
+        extended[EDGE:ahead] = feature[kind, :rows]
+        extended[ahead:] = after[reach + kind * EDGE : reach + (kind + 1) * EDGE]
+    slope_after = after[reach + 3 * EDGE :]
+    key[EDGE:] = mixed(taps, 1, key, EDGE, ahead)
+    value[EDGE:] = mixed(taps, 2, value, EDGE, ahead)
+    product[:span] = before[:span]
+    product[span:] = key[EDGE:] * value[EDGE:]
+    query[EDGE:] = mixed(taps, 0, query, EDGE, ahead)
+    back_filtered[:rows] = grad[...].astype(jnp.float32) * query[EDGE:ahead]
+    back_filtered[rows:ahead] = slope_after * query[ahead:]
+    back_filtered[ahead:] = after[EDGE:reach]
 
     def long_filter(source, later):
+        length = source.shape[0]
+        for shift in range(8):
+            shifts[shift, : length - shift] = source[shift:]
+
         def accumulate(block, total):
             for inner in range(8):
                 offset = block * 8 + inner
-                begin = offset if later else span - offset
-                total = total + filters[pl.ds(offset, 1), :] * source[pl.ds(begin, ahead), :]
+                if later:
+                    shift, begin = inner, block
+                else:
+                    shift, begin = -inner % 8, span // 8 - block - (inner > 0)
+                begin = pl.multiple_of(begin * 8, 8)
+                total = total + filters[pl.ds(offset, 1), :] * shifts[shift, pl.ds(begin, ahead), :]
             return total
 
-        return lax.fori_loop(
-            0, span // 8, accumulate, jnp.zeros((ahead, filters.shape[1]), jnp.float32)
-        )
+        return lax.fori_loop(0, span // 8, accumulate, jnp.zeros((ahead, lanes), jnp.float32))
 
     filtered = long_filter(product, False)
     grads[0, :rows] = grad[...].astype(jnp.float32) * filtered[:rows]
-    grads[0, rows:] = after[reach + 2 * EDGE : reach + 3 * EDGE] * filtered[rows:]
+    grads[0, rows:] = slope_after * filtered[rows:]
     back_product = long_filter(back_filtered, True)
-    grads[1] = back_product * mixed(value, 2, reach, ahead)
-    grads[2] = back_product * mixed(key, 1, reach, ahead)
-    total = jnp.zeros((rows, filters.shape[1]), jnp.float32)
+    grads[1] = back_product * value[EDGE:]
+    grads[2] = back_product * key[EDGE:]
+    total = jnp.zeros((rows, lanes), jnp.float32)
     for index in range(3):
-        back = tap(0, index) * grads[index, :rows]
+        back = tap(taps, 0, index) * grads[index, :rows]
         for offset in (1, 2):
-            back = back + tap(offset, index) * grads[index, offset : offset + rows]
+            back = back + tap(taps, offset, index) * grads[index, offset : offset + rows]
         back = back.astype(jnp.bfloat16).astype(jnp.float32)
         grads[index, :rows] = back
         total = total + back * feature[index, :rows]
     summed[:rows] = total
     for variant in range(variants):
         at = picks[variant] - first
-        change = jnp.zeros((1, filters.shape[1]), jnp.float32)
+        change = jnp.zeros((1, lanes), jnp.float32)
         for index in range(3):
             alternate = feature[index, rows + variant : rows + variant + 1]
             present = feature[index, pl.ds(at, 1)]
             change = change + grads[index, pl.ds(at, 1)] * (alternate - present)
         summed[rows + variant : rows + variant + 1] = change
     scores = lax.dot_general(
-        jnp.full((8, filters.shape[1]), 1.0, jnp.float32),
+        jnp.full((8, lanes), 1.0, jnp.float32),
         summed[...],
         (((1,), (1,)), ((), ())),
         precision=lax.Precision.HIGHEST,
@@ -258,15 +338,15 @@
     effects[...] = scores[0, rows:]
 
 
-def mixer(picks, feature, before, after, grad, taps, filters):
+def mixer(picks, feature, within, across, grad, taps, filters):
     rows, lanes = grad.shape
     span = filters.shape[0]
-    reach = span + EDGE
     count = feature.shape[1]
 
     def body(*refs):
-        mixer_kernel(rows, reach, *refs)
-
+        mixer_kernel(rows, *refs)
+
+    length = span + rows + EDGE
     return pl.pallas_call(
         body,
         out_shape=[
@@ -275,18 +355,18 @@
         ],
         in_specs=[SMEM] + [VMEM] * 6,
         out_specs=[VMEM, VMEM],
-        scratch_shapes=[
-            pltpu.VMEM((EDGE + rows + reach, lanes), jnp.float32),
-            pltpu.VMEM((reach + rows + EDGE, lanes), jnp.float32),
-            pltpu.VMEM((reach + rows + EDGE, lanes), jnp.float32),
-            pltpu.VMEM((span + rows + EDGE, lanes), jnp.float32),
-            pltpu.VMEM((rows + reach, lanes), jnp.float32),
+        scratch_shapes=[pltpu.VMEM((span + 5 * EDGE, lanes), jnp.float32)] * 2
+        + [pltpu.VMEM((rows + 2 * EDGE, lanes), jnp.float32)] * 3
+        + [
+            pltpu.VMEM((length, lanes), jnp.float32),
+            pltpu.VMEM((length, lanes), jnp.float32),
+            pltpu.VMEM((8, length, lanes), jnp.float32),
             pltpu.VMEM((3, rows + EDGE, lanes), jnp.float32),
             pltpu.VMEM((count, lanes), jnp.float32),
         ],
         compiler_params=pltpu.CompilerParams(vmem_limit_bytes=8 << 20),
         name="mixer",
-    )(picks, feature, before, after, grad, taps, filters)
+    )(picks, feature, within, across, grad, taps, filters)
 
 
 def gathered_features(tokens, proj, lanes):
@@ -308,19 +388,19 @@
     keep = lax.dynamic_slice_in_dim(partial, half * lanes, lanes, 2)
     give = lax.dynamic_slice_in_dim(partial, (1 - half) * lanes, lanes, 2)
     chip = keep + crossed(give, "grp", 1)
-    return chip[:, :count] + crossed(chip[:, count:], "rep", 1)
+    return chip[:, :count], crossed(chip[:, count:], "rep", 1)
 
 
 def cube_features(tokens, alternates, proj, early):
     width = proj.shape[2] // lax.axis_size("rep")
     bar = lax.optimization_barrier
 
-    own, own_a, own_b, theirs = prepare(proj, tokens, alternates, width)
+    own, own_a, own_b = panels(proj, width)
     own_4a = crossed(own_a, "seq", 4)
     own_4b = crossed(own_b, "seq", 4)
     own_2 = crossed(own, "seq", 2)
     own_1 = crossed(own, "seq", 1)
-    theirs = crossed(theirs, "rep", 1)
+    theirs = crossed(columns(tokens, alternates, width), "rep", 1)
     own_2, own_1, own_4a = bar((own_2, own_1, own_4a))
     own_3 = crossed(own_2, "seq", 1)
     own_4a, own_4b, own_3, early = bar((own_4a, own_4b, own_3, early))
@@ -336,45 +416,20 @@
     far = own_4a, own_4b, own_5a, own_5b, own_6a, own_6b, own_7a, own_7b
     give_other, keep_other, give_mine, keep_mine = products(tokens, alternates, theirs, near + far)
     other = crossed(keep_other + crossed(give_other, "grp", 1), "rep", 1)
-    return keep_mine + crossed(give_mine, "grp", 1) + other, early
+    return (keep_mine, crossed(give_mine, "grp", 1), other), early
 
 
 def per_device(hidden, proj, short_taps, filters, grad_out, var_pos, alt_hidden):
-    rows = hidden.shape[0]
     lanes = grad_out.shape[1]
-    reach = filters.shape[1] + EDGE
     early = spread(filters), short_taps, var_pos
     if lax.axis_size("seq") == 8:
-        feature, early = cube_features(hidden, alt_hidden, proj, early)
+        terms, early = cube_features(hidden, alt_hidden, proj, early)
     else:
-        feature = gathered_features((hidden, alt_hidden), proj, lanes)
+        terms = gathered_features((hidden, alt_hidden), proj, lanes)
     per_channel, short_taps, picks = early
-    before = shifted(
-        jnp.concatenate(
-            [
-                feature[1, rows - reach : rows],
-                feature[2, rows - reach : rows],
-                feature[0, rows - EDGE : rows],
-            ],
-            0,
-        ),
-        "seq",
-        1,
-    )
-    after = shifted(
-        jnp.concatenate(
-            [
-                feature[0, :reach],
-                feature[1, :EDGE],
-                feature[2, :EDGE],
-                grad_out[:reach].astype(jnp.float32),
-            ],
-            0,
-        ), "seq", -1
-    )
-    scores = mixer(
-        picks, feature, before, after, grad_out, short_taps, per_channel
-    )
+    feature, within, across = edges(grad_out, short_taps, filters.shape[1], terms)
+    within, across = paired(within, "seq", 0), paired(across, "seq", 1)
+    scores = mixer(picks, feature, within, across, grad_out, short_taps, per_channel)
     return tuple(lax.psum(tuple(scores), "grp"))
 
 

time: 86.7 us -> 80.5 us (0.928)
  waiting for transfers between devices: 49.2 us -> 42.6 us
  local copies, waits for them, and re-layouts: 1.05 us -> 3.69 us
  Pallas kernels: 11.4 us -> 8.82 us
  blocking collectives: 3.36 us -> 5.48 us
  starting transfers between devices: 20.2 us -> 18.9 us
    ppermute x15, waiting for transfers between devices: 43.9 us -> 38.4 us  [crossed(): lax.ppermute(block, axis, [(i, i ^ bit) for i in range(lax.axis_size(axis...]
    ppermute x2, starting transfers between devices: 6.18 us -> 3.19 us  [paired(): return lax.ppermute(block, axis, route)]
    unnamed x14 -> x18, local copies, waits for them, and re-layouts: 1.03 us -> 3.69 us
    pallas_call x1 -> x3, Pallas kernels: 2.9 us -> 0.41 us  [the longest x1 0.14 us: edges(): pl.pallas_call(functools.partial(edges_kernel, span, rows), out_shape=[ja...]
    psum x1, blocking collectives: 3.36 us -> 5.48 us  [per_device(): return tuple(lax.psum(tuple(scores), 'grp'))]
    ppermute x15, starting transfers between devices: 14 us -> 15.7 us  [crossed(): lax.ppermute(block, axis, [(i, i ^ bit) for i in range(lax.axis_size(axis...]
    ppermute x2, waiting for transfers between devices: 5.28 us -> 4.2 us  [paired(): return lax.ppermute(block, axis, route)]
  transfers between devices with their start and end apart: 17 -> 17, of which waited for: 11 -> 12; matrix products, arithmetic and copies ran while one was open for 0% -> 0% of each run, Pallas kernels for 2% -> 2%
where the time goes in v4:
time: 80.5 us; the launch traced here: 80.3 us
  waiting for transfers between devices  42.6 us (53%)
  starting transfers between devices  18.9 us (23%)
  Pallas kernels  8.82 us (11%)
  blocking collectives  5.48 us (7%)
  local copies, waits for them, and re-layouts  3.69 us (5%)
    ppermute x15, waiting for transfers between devices, crossed(): lax.ppermute(block, axis, [(i, i ^ bit) for i in range(lax.axis_size(axis...  38.4 us
    ppermute x15, starting transfers between devices, crossed(): lax.ppermute(block, axis, [(i, i ^ bit) for i in range(lax.axis_size(axis...  15.7 us
    psum x1, blocking collectives, per_device(): return tuple(lax.psum(tuple(scores), 'grp'))  5.48 us
    pallas_call x1, Pallas kernels, mixer(): pl.pallas_call(body, out_shape=[jax.ShapeDtypeStruct((rows,), jnp.float32...  4.97 us
    ppermute x2, waiting for transfers between devices, paired(): return lax.ppermute(block, axis, route)  4.2 us
    unnamed x18, local copies, waits for them, and re-layouts  3.69 us
    ppermute x2, starting transfers between devices, paired(): return lax.ppermute(block, axis, route)  3.19 us
  transfers between devices with their start and end apart: 17, of which 12 were waited for; matrix products, arithmetic and copies ran while one was open for 0% of the time, Pallas kernels for 2%

profile of v4, /device:TPU:23, one launch (start us, length us, event | category | flops | bytes accessed | tf_op | source)
XLA Modules:
  0.0 80.3 jit_solution(15810225969098058601)
XLA Ops:
  0.6 0.0 copy-start.2
  0.6 1.1 %copy-done.2 = bf16[3,32,4096]{2,1,0:T(8,128)(2,1)S(1)} copy-done((bf16[3,32,4096]{2,1,0:T(8,128)(2,1)S(1)}, bf16[3,32,4096]{2,1,0:T(8,128)(2,1)}, u32[]{:S(2)}) %copy-start.2) | copy-done | bytes 786456
  1.8 0.0 copy-start.7
  1.8 0.1 panels.1
  1.9 0.3 collective-permute-start.1
  2.2 1.3 %collective-permute-start = (bf16[3,32,2048]{2,1,0:T(8,128)(2,1)S(1)}, bf16[3,32,2048]{2,1,0:T(8,128)(2,1)S(1)}, u32[]{:S(2)}, u32[]{:S(2)}) collective-permute-start(bf16[3,32,2048]{2,1,0:T(8,128)(2,1)S(1)} %get-tuple-element.28.refs_0_), channel_id=1, source_target_pairs={{0,4},{2,6},{4,0},{6,2},{8,12},{10,14},{12,8},{14,10},{1,5},{3,7},... | collective-permute-start | bytes 1179656 | tf_op jit(solution)/shard_map/ppermute | solution.py:29
  3.5 0.0 copy-start
  3.5 1.6 %copy-done = bf16[272,4096]{1,0:T(8,128)(2,1)S(1)} copy-done((bf16[272,4096]{1,0:T(8,128)(2,1)S(1)}, bf16[272,4096]{1,0:T(8,128)(2,1)}, u32[]{:S(2)}) %copy-start) | copy-done | bytes 2228248
  5.2 0.0 copy-start.3
  5.2 0.9 %copy-done.3 = bf16[16,4096]{1,0:T(8,128)(2,1)S(1)} copy-done((bf16[16,4096]{1,0:T(8,128)(2,1)S(1)}, bf16[16,4096]{1,0:T(8,128)(2,1)}, u32[]{:S(2)}) %copy-start.3) | copy-done | bytes 131096
  6.1 0.1 columns.1
  6.2 0.0 copy-start.1
  6.2 0.0 copy-start.4
  6.2 0.3 collective-permute-start.5
  6.5 0.1 collective-permute-start.2
  6.6 9.5 %collective-permute-done.2.refs_4_ = bf16[3,16,2048]{2,1,0:T(8,128)(2,1)S(1)} collective-permute-done((bf16[3,16,2048]{2,1,0:T(8,128)(2,1)S(1)}, bf16[3,16,2048]{2,1,0:T(8,128)(2,1)S(1)}, u32[]{:S(2)}, u32[]{:S(2)}) %collective-permute-start.2) | collective-permute-done | bytes 196640 | tf_op jit(solution)/shard_map/ppermute | solution.py:29
  16.0 0.0 collective-permute-done.1.refs_1_
  16.0 0.0 collective-permute-done.refs_2_
  16.0 1.2 %collective-permute-start.4 = (bf16[3,32,2048]{2,1,0:T(8,128)(2,1)S(1)}, bf16[3,32,2048]{2,1,0:T(8,128)(2,1)S(1)}, u32[]{:S(2)}, u32[]{:S(2)}) collective-permute-start(bf16[3,32,2048]{2,1,0:T(8,128)(2,1)S(1)} %collective-permute-done.refs_2_), channel_id=1, source_target_pairs={{0,2},{2,0},{4,6},{6,4},{8,10},{10,8},{12,14},{14,12},{1,3},{3,1},... | collective-permute-start | bytes 1179656 | tf_op jit(solution)/shard_map/ppermute | solution.py:29
  17.3 0.1 collective-permute-start.3
  17.4 0.0 copy-done.7
  17.4 0.3 spread.1.refs_6_
  17.6 5.1 %collective-permute-done.3.refs_5_ = bf16[3,16,2048]{2,1,0:T(8,128)(2,1)S(1)} collective-permute-done((bf16[3,16,2048]{2,1,0:T(8,128)(2,1)S(1)}, bf16[3,16,2048]{2,1,0:T(8,128)(2,1)S(1)}, u32[]{:S(2)}, u32[]{:S(2)}) %collective-permute-start.3) | collective-permute-done | bytes 196640 | tf_op jit(solution)/shard_map/ppermute | solution.py:29
  22.8 2.0 %collective-permute-done.4.refs_3_ = bf16[3,32,2048]{2,1,0:T(8,128)(2,1)S(1)} collective-permute-done((bf16[3,32,2048]{2,1,0:T(8,128)(2,1)S(1)}, bf16[3,32,2048]{2,1,0:T(8,128)(2,1)S(1)}, u32[]{:S(2)}, u32[]{:S(2)}) %collective-permute-start.4) | collective-permute-done | bytes 393248 | tf_op jit(solution)/shard_map/ppermute | solution.py:29
  24.7 1.2 %collective-permute-start.8 = (bf16[3,16,2048]{2,1,0:T(8,128)(2,1)S(1)}, bf16[3,16,2048]{2,1,0:T(8,128)(2,1)S(1)}, u32[]{:S(2)}, u32[]{:S(2)}) collective-permute-start(bf16[3,16,2048]{2,1,0:T(8,128)(2,1)S(1)} %collective-permute-done.2.refs_4_), channel_id=1, source_target_pairs={{0,2},{2,0},{4,6},{6,4},{8,10},{10,8},{12,14},{14,12},{1,3},{3,1},... | collective-permute-start | bytes 589832 | tf_op jit(solution)/shard_map/ppermute | solution.py:29
  26.0 4.1 %collective-permute-start.6 = (bf16[3,16,2048]{2,1,0:T(8,128)(2,1)S(1)}, bf16[3,16,2048]{2,1,0:T(8,128)(2,1)S(1)}, u32[]{:S(2)}, u32[]{:S(2)}) collective-permute-start(bf16[3,16,2048]{2,1,0:T(8,128)(2,1)S(1)} %collective-permute-done.2.refs_4_), channel_id=1, source_target_pairs={{0,4},{2,6},{4,0},{6,2},{8,12},{10,14},{12,8},{14,10},{1,5},{3,7},... | collective-permute-start | bytes 589832 | tf_op jit(solution)/shard_map/ppermute | solution.py:29
  30.0 1.2 %collective-permute-start.9 = (bf16[3,16,2048]{2,1,0:T(8,128)(2,1)S(1)}, bf16[3,16,2048]{2,1,0:T(8,128)(2,1)S(1)}, u32[]{:S(2)}, u32[]{:S(2)}) collective-permute-start(bf16[3,16,2048]{2,1,0:T(8,128)(2,1)S(1)} %collective-permute-done.3.refs_5_), channel_id=1, source_target_pairs={{0,2},{2,0},{4,6},{6,4},{8,10},{10,8},{12,14},{14,12},{1,3},{3,1},... | collective-permute-start | bytes 589832 | tf_op jit(solution)/shard_map/ppermute | solution.py:29
  31.2 0.0 collective-permute-start.7
  31.2 0.0 collective-permute-done.8.refs_6_
  31.2 2.6 %collective-permute-done.6.refs_8_ = bf16[3,16,2048]{2,1,0:T(8,128)(2,1)S(1)} collective-permute-done((bf16[3,16,2048]{2,1,0:T(8,128)(2,1)S(1)}, bf16[3,16,2048]{2,1,0:T(8,128)(2,1)S(1)}, u32[]{:S(2)}, u32[]{:S(2)}) %collective-permute-start.6) | collective-permute-done | bytes 196640 | tf_op jit(solution)/shard_map/ppermute | solution.py:29
  33.8 1.2 %collective-permute-done.9.refs_7_ = bf16[3,16,2048]{2,1,0:T(8,128)(2,1)S(1)} collective-permute-done((bf16[3,16,2048]{2,1,0:T(8,128)(2,1)S(1)}, bf16[3,16,2048]{2,1,0:T(8,128)(2,1)S(1)}, u32[]{:S(2)}, u32[]{:S(2)}) %collective-permute-start.9) | collective-permute-done | bytes 196640 | tf_op jit(solution)/shard_map/ppermute | solution.py:29
  35.0 3.2 %collective-permute-done.7.refs_9_ = bf16[3,16,2048]{2,1,0:T(8,128)(2,1)S(1)} collective-permute-done((bf16[3,16,2048]{2,1,0:T(8,128)(2,1)S(1)}, bf16[3,16,2048]{2,1,0:T(8,128)(2,1)S(1)}, u32[]{:S(2)}, u32[]{:S(2)}) %collective-permute-start.7) | collective-permute-done | bytes 196640 | tf_op jit(solution)/shard_map/ppermute | solution.py:29
  38.2 1.1 %collective-permute-start.11 = (bf16[3,16,2048]{2,1,0:T(8,128)(2,1)S(1)}, bf16[3,16,2048]{2,1,0:T(8,128)(2,1)S(1)}, u32[]{:S(2)}, u32[]{:S(2)}) collective-permute-start(bf16[3,16,2048]{2,1,0:T(8,128)(2,1)S(1)} %collective-permute-done.9.refs_7_), channel_id=1, source_target_pairs={{0,4},{2,6},{4,0},{6,2},{8,12},{10,14},{12,8},{14,10},{1,5},{3,7},... | collective-permute-start | bytes 589832 | tf_op jit(solution)/shard_map/ppermute | solution.py:29
  39.3 1.2 %collective-permute-start.10 = (bf16[3,16,2048]{2,1,0:T(8,128)(2,1)S(1)}, bf16[3,16,2048]{2,1,0:T(8,128)(2,1)S(1)}, u32[]{:S(2)}, u32[]{:S(2)}) collective-permute-start(bf16[3,16,2048]{2,1,0:T(8,128)(2,1)S(1)} %collective-permute-done.6.refs_8_), channel_id=1, source_target_pairs={{0,2},{2,0},{4,6},{6,4},{8,10},{10,8},{12,14},{14,12},{1,3},{3,1},... | collective-permute-start | bytes 589832 | tf_op jit(solution)/shard_map/ppermute | solution.py:29
  40.4 2.2 %collective-permute-done.11.refs_11_ = bf16[3,16,2048]{2,1,0:T(8,128)(2,1)S(1)} collective-permute-done((bf16[3,16,2048]{2,1,0:T(8,128)(2,1)S(1)}, bf16[3,16,2048]{2,1,0:T(8,128)(2,1)S(1)}, u32[]{:S(2)}, u32[]{:S(2)}) %collective-permute-start.11) | collective-permute-done | bytes 196640 | tf_op jit(solution)/shard_map/ppermute | solution.py:29
  42.7 1.4 %collective-permute-done.10.refs_10_ = bf16[3,16,2048]{2,1,0:T(8,128)(2,1)S(1)} collective-permute-done((bf16[3,16,2048]{2,1,0:T(8,128)(2,1)S(1)}, bf16[3,16,2048]{2,1,0:T(8,128)(2,1)S(1)}, u32[]{:S(2)}, u32[]{:S(2)}) %collective-permute-start.10) | collective-permute-done | bytes 196640 | tf_op jit(solution)/shard_map/ppermute | solution.py:29
  44.1 0.0 collective-permute-done.5.theirs
  44.1 1.6 %theirs.1 = (f32[3,288,128]{2,1,0:T(8,128)S(1)}, f32[3,288,128]{2,1,0:T(8,128)S(1)}, bf16[768,2048]{1,0:T(8,128)(2,1)S(1)}) custom-call(bf16[288,2048]{1,0:T(8,128)(2,1)S(1)} %collective-permute-done.5.theirs, bf16[3,32,2048]{2,1,0:T(8,128)(2,1)S(1)} %get-tuple-element.28.refs_0_, bf16[3,32,2048]{2,1,0:T(8,128)(2,1)S(1)} %collective-permute-done.1.refs_1_, ...), custom_call_target="tpu_custom_call" | custom-call | flops 905969664 | bytes 5210112 | tf_op jit(solution)/shard_map/theirs/pallas_call | solution.py:159
  45.7 3.5 %collective-permute-start.13 = (f32[3,288,128]{2,1,0:T(8,128)S(1)}, f32[3,288,128]{2,1,0:T(8,128)S(1)}, u32[]{:S(2)}, u32[]{:S(2)}) collective-permute-start(f32[3,288,128]{2,1,0:T(8,128)S(1)} %get-tuple-element.47), channel_id=1, source_target_pairs={{0,1},{1,0},{2,3},{3,2},{4,5},{5,4},{6,7},{7,6},{8,9},{9,8},{10,11... | collective-permute-start | bytes 1327112 | tf_op jit(solution)/shard_map/ppermute | solution.py:29
  49.2 0.0 copy-done.1
  49.2 0.0 copy-done.4
  49.2 0.0 copy-start.5
  49.2 0.0 copy-start.6
  49.2 1.6 %ours.1 = (f32[3,288,128]{2,1,0:T(8,128)S(1)}, f32[3,288,128]{2,1,0:T(8,128)S(1)}) custom-call(bf16[272,4096]{1,0:T(8,128)(2,1)S(1)} %copy-done.1, bf16[16,4096]{1,0:T(8,128)(2,1)S(1)} %copy-done.4, bf16[768,2048]{1,0:T(8,128)(2,1)S(1)} %get-tuple-element.43.panel), custom_call_target="tpu_custom_call" | custom-call | flops 905969664 | bytes 5210112 | tf_op jit(solution)/shard_map/ours/pallas_call | solution.py:168
  50.8 0.0 copy-start.8
  50.8 0.1 collective-permute-start.12
  50.9 0.0 collective-permute-done.13
  50.9 0.1 add.7
  51.0 0.1 collective-permute-start.14
  51.0 1.6 %collective-permute-done.12.refs_1_ = f32[3,288,128]{2,1,0:T(8,128)S(1)} collective-permute-done((f32[3,288,128]{2,1,0:T(8,128)S(1)}, f32[3,288,128]{2,1,0:T(8,128)S(1)}, u32[]{:S(2)}, u32[]{:S(2)}) %collective-permute-start.12) | collective-permute-done | bytes 442400 | tf_op jit(solution)/shard_map/ppermute | solution.py:29
  52.6 9.6 %collective-permute-done.14.refs_2_ = f32[3,288,128]{2,1,0:T(8,128)S(1)} collective-permute-done((f32[3,288,128]{2,1,0:T(8,128)S(1)}, f32[3,288,128]{2,1,0:T(8,128)S(1)}, u32[]{:S(2)}, u32[]{:S(2)}) %collective-permute-start.14) | collective-permute-done | bytes 442400 | tf_op jit(solution)/shard_map/ppermute | solution.py:29
  62.3 0.0 copy-done.5
  62.3 0.0 copy-done.6
  62.3 0.1 edges.1
  62.4 1.3 %collective-permute-start.15 = (f32[168,128]{1,0:T(8,128)S(1)}, f32[168,128]{1,0:T(8,128)S(1)}, u32[]{:S(2)}, u32[]{:S(2)}) collective-permute-start(f32[168,128]{1,0:T(8,128)S(1)} %get-tuple-element.49), channel_id=1, source_target_pairs={{0,2},{2,0},{4,6},{6,4},{8,10},{10,8},{12,14},{14,12},{1,3},{3,1},... | collective-permute-start | bytes 258056 | tf_op jit(solution)/shard_map/ppermute | solution.py:25
  63.7 1.9 %collective-permute-start.16 = (f32[168,128]{1,0:T(8,128)S(1)}, f32[168,128]{1,0:T(8,128)S(1)}, u32[]{:S(2)}, u32[]{:S(2)}) collective-permute-start(f32[168,128]{1,0:T(8,128)S(1)} %get-tuple-element.50), channel_id=1, source_target_pairs={{2,4},{4,2},{6,8},{8,6},{10,12},{12,10},{3,5},{5,3},{7,9},{9,7},{1... | collective-permute-start | bytes 258056 | tf_op jit(solution)/shard_map/ppermute | solution.py:25
  65.6 0.2 collective-permute-done.15.refs_2_
  65.9 4.0 %collective-permute-done.16.refs_3_ = f32[168,128]{1,0:T(8,128)S(1)} collective-permute-done((f32[168,128]{1,0:T(8,128)S(1)}, f32[168,128]{1,0:T(8,128)S(1)}, u32[]{:S(2)}, u32[]{:S(2)}) %collective-permute-start.16) | collective-permute-done | bytes 86048 | tf_op jit(solution)/shard_map/ppermute | solution.py:25
  69.8 0.0 copy-done.8
  69.9 5.0 %mixer.1 = (f32[272]{0:T(512)S(1)}, f32[16]{0:T(128)S(1)}) custom-call(s32[16]{0:T(128)S(1)} %copy-done.8, f32[3,288,128]{2,1,0:T(8,128)S(1)} %get-tuple-element.48.refs_1_, f32[168,128]{1,0:T(8,128)S(1)} %collective-permute-done.15.refs_2_, f32[168,128]{1,0:T(8,128)S(1)} %collective-permute-done.16.refs_3_, bf16[272,128]{1,0:T(8,128)(2,1)S(1)} %copy-done.5, ...), custom_call_target="tpu_custom_call" | custom-call | tf_op jit(solution)/shard_map/mixer/pallas_call | solution.py:350
  74.8 5.5 %all-reduce = (f32[272]{0:T(512)}, f32[16]{0:T(128)}) all-reduce(f32[272]{0:T(512)S(1)} %get-tuple-element.52, f32[16]{0:T(128)S(1)} %get-tuple-element.53), channel_id=1, replica_groups=mesh['rep'=2,'seq'=8,'grp'=2] {'grp'}, use_global_device_ids=true, to_apply=%region_0.0 | all-reduce | flops 288 | bytes 2304 | tf_op jit(solution)/shard_map/psum | solution.py:433
Async XLA Ops:
  0.6 1.1 %copy-start.2 = (bf16[3,32,4096]{2,1,0:T(8,128)(2,1)S(1)}, bf16[3,32,4096]{2,1,0:T(8,128)(2,1)}, u32[]{:S(2)}) copy-start(bf16[3,32,4096]{2,1,0:T(8,128)(2,1)} %proj.1) | copy-start | bytes 2359300
  1.8 15.6 %copy-start.7 = (f32[8,128]{1,0:T(8,128)S(1)}, f32[8,128]{1,0:T(8,128)}, u32[]{:S(2)}) copy-start(f32[8,128]{1,0:T(8,128)} %filters.1) | copy-start | bytes 12292
  1.9 14.1 %collective-permute-start.1 = (bf16[3,32,2048]{2,1,0:T(8,128)(2,1)S(1)}, bf16[3,32,2048]{2,1,0:T(8,128)(2,1)S(1)}, u32[]{:S(2)}, u32[]{:S(2)}) collective-permute-start(bf16[3,32,2048]{2,1,0:T(8,128)(2,1)S(1)} %get-tuple-element.28.refs_0_), channel_id=1, source_target_pairs={{0,2},{2,0},{4,6},{6,4},{8,10},{10,8},{12,14},{14,12},{1,3},{3,1},... | collective-permute-start | bytes 1179656 | tf_op jit(solution)/shard_map/ppermute | solution.py:29
  2.2 13.8 %collective-permute-start = (bf16[3,32,2048]{2,1,0:T(8,128)(2,1)S(1)}, bf16[3,32,2048]{2,1,0:T(8,128)(2,1)S(1)}, u32[]{:S(2)}, u32[]{:S(2)}) collective-permute-start(bf16[3,32,2048]{2,1,0:T(8,128)(2,1)S(1)} %get-tuple-element.28.refs_0_), channel_id=1, source_target_pairs={{0,4},{2,6},{4,0},{6,2},{8,12},{10,14},{12,8},{14,10},{1,5},{3,7},... | collective-permute-start | bytes 1179656 | tf_op jit(solution)/shard_map/ppermute | solution.py:29
  3.5 1.6 %copy-start = (bf16[272,4096]{1,0:T(8,128)(2,1)S(1)}, bf16[272,4096]{1,0:T(8,128)(2,1)}, u32[]{:S(2)}) copy-start(bf16[272,4096]{1,0:T(8,128)(2,1)} %tokens.3) | copy-start | bytes 6684676
  5.2 0.9 %copy-start.3 = (bf16[16,4096]{1,0:T(8,128)(2,1)S(1)}, bf16[16,4096]{1,0:T(8,128)(2,1)}, u32[]{:S(2)}) copy-start(bf16[16,4096]{1,0:T(8,128)(2,1)} %alternates.3) | copy-start | bytes 393220
  6.2 43.0 %copy-start.1 = (bf16[272,4096]{1,0:T(8,128)(2,1)S(1)}, bf16[272,4096]{1,0:T(8,128)(2,1)}, u32[]{:S(2)}) copy-start(bf16[272,4096]{1,0:T(8,128)(2,1)} %tokens.3) | copy-start | bytes 6684676
  6.2 43.0 %copy-start.4 = (bf16[16,4096]{1,0:T(8,128)(2,1)S(1)}, bf16[16,4096]{1,0:T(8,128)(2,1)}, u32[]{:S(2)}) copy-start(bf16[16,4096]{1,0:T(8,128)(2,1)} %alternates.3) | copy-start | bytes 393220
  6.2 37.9 %collective-permute-start.5 = (bf16[288,2048]{1,0:T(8,128)(2,1)S(1)}, bf16[288,2048]{1,0:T(8,128)(2,1)S(1)}, u32[]{:S(2)}, u32[]{:S(2)}) collective-permute-start(bf16[288,2048]{1,0:T(8,128)(2,1)S(1)} %columns.1), channel_id=1, source_target_pairs={{0,16},{16,0},{1,17},{17,1},{2,18},{18,2},{3,19},{19,3},{4,20},{20... | collective-permute-start | bytes 3538952 | tf_op jit(solution)/shard_map/ppermute | solution.py:29
  6.5 9.5 %collective-permute-start.2 = (bf16[3,16,2048]{2,1,0:T(8,128)(2,1)S(1)}, bf16[3,16,2048]{2,1,0:T(8,128)(2,1)S(1)}, u32[]{:S(2)}, u32[]{:S(2)}) collective-permute-start(bf16[3,16,2048]{2,1,0:T(8,128)(2,1)S(1)} %get-tuple-element.29), channel_id=1, source_target_pairs={{0,8},{2,10},{4,12},{6,14},{8,0},{10,2},{12,4},{14,6},{1,9},{3,11}... | collective-permute-start | bytes 589832 | tf_op jit(solution)/shard_map/ppermute | solution.py:29
  16.0 8.7 %collective-permute-start.4 = (bf16[3,32,2048]{2,1,0:T(8,128)(2,1)S(1)}, bf16[3,32,2048]{2,1,0:T(8,128)(2,1)S(1)}, u32[]{:S(2)}, u32[]{:S(2)}) collective-permute-start(bf16[3,32,2048]{2,1,0:T(8,128)(2,1)S(1)} %collective-permute-done.refs_2_), channel_id=1, source_target_pairs={{0,2},{2,0},{4,6},{6,4},{8,10},{10,8},{12,14},{14,12},{1,3},{3,1},... | collective-permute-start | bytes 1179656 | tf_op jit(solution)/shard_map/ppermute | solution.py:29
  17.3 5.5 %collective-permute-start.3 = (bf16[3,16,2048]{2,1,0:T(8,128)(2,1)S(1)}, bf16[3,16,2048]{2,1,0:T(8,128)(2,1)S(1)}, u32[]{:S(2)}, u32[]{:S(2)}) collective-permute-start(bf16[3,16,2048]{2,1,0:T(8,128)(2,1)S(1)} %get-tuple-element.31), channel_id=1, source_target_pairs={{0,8},{2,10},{4,12},{6,14},{8,0},{10,2},{12,4},{14,6},{1,9},{3,11}... | collective-permute-start | bytes 589832 | tf_op jit(solution)/shard_map/ppermute | solution.py:29
  24.7 6.5 %collective-permute-start.8 = (bf16[3,16,2048]{2,1,0:T(8,128)(2,1)S(1)}, bf16[3,16,2048]{2,1,0:T(8,128)(2,1)S(1)}, u32[]{:S(2)}, u32[]{:S(2)}) collective-permute-start(bf16[3,16,2048]{2,1,0:T(8,128)(2,1)S(1)} %collective-permute-done.2.refs_4_), channel_id=1, source_target_pairs={{0,2},{2,0},{4,6},{6,4},{8,10},{10,8},{12,14},{14,12},{1,3},{3,1},... | collective-permute-start | bytes 589832 | tf_op jit(solution)/shard_map/ppermute | solution.py:29
  26.0 7.9 %collective-permute-start.6 = (bf16[3,16,2048]{2,1,0:T(8,128)(2,1)S(1)}, bf16[3,16,2048]{2,1,0:T(8,128)(2,1)S(1)}, u32[]{:S(2)}, u32[]{:S(2)}) collective-permute-start(bf16[3,16,2048]{2,1,0:T(8,128)(2,1)S(1)} %collective-permute-done.2.refs_4_), channel_id=1, source_target_pairs={{0,4},{2,6},{4,0},{6,2},{8,12},{10,14},{12,8},{14,10},{1,5},{3,7},... | collective-permute-start | bytes 589832 | tf_op jit(solution)/shard_map/ppermute | solution.py:29
  30.0 5.0 %collective-permute-start.9 = (bf16[3,16,2048]{2,1,0:T(8,128)(2,1)S(1)}, bf16[3,16,2048]{2,1,0:T(8,128)(2,1)S(1)}, u32[]{:S(2)}, u32[]{:S(2)}) collective-permute-start(bf16[3,16,2048]{2,1,0:T(8,128)(2,1)S(1)} %collective-permute-done.3.refs_5_), channel_id=1, source_target_pairs={{0,2},{2,0},{4,6},{6,4},{8,10},{10,8},{12,14},{14,12},{1,3},{3,1},... | collective-permute-start | bytes 589832 | tf_op jit(solution)/shard_map/ppermute | solution.py:29
  31.2 6.9 %collective-permute-start.7 = (bf16[3,16,2048]{2,1,0:T(8,128)(2,1)S(1)}, bf16[3,16,2048]{2,1,0:T(8,128)(2,1)S(1)}, u32[]{:S(2)}, u32[]{:S(2)}) collective-permute-start(bf16[3,16,2048]{2,1,0:T(8,128)(2,1)S(1)} %collective-permute-done.3.refs_5_), channel_id=1, source_target_pairs={{0,4},{2,6},{4,0},{6,2},{8,12},{10,14},{12,8},{14,10},{1,5},{3,7},... | collective-permute-start | bytes 589832 | tf_op jit(solution)/shard_map/ppermute | solution.py:29
  38.2 4.5 %collective-permute-start.11 = (bf16[3,16,2048]{2,1,0:T(8,128)(2,1)S(1)}, bf16[3,16,2048]{2,1,0:T(8,128)(2,1)S(1)}, u32[]{:S(2)}, u32[]{:S(2)}) collective-permute-start(bf16[3,16,2048]{2,1,0:T(8,128)(2,1)S(1)} %collective-permute-done.9.refs_7_), channel_id=1, source_target_pairs={{0,4},{2,6},{4,0},{6,2},{8,12},{10,14},{12,8},{14,10},{1,5},{3,7},... | collective-permute-start | bytes 589832 | tf_op jit(solution)/shard_map/ppermute | solution.py:29
  39.3 4.8 %collective-permute-start.10 = (bf16[3,16,2048]{2,1,0:T(8,128)(2,1)S(1)}, bf16[3,16,2048]{2,1,0:T(8,128)(2,1)S(1)}, u32[]{:S(2)}, u32[]{:S(2)}) collective-permute-start(bf16[3,16,2048]{2,1,0:T(8,128)(2,1)S(1)} %collective-permute-done.6.refs_8_), channel_id=1, source_target_pairs={{0,2},{2,0},{4,6},{6,4},{8,10},{10,8},{12,14},{14,12},{1,3},{3,1},... | collective-permute-start | bytes 589832 | tf_op jit(solution)/shard_map/ppermute | solution.py:29
  45.7 5.2 %collective-permute-start.13 = (f32[3,288,128]{2,1,0:T(8,128)S(1)}, f32[3,288,128]{2,1,0:T(8,128)S(1)}, u32[]{:S(2)}, u32[]{:S(2)}) collective-permute-start(f32[3,288,128]{2,1,0:T(8,128)S(1)} %get-tuple-element.47), channel_id=1, source_target_pairs={{0,1},{1,0},{2,3},{3,2},{4,5},{5,4},{6,7},{7,6},{8,9},{9,8},{10,11... | collective-permute-start | bytes 1327112 | tf_op jit(solution)/shard_map/ppermute | solution.py:29
  49.2 13.1 %copy-start.5 = (bf16[272,128]{1,0:T(8,128)(2,1)S(1)}, bf16[272,128]{1,0:T(8,128)(2,1)}, u32[]{:S(2)}) copy-start(bf16[272,128]{1,0:T(8,128)(2,1)} %refs_4_.1) | copy-start | bytes 208900
  49.2 13.1 %copy-start.6 = (f32[3,3,128]{2,1,0:T(4,128)S(1)}, f32[3,3,128]{2,1,0:T(4,128)}, u32[]{:S(2)}) copy-start(f32[3,3,128]{2,1,0:T(4,128)} %refs_5_) | copy-start | bytes 13828
  50.8 19.1 %copy-start.8 = (s32[16]{0:T(128)S(1)}, s32[16]{0:T(128)}, u32[]{:S(2)}) copy-start(s32[16]{0:T(128)} %refs_0_) | copy-start | bytes 196
  50.8 1.9 %collective-permute-start.12 = (f32[3,288,128]{2,1,0:T(8,128)S(1)}, f32[3,288,128]{2,1,0:T(8,128)S(1)}, u32[]{:S(2)}, u32[]{:S(2)}) collective-permute-start(f32[3,288,128]{2,1,0:T(8,128)S(1)} %get-tuple-element.45), channel_id=1, source_target_pairs={{0,1},{1,0},{2,3},{3,2},{4,5},{5,4},{6,7},{7,6},{8,9},{9,8},{10,11... | collective-permute-start | bytes 1327112 | tf_op jit(solution)/shard_map/ppermute | solution.py:29
  51.0 11.3 %collective-permute-start.14 = (f32[3,288,128]{2,1,0:T(8,128)S(1)}, f32[3,288,128]{2,1,0:T(8,128)S(1)}, u32[]{:S(2)}, u32[]{:S(2)}) collective-permute-start(f32[3,288,128]{2,1,0:T(8,128)S(1)} %add.7), channel_id=1, source_target_pairs={{0,16},{16,0},{1,17},{17,1},{2,18},{18,2},{3,19},{19,3},{4,20},{20... | collective-permute-start | bytes 1327112 | tf_op jit(solution)/shard_map/ppermute | solution.py:29
  62.4 3.4 %collective-permute-start.15 = (f32[168,128]{1,0:T(8,128)S(1)}, f32[168,128]{1,0:T(8,128)S(1)}, u32[]{:S(2)}, u32[]{:S(2)}) collective-permute-start(f32[168,128]{1,0:T(8,128)S(1)} %get-tuple-element.49), channel_id=1, source_target_pairs={{0,2},{2,0},{4,6},{6,4},{8,10},{10,8},{12,14},{14,12},{1,3},{3,1},... | collective-permute-start | bytes 258056 | tf_op jit(solution)/shard_map/ppermute | solution.py:25
  63.7 6.1 %collective-permute-start.16 = (f32[168,128]{1,0:T(8,128)S(1)}, f32[168,128]{1,0:T(8,128)S(1)}, u32[]{:S(2)}, u32[]{:S(2)}) collective-permute-start(f32[168,128]{1,0:T(8,128)S(1)} %get-tuple-element.50), channel_id=1, source_target_pairs={{2,4},{4,2},{6,8},{8,6},{10,12},{12,10},{3,5},{5,3},{7,9},{9,7},{1... | collective-permute-start | bytes 258056 | tf_op jit(solution)/shard_map/ppermute | solution.py:25

commit v5 on v4

--- a/solution.py
+++ b/solution.py
@@ -10,6 +10,7 @@
 D = 8192
 GROUP = 16
 EDGE = 8
+BAND = 96
 PIECES = 2
 AXES = ("rep", "seq", "grp")
 VMEM = pl.BlockSpec(memory_space=pltpu.VMEM)
@@ -103,7 +104,7 @@
 
 
 def dots(tokens, panel, give, keep):
-    kinds, _, lanes = give.shape
+    kinds, _, lanes = keep.shape
     size = kinds * lanes
     for begin, out in ((size, give), (0, keep)):
         result = lax.dot_general(
@@ -113,7 +114,8 @@
             preferred_element_type=jnp.float32,
         )
         for kind in range(kinds):
-            out[kind] = result[:, kind * lanes : (kind + 1) * lanes]
+            out_part = out[kind] if isinstance(out, tuple) else out.at[kind]
+            out_part[...] = result[:, kind * lanes : (kind + 1) * lanes]
 
 
 def theirs_kernel(theirs, *refs):
@@ -134,7 +136,7 @@
     dots(theirs, panel, give, keep)
 
 
-def ours_kernel(tokens, alternates, panel, give, keep, ours, sems):
+def ours_kernel(tokens, alternates, panel, give_query, give_key, give_value, keep, ours, sems):
     rows = tokens.shape[0]
     home = part(lax.axis_index("rep"), ours.shape[1])
     copies = moved(
@@ -142,7 +144,7 @@
     )
     for copy in copies:
         copy.wait()
-    dots(ours, panel, give, keep)
+    dots(ours, panel, (give_query, give_key, give_value), keep)
 
 
 def products(tokens, alternates, theirs, blocks):
@@ -165,11 +167,11 @@
         cost_estimate=cost,
         name="theirs",
     )(theirs, *blocks)
-    give_mine, keep_mine = pl.pallas_call(
+    *give_mine, keep_mine = pl.pallas_call(
         ours_kernel,
-        out_shape=[half, half],
+        out_shape=[jax.ShapeDtypeStruct((count, lanes), jnp.float32)] * kinds + [half],
         in_specs=[ANY, ANY, VMEM],
-        out_specs=[VMEM] * 2,
+        out_specs=[VMEM] * (kinds + 1),
         scratch_shapes=[pltpu.VMEM((count, width), theirs.dtype), pltpu.SemaphoreType.DMA((2,))],
         compiler_params=params,
         cost_estimate=cost,
@@ -178,28 +180,38 @@
     return give_other, keep_other, give_mine, keep_mine
 
 
-def spread_kernel(filters, out):
-    groups, lanes = filters.shape[0], out.shape[1]
-    row = lax.broadcasted_iota(jnp.int32, (groups, lanes), 0)
-    lane = lax.broadcasted_iota(jnp.int32, (groups, lanes), 1)
-    out[...] = lax.dot_general(
-        filters[...],
-        jnp.where(lane // GROUP == row, 1.0, 0.0),
-        (((0,), (0,)), ((), ())),
-        precision=lax.Precision.HIGHEST,
-        preferred_element_type=jnp.float32,
-    )
-
-
-def spread(filters):
+def bands_kernel(filters, *outs):
+    groups, span = filters.shape
+    deep = 2 * span
+    row = lax.broadcasted_iota(jnp.int32, (span, deep), 0)
+    column = lax.broadcasted_iota(jnp.int32, (span, deep), 1)
+    for later in (False, True):
+        place = jnp.where(column == (row if later else span - row), 1.0, 0.0)
+        taps = lax.dot_general(
+            filters[...],
+            place,
+            (((1,), (0,)), ((), ())),
+            precision=lax.Precision.HIGHEST,
+            preferred_element_type=jnp.float32,
+        )
+        for group in range(groups):
+            band = jnp.broadcast_to(taps[group : group + 1], (BAND, deep))
+            band = pltpu.roll(band, 0, 1, stride=1, stride_axis=0)
+            high = band.astype(jnp.bfloat16)
+            at = pl.ds(group * BAND, BAND)
+            outs[2 * later][at] = high
+            outs[2 * later + 1][at] = (band - high.astype(jnp.float32)).astype(jnp.bfloat16)
+
+
+def bands(filters):
     groups, span = filters.shape
     return pl.pallas_call(
-        spread_kernel,
-        out_shape=jax.ShapeDtypeStruct((span, groups * GROUP), jnp.float32),
+        bands_kernel,
+        out_shape=[jax.ShapeDtypeStruct((groups * BAND, 2 * span), jnp.bfloat16)] * 4,
         in_specs=[VMEM],
-        out_specs=VMEM,
-        compiler_params=pltpu.CompilerParams(vmem_limit_bytes=2 << 20),
-        name="spread",
+        out_specs=[VMEM] * 4,
+        compiler_params=pltpu.CompilerParams(vmem_limit_bytes=4 << 20),
+        name="bands",
     )(filters)
 
 
@@ -217,9 +229,9 @@
 def edges_kernel(span, rows, grad, taps, *refs):
     terms, (feature, within, across, before, after, head) = refs[:-6], refs[-6:]
     for kind in range(3):
-        total = terms[0][kind]
-        for term in terms[1:]:
-            total = total + term[kind]
+        total = terms[0][kind] + terms[1][kind]
+        if len(terms) > 2:
+            total = total + terms[2 + kind][...]
         feature[kind] = total
     begin = rows - span
     before[:span] = mixed(taps, 1, feature.at[1], begin, span) * mixed(
@@ -260,10 +272,11 @@
 
 
 def mixer_kernel(
-    rows, picks, feature, within, across, grad, taps, filters, out, effects,
-    before, after, query, key, value, product, back_filtered, shifts, grads, summed,
+    rows, span, picks, feature, within, across, grad, taps, high, low, later_high, later_low,
+    out, effects, before, after, query, key, value, product, back_filtered, filtered,
+    back_product, grads, summed,
 ):
-    span, lanes = filters.shape
+    lanes = grad.shape[1]
     variants = picks.shape[0]
     first = lax.axis_index("seq") * rows
     ahead = rows + EDGE
@@ -279,36 +292,41 @@
     key[EDGE:] = mixed(taps, 1, key, EDGE, ahead)
     value[EDGE:] = mixed(taps, 2, value, EDGE, ahead)
     product[:span] = before[:span]
-    product[span:] = key[EDGE:] * value[EDGE:]
+    product[span : span + ahead] = key[EDGE:] * value[EDGE:]
+    product[span + ahead :] = jnp.zeros((product.shape[0] - span - ahead, lanes), jnp.float32)
     query[EDGE:] = mixed(taps, 0, query, EDGE, ahead)
     back_filtered[:rows] = grad[...].astype(jnp.float32) * query[EDGE:ahead]
     back_filtered[rows:ahead] = slope_after * query[ahead:]
-    back_filtered[ahead:] = after[EDGE:reach]
-
-    def long_filter(source, later):
-        length = source.shape[0]
-        for shift in range(8):
-            shifts[shift, : length - shift] = source[shift:]
-
-        def accumulate(block, total):
-            for inner in range(8):
-                offset = block * 8 + inner
-                if later:
-                    shift, begin = inner, block
-                else:
-                    shift, begin = -inner % 8, span // 8 - block - (inner > 0)
-                begin = pl.multiple_of(begin * 8, 8)
-                total = total + filters[pl.ds(offset, 1), :] * shifts[shift, pl.ds(begin, ahead), :]
-            return total
-
-        return lax.fori_loop(0, span // 8, accumulate, jnp.zeros((ahead, lanes), jnp.float32))
-
-    filtered = long_filter(product, False)
+    back_filtered[ahead : rows + reach] = after[EDGE:reach]
+    back_filtered[rows + reach :] = jnp.zeros(
+        (back_filtered.shape[0] - rows - reach, lanes), jnp.float32
+    )
+
+    owner = lax.broadcasted_iota(jnp.int32, (BAND, lanes), 1) // GROUP
+
+    def long_filter(source, high, low, out):
+        for begin in range(0, out.shape[0], BAND):
+            section = source[begin : begin + 2 * span]
+            upper = section.astype(jnp.bfloat16)
+            lower = (section - upper.astype(jnp.float32)).astype(jnp.bfloat16)
+            both = jnp.dot(
+                high[...], jnp.concatenate([upper, lower], 1), preferred_element_type=jnp.float32
+            )
+            rest = jnp.dot(low[...], upper, preferred_element_type=jnp.float32)
+            summed = both[:, :lanes] + both[:, lanes:] + rest
+            chosen = summed[:BAND]
+            for group in range(1, lanes // GROUP):
+                chosen = jnp.where(
+                    owner == group, summed[group * BAND : (group + 1) * BAND], chosen
+                )
+            out[begin : begin + BAND] = chosen
+
+    long_filter(product, high, low, filtered)
+    long_filter(back_filtered, later_high, later_low, back_product)
     grads[0, :rows] = grad[...].astype(jnp.float32) * filtered[:rows]
-    grads[0, rows:] = slope_after * filtered[rows:]
-    back_product = long_filter(back_filtered, True)
-    grads[1] = back_product * value[EDGE:]
-    grads[2] = back_product * key[EDGE:]
+    grads[0, rows:] = slope_after * filtered[rows:ahead]
+    grads[1] = back_product[:ahead] * value[EDGE:]
+    grads[2] = back_product[:ahead] * key[EDGE:]
     total = jnp.zeros((rows, lanes), jnp.float32)
     for index in range(3):
         back = tap(taps, 0, index) * grads[index, :rows]
@@ -338,35 +356,36 @@
     effects[...] = scores[0, rows:]
 
 
-def mixer(picks, feature, within, across, grad, taps, filters):
+def mixer(picks, feature, within, across, grad, taps, span, weights):
     rows, lanes = grad.shape
-    span = filters.shape[0]
     count = feature.shape[1]
 
     def body(*refs):
-        mixer_kernel(rows, *refs)
-
-    length = span + rows + EDGE
+        mixer_kernel(rows, span, *refs)
+
+    steps = pl.cdiv(rows + EDGE, BAND)
+    length = (steps - 1) * BAND + 2 * span
     return pl.pallas_call(
         body,
         out_shape=[
             jax.ShapeDtypeStruct((rows,), jnp.float32),
             jax.ShapeDtypeStruct((count - rows,), jnp.float32),
         ],
-        in_specs=[SMEM] + [VMEM] * 6,
+        in_specs=[SMEM] + [VMEM] * 9,
         out_specs=[VMEM, VMEM],
         scratch_shapes=[pltpu.VMEM((span + 5 * EDGE, lanes), jnp.float32)] * 2
         + [pltpu.VMEM((rows + 2 * EDGE, lanes), jnp.float32)] * 3
         + [
             pltpu.VMEM((length, lanes), jnp.float32),
             pltpu.VMEM((length, lanes), jnp.float32),
-            pltpu.VMEM((8, length, lanes), jnp.float32),
+            pltpu.VMEM((steps * BAND, lanes), jnp.float32),
+            pltpu.VMEM((steps * BAND, lanes), jnp.float32),
             pltpu.VMEM((3, rows + EDGE, lanes), jnp.float32),
             pltpu.VMEM((count, lanes), jnp.float32),
         ],
-        compiler_params=pltpu.CompilerParams(vmem_limit_bytes=8 << 20),
+        compiler_params=pltpu.CompilerParams(vmem_limit_bytes=12 << 20),
         name="mixer",
-    )(picks, feature, within, across, grad, taps, filters)
+    )(picks, feature, within, across, grad, taps, *weights)
 
 
 def gathered_features(tokens, proj, lanes):
@@ -416,20 +435,21 @@
     far = own_4a, own_4b, own_5a, own_5b, own_6a, own_6b, own_7a, own_7b
     give_other, keep_other, give_mine, keep_mine = products(tokens, alternates, theirs, near + far)
     other = crossed(keep_other + crossed(give_other, "grp", 1), "rep", 1)
-    return (keep_mine, crossed(give_mine, "grp", 1), other), early
+    return (keep_mine, other) + tuple(crossed(part, "grp", 1) for part in give_mine), early
 
 
 def per_device(hidden, proj, short_taps, filters, grad_out, var_pos, alt_hidden):
     lanes = grad_out.shape[1]
-    early = spread(filters), short_taps, var_pos
+    span = filters.shape[1]
+    early = bands(filters), short_taps, var_pos
     if lax.axis_size("seq") == 8:
         terms, early = cube_features(hidden, alt_hidden, proj, early)
     else:
         terms = gathered_features((hidden, alt_hidden), proj, lanes)
-    per_channel, short_taps, picks = early
-    feature, within, across = edges(grad_out, short_taps, filters.shape[1], terms)
+    weights, short_taps, picks = early
+    feature, within, across = edges(grad_out, short_taps, span, terms)
     within, across = paired(within, "seq", 0), paired(across, "seq", 1)
-    scores = mixer(picks, feature, within, across, grad_out, short_taps, per_channel)
+    scores = mixer(picks, feature, within, across, grad_out, short_taps, span, weights)
     return tuple(lax.psum(tuple(scores), "grp"))
 
 

time: 80.5 us -> 77.7 us (0.965)
  Pallas kernels: 8.82 us -> 6.75 us
  waiting for transfers between devices: 42.6 us -> 41.1 us
  starting transfers between devices: 18.9 us -> 19.8 us
    pallas_call x1, Pallas kernels: 4.97 us -> 2.46 us  [mixer(): pl.pallas_call(body, out_shape=[jax.ShapeDtypeStruct((rows,), jnp.float32...]
    ppermute x15 -> x17, waiting for transfers between devices: 38.4 us -> 36.9 us  [crossed(): lax.ppermute(block, axis, [(i, i ^ bit) for i in range(lax.axis_size(axis...]
    ppermute x15 -> x17, starting transfers between devices: 15.7 us -> 16.6 us  [crossed(): lax.ppermute(block, axis, [(i, i ^ bit) for i in range(lax.axis_size(axis...]
  transfers between devices with their start and end apart: 17 -> 19, of which waited for: 12 -> 15; matrix products, arithmetic and copies ran while one was open for 0% -> 0% of each run, Pallas kernels for 2% -> 3%
where the time goes in v5:
time: 77.7 us; the launch traced here: 77.5 us
  waiting for transfers between devices  41.1 us (53%)
  starting transfers between devices  19.8 us (25%)
  Pallas kernels  6.75 us (9%)
  blocking collectives  5.34 us (7%)
  local copies, waits for them, and re-layouts  3.69 us (5%)
    ppermute x17, waiting for transfers between devices, crossed(): lax.ppermute(block, axis, [(i, i ^ bit) for i in range(lax.axis_size(axis...  36.9 us
    ppermute x17, starting transfers between devices, crossed(): lax.ppermute(block, axis, [(i, i ^ bit) for i in range(lax.axis_size(axis...  16.6 us
    psum x1, blocking collectives, per_device(): return tuple(lax.psum(tuple(scores), 'grp'))  5.34 us
    ppermute x2, waiting for transfers between devices, paired(): return lax.ppermute(block, axis, route)  4.2 us
    unnamed x18, local copies, waits for them, and re-layouts  3.69 us
    ppermute x2, starting transfers between devices, paired(): return lax.ppermute(block, axis, route)  3.19 us
    pallas_call x1, Pallas kernels, mixer(): pl.pallas_call(body, out_shape=[jax.ShapeDtypeStruct((rows,), jnp.float32...  2.46 us
    pallas_call x1, Pallas kernels, products(): pl.pallas_call(theirs_kernel, out_shape=[half, half, jax.ShapeDtypeStruct...  1.61 us
  transfers between devices with their start and end apart: 19, of which 15 were waited for; matrix products, arithmetic and copies ran while one was open for 0% of the time, Pallas kernels for 3%

profile of v5, /device:TPU:23, one launch (start us, length us, event | category | flops | bytes accessed | tf_op | source)
XLA Modules:
  0.0 77.5 jit_solution(15375967615507889473)
XLA Ops:
  0.6 0.0 copy-start.2
  0.6 1.1 %copy-done.2 = bf16[3,32,4096]{2,1,0:T(8,128)(2,1)S(1)} copy-done((bf16[3,32,4096]{2,1,0:T(8,128)(2,1)S(1)}, bf16[3,32,4096]{2,1,0:T(8,128)(2,1)}, u32[]{:S(2)}) %copy-start.2) | copy-done | bytes 786456
  1.8 0.0 copy-start.7
  1.8 0.1 panels.1
  1.9 0.3 collective-permute-start.1
  2.2 1.3 %collective-permute-start = (bf16[3,32,2048]{2,1,0:T(8,128)(2,1)S(1)}, bf16[3,32,2048]{2,1,0:T(8,128)(2,1)S(1)}, u32[]{:S(2)}, u32[]{:S(2)}) collective-permute-start(bf16[3,32,2048]{2,1,0:T(8,128)(2,1)S(1)} %get-tuple-element.37.refs_0_), channel_id=1, source_target_pairs={{0,4},{2,6},{4,0},{6,2},{8,12},{10,14},{12,8},{14,10},{1,5},{3,7},... | collective-permute-start | bytes 1179656 | tf_op jit(solution)/shard_map/ppermute | solution.py:30
  3.5 0.0 copy-start
  3.5 1.6 %copy-done = bf16[272,4096]{1,0:T(8,128)(2,1)S(1)} copy-done((bf16[272,4096]{1,0:T(8,128)(2,1)S(1)}, bf16[272,4096]{1,0:T(8,128)(2,1)}, u32[]{:S(2)}) %copy-start) | copy-done | bytes 2228248
  5.2 0.0 copy-start.3
  5.2 0.9 %copy-done.3 = bf16[16,4096]{1,0:T(8,128)(2,1)S(1)} copy-done((bf16[16,4096]{1,0:T(8,128)(2,1)S(1)}, bf16[16,4096]{1,0:T(8,128)(2,1)}, u32[]{:S(2)}) %copy-start.3) | copy-done | bytes 131096
  6.1 0.1 columns.1
  6.2 0.3 collective-permute-start.5
  6.5 0.1 collective-permute-start.2
  6.5 9.5 %collective-permute-done.2.refs_4_ = bf16[3,16,2048]{2,1,0:T(8,128)(2,1)S(1)} collective-permute-done((bf16[3,16,2048]{2,1,0:T(8,128)(2,1)S(1)}, bf16[3,16,2048]{2,1,0:T(8,128)(2,1)S(1)}, u32[]{:S(2)}, u32[]{:S(2)}) %collective-permute-start.2) | collective-permute-done | bytes 196640 | tf_op jit(solution)/shard_map/ppermute | solution.py:30
  16.0 0.0 collective-permute-done.1.refs_1_
  16.0 0.0 collective-permute-done.refs_2_
  16.0 1.2 %collective-permute-start.4 = (bf16[3,32,2048]{2,1,0:T(8,128)(2,1)S(1)}, bf16[3,32,2048]{2,1,0:T(8,128)(2,1)S(1)}, u32[]{:S(2)}, u32[]{:S(2)}) collective-permute-start(bf16[3,32,2048]{2,1,0:T(8,128)(2,1)S(1)} %collective-permute-done.refs_2_), channel_id=1, source_target_pairs={{0,2},{2,0},{4,6},{6,4},{8,10},{10,8},{12,14},{14,12},{1,3},{3,1},... | collective-permute-start | bytes 1179656 | tf_op jit(solution)/shard_map/ppermute | solution.py:30
  17.3 0.1 collective-permute-start.3
  17.4 0.0 copy-done.7
  17.4 0.7 bands.1
  18.1 4.7 %collective-permute-done.3.refs_5_ = bf16[3,16,2048]{2,1,0:T(8,128)(2,1)S(1)} collective-permute-done((bf16[3,16,2048]{2,1,0:T(8,128)(2,1)S(1)}, bf16[3,16,2048]{2,1,0:T(8,128)(2,1)S(1)}, u32[]{:S(2)}, u32[]{:S(2)}) %collective-permute-start.3) | collective-permute-done | bytes 196640 | tf_op jit(solution)/shard_map/ppermute | solution.py:30
  22.8 2.0 %collective-permute-done.4.refs_3_ = bf16[3,32,2048]{2,1,0:T(8,128)(2,1)S(1)} collective-permute-done((bf16[3,32,2048]{2,1,0:T(8,128)(2,1)S(1)}, bf16[3,32,2048]{2,1,0:T(8,128)(2,1)S(1)}, u32[]{:S(2)}, u32[]{:S(2)}) %collective-permute-start.4) | collective-permute-done | bytes 393248 | tf_op jit(solution)/shard_map/ppermute | solution.py:30
  24.7 0.0 copy-start.1
  24.7 0.0 copy-start.4
  24.7 1.2 %collective-permute-start.8 = (bf16[3,16,2048]{2,1,0:T(8,128)(2,1)S(1)}, bf16[3,16,2048]{2,1,0:T(8,128)(2,1)S(1)}, u32[]{:S(2)}, u32[]{:S(2)}) collective-permute-start(bf16[3,16,2048]{2,1,0:T(8,128)(2,1)S(1)} %collective-permute-done.2.refs_4_), channel_id=1, source_target_pairs={{0,2},{2,0},{4,6},{6,4},{8,10},{10,8},{12,14},{14,12},{1,3},{3,1},... | collective-permute-start | bytes 589832 | tf_op jit(solution)/shard_map/ppermute | solution.py:30
  25.9 4.1 %collective-permute-start.6 = (bf16[3,16,2048]{2,1,0:T(8,128)(2,1)S(1)}, bf16[3,16,2048]{2,1,0:T(8,128)(2,1)S(1)}, u32[]{:S(2)}, u32[]{:S(2)}) collective-permute-start(bf16[3,16,2048]{2,1,0:T(8,128)(2,1)S(1)} %collective-permute-done.2.refs_4_), channel_id=1, source_target_pairs={{0,4},{2,6},{4,0},{6,2},{8,12},{10,14},{12,8},{14,10},{1,5},{3,7},... | collective-permute-start | bytes 589832 | tf_op jit(solution)/shard_map/ppermute | solution.py:30
  30.1 1.2 %collective-permute-start.9 = (bf16[3,16,2048]{2,1,0:T(8,128)(2,1)S(1)}, bf16[3,16,2048]{2,1,0:T(8,128)(2,1)S(1)}, u32[]{:S(2)}, u32[]{:S(2)}) collective-permute-start(bf16[3,16,2048]{2,1,0:T(8,128)(2,1)S(1)} %collective-permute-done.3.refs_5_), channel_id=1, source_target_pairs={{0,2},{2,0},{4,6},{6,4},{8,10},{10,8},{12,14},{14,12},{1,3},{3,1},... | collective-permute-start | bytes 589832 | tf_op jit(solution)/shard_map/ppermute | solution.py:30
  31.3 0.0 collective-permute-start.7
  31.3 0.0 collective-permute-done.8.refs_6_
  31.3 2.6 %collective-permute-done.6.refs_8_ = bf16[3,16,2048]{2,1,0:T(8,128)(2,1)S(1)} collective-permute-done((bf16[3,16,2048]{2,1,0:T(8,128)(2,1)S(1)}, bf16[3,16,2048]{2,1,0:T(8,128)(2,1)S(1)}, u32[]{:S(2)}, u32[]{:S(2)}) %collective-permute-start.6) | collective-permute-done | bytes 196640 | tf_op jit(solution)/shard_map/ppermute | solution.py:30
  33.9 1.1 %collective-permute-done.9.refs_7_ = bf16[3,16,2048]{2,1,0:T(8,128)(2,1)S(1)} collective-permute-done((bf16[3,16,2048]{2,1,0:T(8,128)(2,1)S(1)}, bf16[3,16,2048]{2,1,0:T(8,128)(2,1)S(1)}, u32[]{:S(2)}, u32[]{:S(2)}) %collective-permute-start.9) | collective-permute-done | bytes 196640 | tf_op jit(solution)/shard_map/ppermute | solution.py:30
  35.0 3.3 %collective-permute-done.7.refs_9_ = bf16[3,16,2048]{2,1,0:T(8,128)(2,1)S(1)} collective-permute-done((bf16[3,16,2048]{2,1,0:T(8,128)(2,1)S(1)}, bf16[3,16,2048]{2,1,0:T(8,128)(2,1)S(1)}, u32[]{:S(2)}, u32[]{:S(2)}) %collective-permute-start.7) | collective-permute-done | bytes 196640 | tf_op jit(solution)/shard_map/ppermute | solution.py:30
  38.2 1.1 %collective-permute-start.11 = (bf16[3,16,2048]{2,1,0:T(8,128)(2,1)S(1)}, bf16[3,16,2048]{2,1,0:T(8,128)(2,1)S(1)}, u32[]{:S(2)}, u32[]{:S(2)}) collective-permute-start(bf16[3,16,2048]{2,1,0:T(8,128)(2,1)S(1)} %collective-permute-done.9.refs_7_), channel_id=1, source_target_pairs={{0,4},{2,6},{4,0},{6,2},{8,12},{10,14},{12,8},{14,10},{1,5},{3,7},... | collective-permute-start | bytes 589832 | tf_op jit(solution)/shard_map/ppermute | solution.py:30
  39.3 1.2 %collective-permute-start.10 = (bf16[3,16,2048]{2,1,0:T(8,128)(2,1)S(1)}, bf16[3,16,2048]{2,1,0:T(8,128)(2,1)S(1)}, u32[]{:S(2)}, u32[]{:S(2)}) collective-permute-start(bf16[3,16,2048]{2,1,0:T(8,128)(2,1)S(1)} %collective-permute-done.6.refs_8_), channel_id=1, source_target_pairs={{0,2},{2,0},{4,6},{6,4},{8,10},{10,8},{12,14},{14,12},{1,3},{3,1},... | collective-permute-start | bytes 589832 | tf_op jit(solution)/shard_map/ppermute | solution.py:30
  40.5 0.0 collective-permute-done.5.theirs
  40.5 2.2 %collective-permute-done.11.refs_11_ = bf16[3,16,2048]{2,1,0:T(8,128)(2,1)S(1)} collective-permute-done((bf16[3,16,2048]{2,1,0:T(8,128)(2,1)S(1)}, bf16[3,16,2048]{2,1,0:T(8,128)(2,1)S(1)}, u32[]{:S(2)}, u32[]{:S(2)}) %collective-permute-start.11) | collective-permute-done | bytes 196640 | tf_op jit(solution)/shard_map/ppermute | solution.py:30
  42.7 1.4 %collective-permute-done.10.refs_10_ = bf16[3,16,2048]{2,1,0:T(8,128)(2,1)S(1)} collective-permute-done((bf16[3,16,2048]{2,1,0:T(8,128)(2,1)S(1)}, bf16[3,16,2048]{2,1,0:T(8,128)(2,1)S(1)}, u32[]{:S(2)}, u32[]{:S(2)}) %collective-permute-start.10) | collective-permute-done | bytes 196640 | tf_op jit(solution)/shard_map/ppermute | solution.py:30
  44.1 1.6 %theirs.1 = (f32[3,288,128]{2,1,0:T(8,128)S(1)}, f32[3,288,128]{2,1,0:T(8,128)S(1)}, bf16[768,2048]{1,0:T(8,128)(2,1)S(1)}) custom-call(bf16[288,2048]{1,0:T(8,128)(2,1)S(1)} %collective-permute-done.5.theirs, bf16[3,32,2048]{2,1,0:T(8,128)(2,1)S(1)} %get-tuple-element.37.refs_0_, bf16[3,32,2048]{2,1,0:T(8,128)(2,1)S(1)} %collective-permute-done.1.refs_1_, ...), custom_call_target="tpu_custom_call" | custom-call | flops 905969664 | bytes 5210112 | tf_op jit(solution)/shard_map/theirs/pallas_call | solution.py:161
  45.7 3.5 %collective-permute-start.12 = (f32[3,288,128]{2,1,0:T(8,128)S(1)}, f32[3,288,128]{2,1,0:T(8,128)S(1)}, u32[]{:S(2)}, u32[]{:S(2)}) collective-permute-start(f32[3,288,128]{2,1,0:T(8,128)S(1)} %get-tuple-element.59), channel_id=1, source_target_pairs={{0,1},{1,0},{2,3},{3,2},{4,5},{5,4},{6,7},{7,6},{8,9},{9,8},{10,11... | collective-permute-start | bytes 1327112 | tf_op jit(solution)/shard_map/ppermute | solution.py:30
  49.2 1.4 %collective-permute-done.12 = f32[3,288,128]{2,1,0:T(8,128)S(1)} collective-permute-done((f32[3,288,128]{2,1,0:T(8,128)S(1)}, f32[3,288,128]{2,1,0:T(8,128)S(1)}, u32[]{:S(2)}, u32[]{:S(2)}) %collective-permute-start.12) | collective-permute-done | bytes 442400 | tf_op jit(solution)/shard_map/ppermute | solution.py:30
  50.7 0.1 collective-permute-start.13
  50.8 0.0 copy-done.1
  50.8 0.0 copy-done.4
  50.8 0.0 copy-start.5
  50.8 0.0 copy-start.6
  50.8 0.0 copy-start.8
  50.8 1.6 %ours.1 = (f32[288,128]{1,0:T(8,128)S(1)}, f32[288,128]{1,0:T(8,128)S(1)}, f32[288,128]{1,0:T(8,128)S(1)}, f32[3,288,128]{2,1,0:T(8,128)S(1)}) custom-call(bf16[272,4096]{1,0:T(8,128)(2,1)S(1)} %copy-done.1, bf16[16,4096]{1,0:T(8,128)(2,1)S(1)} %copy-done.4, bf16[768,2048]{1,0:T(8,128)(2,1)S(1)} %get-tuple-element.56.panel), custom_call_target="tpu_custom_call" | custom-call | flops 905969664 | bytes 5210112 | tf_op jit(solution)/shard_map/ours/pallas_call | solution.py:170
  52.4 0.4 collective-permute-start.14
  52.9 0.1 collective-permute-start.15
  53.0 0.4 collective-permute-start.16
  53.4 0.5 collective-permute-done.14.refs_2_
  53.9 0.4 collective-permute-done.15.refs_3_
  54.2 0.2 collective-permute-done.16.refs_4_
  54.4 7.7 %collective-permute-done.13.refs_1_ = f32[3,288,128]{2,1,0:T(8,128)S(1)} collective-permute-done((f32[3,288,128]{2,1,0:T(8,128)S(1)}, f32[3,288,128]{2,1,0:T(8,128)S(1)}, u32[]{:S(2)}, u32[]{:S(2)}) %collective-permute-start.13) | collective-permute-done | bytes 442400 | tf_op jit(solution)/shard_map/ppermute | solution.py:30
  62.1 0.0 copy-done.5
  62.1 0.0 copy-done.6
  62.2 0.1 edges.1
  62.3 1.3 %collective-permute-start.17 = (f32[168,128]{1,0:T(8,128)S(1)}, f32[168,128]{1,0:T(8,128)S(1)}, u32[]{:S(2)}, u32[]{:S(2)}) collective-permute-start(f32[168,128]{1,0:T(8,128)S(1)} %get-tuple-element.64), channel_id=1, source_target_pairs={{0,2},{2,0},{4,6},{6,4},{8,10},{10,8},{12,14},{14,12},{1,3},{3,1},... | collective-permute-start | bytes 258056 | tf_op jit(solution)/shard_map/ppermute | solution.py:26
  63.6 1.9 %collective-permute-start.18 = (f32[168,128]{1,0:T(8,128)S(1)}, f32[168,128]{1,0:T(8,128)S(1)}, u32[]{:S(2)}, u32[]{:S(2)}) collective-permute-start(f32[168,128]{1,0:T(8,128)S(1)} %get-tuple-element.65), channel_id=1, source_target_pairs={{2,4},{4,2},{6,8},{8,6},{10,12},{12,10},{3,5},{5,3},{7,9},{9,7},{1... | collective-permute-start | bytes 258056 | tf_op jit(solution)/shard_map/ppermute | solution.py:26
  65.5 0.2 collective-permute-done.17.refs_2_
  65.7 4.0 %collective-permute-done.18.refs_3_ = f32[168,128]{1,0:T(8,128)S(1)} collective-permute-done((f32[168,128]{1,0:T(8,128)S(1)}, f32[168,128]{1,0:T(8,128)S(1)}, u32[]{:S(2)}, u32[]{:S(2)}) %collective-permute-start.18) | collective-permute-done | bytes 86048 | tf_op jit(solution)/shard_map/ppermute | solution.py:26
  69.7 0.0 copy-done.8
  69.7 2.5 %mixer.1 = (f32[272]{0:T(512)S(1)}, f32[16]{0:T(128)S(1)}) custom-call(s32[16]{0:T(128)S(1)} %copy-done.8, f32[3,288,128]{2,1,0:T(8,128)S(1)} %get-tuple-element.63.refs_1_, f32[168,128]{1,0:T(8,128)S(1)} %collective-permute-done.17.refs_2_, f32[168,128]{1,0:T(8,128)S(1)} %collective-permute-done.18.refs_3_, bf16[272,128]{1,0:T(8,128)(2,1)S(1)} %copy-done.5, ...), custom_call_target="tpu_custom_call" | custom-call | tf_op jit(solution)/shard_map/mixer/pallas_call | solution.py:368
  72.2 5.3 %all-reduce = (f32[272]{0:T(512)}, f32[16]{0:T(128)}) all-reduce(f32[272]{0:T(512)S(1)} %get-tuple-element.70, f32[16]{0:T(128)S(1)} %get-tuple-element.71), channel_id=1, replica_groups=mesh['rep'=2,'seq'=8,'grp'=2] {'grp'}, use_global_device_ids=true, to_apply=%region_0.0 | all-reduce | flops 288 | bytes 2304 | tf_op jit(solution)/shard_map/psum | solution.py:453
  (1 shorter events, 0.0 us)
Async XLA Ops:
  0.6 1.1 %copy-start.2 = (bf16[3,32,4096]{2,1,0:T(8,128)(2,1)S(1)}, bf16[3,32,4096]{2,1,0:T(8,128)(2,1)}, u32[]{:S(2)}) copy-start(bf16[3,32,4096]{2,1,0:T(8,128)(2,1)} %proj.1) | copy-start | bytes 2359300
  1.8 15.6 %copy-start.7 = (f32[8,128]{1,0:T(8,128)S(1)}, f32[8,128]{1,0:T(8,128)}, u32[]{:S(2)}) copy-start(f32[8,128]{1,0:T(8,128)} %filters.1) | copy-start | bytes 12292
  1.9 14.1 %collective-permute-start.1 = (bf16[3,32,2048]{2,1,0:T(8,128)(2,1)S(1)}, bf16[3,32,2048]{2,1,0:T(8,128)(2,1)S(1)}, u32[]{:S(2)}, u32[]{:S(2)}) collective-permute-start(bf16[3,32,2048]{2,1,0:T(8,128)(2,1)S(1)} %get-tuple-element.37.refs_0_), channel_id=1, source_target_pairs={{0,2},{2,0},{4,6},{6,4},{8,10},{10,8},{12,14},{14,12},{1,3},{3,1},... | collective-permute-start | bytes 1179656 | tf_op jit(solution)/shard_map/ppermute | solution.py:30
  2.2 13.8 %collective-permute-start = (bf16[3,32,2048]{2,1,0:T(8,128)(2,1)S(1)}, bf16[3,32,2048]{2,1,0:T(8,128)(2,1)S(1)}, u32[]{:S(2)}, u32[]{:S(2)}) collective-permute-start(bf16[3,32,2048]{2,1,0:T(8,128)(2,1)S(1)} %get-tuple-element.37.refs_0_), channel_id=1, source_target_pairs={{0,4},{2,6},{4,0},{6,2},{8,12},{10,14},{12,8},{14,10},{1,5},{3,7},... | collective-permute-start | bytes 1179656 | tf_op jit(solution)/shard_map/ppermute | solution.py:30
  3.5 1.6 %copy-start = (bf16[272,4096]{1,0:T(8,128)(2,1)S(1)}, bf16[272,4096]{1,0:T(8,128)(2,1)}, u32[]{:S(2)}) copy-start(bf16[272,4096]{1,0:T(8,128)(2,1)} %tokens.3) | copy-start | bytes 6684676
  5.2 0.9 %copy-start.3 = (bf16[16,4096]{1,0:T(8,128)(2,1)S(1)}, bf16[16,4096]{1,0:T(8,128)(2,1)}, u32[]{:S(2)}) copy-start(bf16[16,4096]{1,0:T(8,128)(2,1)} %alternates.3) | copy-start | bytes 393220
  6.2 34.3 %collective-permute-start.5 = (bf16[288,2048]{1,0:T(8,128)(2,1)S(1)}, bf16[288,2048]{1,0:T(8,128)(2,1)S(1)}, u32[]{:S(2)}, u32[]{:S(2)}) collective-permute-start(bf16[288,2048]{1,0:T(8,128)(2,1)S(1)} %columns.1), channel_id=1, source_target_pairs={{0,16},{16,0},{1,17},{17,1},{2,18},{18,2},{3,19},{19,3},{4,20},{20... | collective-permute-start | bytes 3538952 | tf_op jit(solution)/shard_map/ppermute | solution.py:30
  6.5 9.5 %collective-permute-start.2 = (bf16[3,16,2048]{2,1,0:T(8,128)(2,1)S(1)}, bf16[3,16,2048]{2,1,0:T(8,128)(2,1)S(1)}, u32[]{:S(2)}, u32[]{:S(2)}) collective-permute-start(bf16[3,16,2048]{2,1,0:T(8,128)(2,1)S(1)} %get-tuple-element.38), channel_id=1, source_target_pairs={{0,8},{2,10},{4,12},{6,14},{8,0},{10,2},{12,4},{14,6},{1,9},{3,11}... | collective-permute-start | bytes 589832 | tf_op jit(solution)/shard_map/ppermute | solution.py:30
  16.0 8.7 %collective-permute-start.4 = (bf16[3,32,2048]{2,1,0:T(8,128)(2,1)S(1)}, bf16[3,32,2048]{2,1,0:T(8,128)(2,1)S(1)}, u32[]{:S(2)}, u32[]{:S(2)}) collective-permute-start(bf16[3,32,2048]{2,1,0:T(8,128)(2,1)S(1)} %collective-permute-done.refs_2_), channel_id=1, source_target_pairs={{0,2},{2,0},{4,6},{6,4},{8,10},{10,8},{12,14},{14,12},{1,3},{3,1},... | collective-permute-start | bytes 1179656 | tf_op jit(solution)/shard_map/ppermute | solution.py:30
  17.3 5.5 %collective-permute-start.3 = (bf16[3,16,2048]{2,1,0:T(8,128)(2,1)S(1)}, bf16[3,16,2048]{2,1,0:T(8,128)(2,1)S(1)}, u32[]{:S(2)}, u32[]{:S(2)}) collective-permute-start(bf16[3,16,2048]{2,1,0:T(8,128)(2,1)S(1)} %get-tuple-element.40), channel_id=1, source_target_pairs={{0,8},{2,10},{4,12},{6,14},{8,0},{10,2},{12,4},{14,6},{1,9},{3,11}... | collective-permute-start | bytes 589832 | tf_op jit(solution)/shard_map/ppermute | solution.py:30
  24.7 26.1 %copy-start.1 = (bf16[272,4096]{1,0:T(8,128)(2,1)S(1)}, bf16[272,4096]{1,0:T(8,128)(2,1)}, u32[]{:S(2)}) copy-start(bf16[272,4096]{1,0:T(8,128)(2,1)} %tokens.3) | copy-start | bytes 6684676
  24.7 26.1 %copy-start.4 = (bf16[16,4096]{1,0:T(8,128)(2,1)S(1)}, bf16[16,4096]{1,0:T(8,128)(2,1)}, u32[]{:S(2)}) copy-start(bf16[16,4096]{1,0:T(8,128)(2,1)} %alternates.3) | copy-start | bytes 393220
  24.7 6.6 %collective-permute-start.8 = (bf16[3,16,2048]{2,1,0:T(8,128)(2,1)S(1)}, bf16[3,16,2048]{2,1,0:T(8,128)(2,1)S(1)}, u32[]{:S(2)}, u32[]{:S(2)}) collective-permute-start(bf16[3,16,2048]{2,1,0:T(8,128)(2,1)S(1)} %collective-permute-done.2.refs_4_), channel_id=1, source_target_pairs={{0,2},{2,0},{4,6},{6,4},{8,10},{10,8},{12,14},{14,12},{1,3},{3,1},... | collective-permute-start | bytes 589832 | tf_op jit(solution)/shard_map/ppermute | solution.py:30
  25.9 7.9 %collective-permute-start.6 = (bf16[3,16,2048]{2,1,0:T(8,128)(2,1)S(1)}, bf16[3,16,2048]{2,1,0:T(8,128)(2,1)S(1)}, u32[]{:S(2)}, u32[]{:S(2)}) collective-permute-start(bf16[3,16,2048]{2,1,0:T(8,128)(2,1)S(1)} %collective-permute-done.2.refs_4_), channel_id=1, source_target_pairs={{0,4},{2,6},{4,0},{6,2},{8,12},{10,14},{12,8},{14,10},{1,5},{3,7},... | collective-permute-start | bytes 589832 | tf_op jit(solution)/shard_map/ppermute | solution.py:30
  30.1 4.9 %collective-permute-start.9 = (bf16[3,16,2048]{2,1,0:T(8,128)(2,1)S(1)}, bf16[3,16,2048]{2,1,0:T(8,128)(2,1)S(1)}, u32[]{:S(2)}, u32[]{:S(2)}) collective-permute-start(bf16[3,16,2048]{2,1,0:T(8,128)(2,1)S(1)} %collective-permute-done.3.refs_5_), channel_id=1, source_target_pairs={{0,2},{2,0},{4,6},{6,4},{8,10},{10,8},{12,14},{14,12},{1,3},{3,1},... | collective-permute-start | bytes 589832 | tf_op jit(solution)/shard_map/ppermute | solution.py:30
  31.3 6.9 %collective-permute-start.7 = (bf16[3,16,2048]{2,1,0:T(8,128)(2,1)S(1)}, bf16[3,16,2048]{2,1,0:T(8,128)(2,1)S(1)}, u32[]{:S(2)}, u32[]{:S(2)}) collective-permute-start(bf16[3,16,2048]{2,1,0:T(8,128)(2,1)S(1)} %collective-permute-done.3.refs_5_), channel_id=1, source_target_pairs={{0,4},{2,6},{4,0},{6,2},{8,12},{10,14},{12,8},{14,10},{1,5},{3,7},... | collective-permute-start | bytes 589832 | tf_op jit(solution)/shard_map/ppermute | solution.py:30
  38.2 4.5 %collective-permute-start.11 = (bf16[3,16,2048]{2,1,0:T(8,128)(2,1)S(1)}, bf16[3,16,2048]{2,1,0:T(8,128)(2,1)S(1)}, u32[]{:S(2)}, u32[]{:S(2)}) collective-permute-start(bf16[3,16,2048]{2,1,0:T(8,128)(2,1)S(1)} %collective-permute-done.9.refs_7_), channel_id=1, source_target_pairs={{0,4},{2,6},{4,0},{6,2},{8,12},{10,14},{12,8},{14,10},{1,5},{3,7},... | collective-permute-start | bytes 589832 | tf_op jit(solution)/shard_map/ppermute | solution.py:30
  39.3 4.8 %collective-permute-start.10 = (bf16[3,16,2048]{2,1,0:T(8,128)(2,1)S(1)}, bf16[3,16,2048]{2,1,0:T(8,128)(2,1)S(1)}, u32[]{:S(2)}, u32[]{:S(2)}) collective-permute-start(bf16[3,16,2048]{2,1,0:T(8,128)(2,1)S(1)} %collective-permute-done.6.refs_8_), channel_id=1, source_target_pairs={{0,2},{2,0},{4,6},{6,4},{8,10},{10,8},{12,14},{14,12},{1,3},{3,1},... | collective-permute-start | bytes 589832 | tf_op jit(solution)/shard_map/ppermute | solution.py:30
  45.7 4.9 %collective-permute-start.12 = (f32[3,288,128]{2,1,0:T(8,128)S(1)}, f32[3,288,128]{2,1,0:T(8,128)S(1)}, u32[]{:S(2)}, u32[]{:S(2)}) collective-permute-start(f32[3,288,128]{2,1,0:T(8,128)S(1)} %get-tuple-element.59), channel_id=1, source_target_pairs={{0,1},{1,0},{2,3},{3,2},{4,5},{5,4},{6,7},{7,6},{8,9},{9,8},{10,11... | collective-permute-start | bytes 1327112 | tf_op jit(solution)/shard_map/ppermute | solution.py:30
  50.7 11.4 %collective-permute-start.13 = (f32[3,288,128]{2,1,0:T(8,128)S(1)}, f32[3,288,128]{2,1,0:T(8,128)S(1)}, u32[]{:S(2)}, u32[]{:S(2)}) collective-permute-start(f32[3,288,128]{2,1,0:T(8,128)S(1)} %add.7), channel_id=1, source_target_pairs={{0,16},{16,0},{1,17},{17,1},{2,18},{18,2},{3,19},{19,3},{4,20},{20... | collective-permute-start | bytes 1327112 | tf_op jit(solution)/shard_map/ppermute | solution.py:30
  50.8 11.4 %copy-start.5 = (bf16[272,128]{1,0:T(8,128)(2,1)S(1)}, bf16[272,128]{1,0:T(8,128)(2,1)}, u32[]{:S(2)}) copy-start(bf16[272,128]{1,0:T(8,128)(2,1)} %refs_4_.1) | copy-start | bytes 208900
  50.8 11.3 %copy-start.6 = (f32[3,3,128]{2,1,0:T(4,128)S(1)}, f32[3,3,128]{2,1,0:T(4,128)}, u32[]{:S(2)}) copy-start(f32[3,3,128]{2,1,0:T(4,128)} %refs_5_) | copy-start | bytes 13828
  50.8 18.9 %copy-start.8 = (s32[16]{0:T(128)S(1)}, s32[16]{0:T(128)}, u32[]{:S(2)}) copy-start(s32[16]{0:T(128)} %refs_0_) | copy-start | bytes 196
  52.4 1.4 %collective-permute-start.14 = (f32[288,128]{1,0:T(8,128)S(1)}, f32[288,128]{1,0:T(8,128)S(1)}, u32[]{:S(2)}, u32[]{:S(2)}) collective-permute-start(f32[288,128]{1,0:T(8,128)S(1)} %get-tuple-element.60), channel_id=1, source_target_pairs={{0,1},{1,0},{2,3},{3,2},{4,5},{5,4},{6,7},{7,6},{8,9},{9,8},{10,11... | collective-permute-start | bytes 442376 | tf_op jit(solution)/shard_map/ppermute | solution.py:30
  52.9 1.4 %collective-permute-start.15 = (f32[288,128]{1,0:T(8,128)S(1)}, f32[288,128]{1,0:T(8,128)S(1)}, u32[]{:S(2)}, u32[]{:S(2)}) collective-permute-start(f32[288,128]{1,0:T(8,128)S(1)} %get-tuple-element.61), channel_id=1, source_target_pairs={{0,1},{1,0},{2,3},{3,2},{4,5},{5,4},{6,7},{7,6},{8,9},{9,8},{10,11... | collective-permute-start | bytes 442376 | tf_op jit(solution)/shard_map/ppermute | solution.py:30
  53.0 1.4 %collective-permute-start.16 = (f32[288,128]{1,0:T(8,128)S(1)}, f32[288,128]{1,0:T(8,128)S(1)}, u32[]{:S(2)}, u32[]{:S(2)}) collective-permute-start(f32[288,128]{1,0:T(8,128)S(1)} %get-tuple-element.62), channel_id=1, source_target_pairs={{0,1},{1,0},{2,3},{3,2},{4,5},{5,4},{6,7},{7,6},{8,9},{9,8},{10,11... | collective-permute-start | bytes 442376 | tf_op jit(solution)/shard_map/ppermute | solution.py:30
  62.3 3.4 %collective-permute-start.17 = (f32[168,128]{1,0:T(8,128)S(1)}, f32[168,128]{1,0:T(8,128)S(1)}, u32[]{:S(2)}, u32[]{:S(2)}) collective-permute-start(f32[168,128]{1,0:T(8,128)S(1)} %get-tuple-element.64), channel_id=1, source_target_pairs={{0,2},{2,0},{4,6},{6,4},{8,10},{10,8},{12,14},{14,12},{1,3},{3,1},... | collective-permute-start | bytes 258056 | tf_op jit(solution)/shard_map/ppermute | solution.py:26
  63.6 6.1 %collective-permute-start.18 = (f32[168,128]{1,0:T(8,128)S(1)}, f32[168,128]{1,0:T(8,128)S(1)}, u32[]{:S(2)}, u32[]{:S(2)}) collective-permute-start(f32[168,128]{1,0:T(8,128)S(1)} %get-tuple-element.65), channel_id=1, source_target_pairs={{2,4},{4,2},{6,8},{8,6},{10,12},{12,10},{3,5},{5,3},{7,9},{9,7},{1... | collective-permute-start | bytes 258056 | tf_op jit(solution)/shard_map/ppermute | solution.py:26

commit v6 on v5

--- a/solution.py
+++ b/solution.py
@@ -103,23 +103,25 @@
     )(tokens, alternates)
 
 
-def dots(tokens, panel, give, keep):
-    kinds, _, lanes = keep.shape
-    size = kinds * lanes
-    for begin, out in ((size, give), (0, keep)):
-        result = lax.dot_general(
-            tokens[...],
-            panel[begin : begin + size],
-            (((1,), (1,)), ((), ())),
-            preferred_element_type=jnp.float32,
-        )
-        for kind in range(kinds):
-            out_part = out[kind] if isinstance(out, tuple) else out.at[kind]
-            out_part[...] = result[:, kind * lanes : (kind + 1) * lanes]
+def dots(tokens, panel, side, outs):
+    lanes = outs[0].shape[1]
+    size = len(outs) * lanes
+    result = lax.dot_general(
+        tokens[...],
+        panel[side * size : (side + 1) * size],
+        (((1,), (1,)), ((), ())),
+        preferred_element_type=jnp.float32,
+    )
+    for kind, out in enumerate(outs):
+        out[...] = result[:, kind * lanes : (kind + 1) * lanes]
+
+
+def kinds_of(out):
+    return [out.at[kind] for kind in range(out.shape[0])]
 
 
 def theirs_kernel(theirs, *refs):
-    blocks, (give, keep, panel) = refs[:-3], refs[-3:]
+    blocks, (give, panel) = refs[:-2], refs[-2:]
     kinds, _, lanes = give.shape
     quarter = lanes // 4
     seq = lax.axis_index("seq")
@@ -133,7 +135,11 @@
         for kind in range(kinds):
             panel[pl.ds(pl.multiple_of(side + kind * lanes + at, 16), height), :] = block[kind]
         done += height
-    dots(theirs, panel, give, keep)
+    dots(theirs, panel, 1, kinds_of(give))
+
+
+def keep_kernel(theirs, panel, keep):
+    dots(theirs, panel, 0, kinds_of(keep))
 
 
 def ours_kernel(tokens, alternates, panel, give_query, give_key, give_value, keep, ours, sems):
@@ -144,7 +150,8 @@
     )
     for copy in copies:
         copy.wait()
-    dots(ours, panel, (give_query, give_key, give_value), keep)
+    dots(ours, panel, 1, (give_query, give_key, give_value))
+    dots(ours, panel, 0, kinds_of(keep))
 
 
 def products(tokens, alternates, theirs, blocks):
@@ -158,15 +165,24 @@
         bytes_accessed=2 * width * (count + 2 * kinds * lanes) + 8 * kinds * count * lanes,
         transcendentals=0,
     )
-    give_other, keep_other, panel = pl.pallas_call(
+    give_other, panel = pl.pallas_call(
         theirs_kernel,
-        out_shape=[half, half, jax.ShapeDtypeStruct((2 * kinds * lanes, width), theirs.dtype)],
+        out_shape=[half, jax.ShapeDtypeStruct((2 * kinds * lanes, width), theirs.dtype)],
         in_specs=[VMEM] * (1 + len(blocks)),
-        out_specs=[VMEM] * 3,
+        out_specs=[VMEM] * 2,
         compiler_params=params,
         cost_estimate=cost,
         name="theirs",
     )(theirs, *blocks)
+    keep_other = pl.pallas_call(
+        keep_kernel,
+        out_shape=half,
+        in_specs=[VMEM] * 2,
+        out_specs=VMEM,
+        compiler_params=params,
+        cost_estimate=cost,
+        name="keep",
+    )(theirs, panel)
     *give_mine, keep_mine = pl.pallas_call(
         ours_kernel,
         out_shape=[jax.ShapeDtypeStruct((count, lanes), jnp.float32)] * kinds + [half],
@@ -273,7 +289,7 @@
 
 def mixer_kernel(
     rows, span, picks, feature, within, across, grad, taps, high, low, later_high, later_low,
-    out, effects, before, after, query, key, value, product, back_filtered, filtered,
+    out, before, after, query, key, value, product, back_filtered, filtered,
     back_product, grads, summed,
 ):
     lanes = grad.shape[1]
@@ -351,9 +367,7 @@
         precision=lax.Precision.HIGHEST,
         preferred_element_type=jnp.float32,
     )
-    scores = scores * D ** (-0.5)
-    out[...] = scores[0, :rows]
-    effects[...] = scores[0, rows:]
+    out[...] = scores * D ** (-0.5)
 
 
 def mixer(picks, feature, within, across, grad, taps, span, weights):
@@ -367,12 +381,9 @@
     length = (steps - 1) * BAND + 2 * span
     return pl.pallas_call(
         body,
-        out_shape=[
-            jax.ShapeDtypeStruct((rows,), jnp.float32),
-            jax.ShapeDtypeStruct((count - rows,), jnp.float32),
-        ],
+        out_shape=jax.ShapeDtypeStruct((8, count), jnp.float32),
         in_specs=[SMEM] + [VMEM] * 9,
-        out_specs=[VMEM, VMEM],
+        out_specs=VMEM,
         scratch_shapes=[pltpu.VMEM((span + 5 * EDGE, lanes), jnp.float32)] * 2
         + [pltpu.VMEM((rows + 2 * EDGE, lanes), jnp.float32)] * 3
         + [
@@ -386,6 +397,25 @@
         compiler_params=pltpu.CompilerParams(vmem_limit_bytes=12 << 20),
         name="mixer",
     )(picks, feature, within, across, grad, taps, *weights)
+
+
+def total_kernel(mine, other, out, effects):
+    rows = out.shape[0]
+    scores = mine[:1] + other[:1]
+    out[...] = scores[0, :rows]
+    effects[...] = scores[0, rows:]
+
+
+def total(mine, other, rows):
+    sizes = (rows, mine.shape[1] - rows)
+    return pl.pallas_call(
+        total_kernel,
+        out_shape=[jax.ShapeDtypeStruct((size,), jnp.float32) for size in sizes],
+        in_specs=[VMEM] * 2,
+        out_specs=[VMEM] * 2,
+        compiler_params=pltpu.CompilerParams(vmem_limit_bytes=1 << 20),
+        name="total",
+    )(mine, other)
 
 
 def gathered_features(tokens, proj, lanes):
@@ -450,7 +480,7 @@
     feature, within, across = edges(grad_out, short_taps, span, terms)
     within, across = paired(within, "seq", 0), paired(across, "seq", 1)
     scores = mixer(picks, feature, within, across, grad_out, short_taps, span, weights)
-    return tuple(lax.psum(tuple(scores), "grp"))
+    return tuple(total(scores, crossed(scores, "grp", 1), grad_out.shape[0]))
 
 
 def solution(mesh):

time: 77.7 us -> 75.8 us (0.976)
  blocking collectives: 5.34 us -> 0 us
  starting transfers between devices: 19.8 us -> 22.4 us
    psum x1 -> x0, blocking collectives: 5.34 us -> none  [per_device(): return tuple(lax.psum(tuple(scores), 'grp'))]
    ppermute x17 -> x18, starting transfers between devices: 16.6 us -> 19.2 us  [crossed(): lax.ppermute(block, axis, [(i, i ^ bit) for i in range(lax.axis_size(axis...]
    pallas_call x2 -> x4, Pallas kernels: 4.07 us -> 4.84 us  [the longest x1 2.46 us: mixer(): pl.pallas_call(body, out_shape=jax.ShapeDtypeStruct((8, count), jnp.float...]
    ppermute x17 -> x18, waiting for transfers between devices: 36.9 us -> 37 us  [crossed(): lax.ppermute(block, axis, [(i, i ^ bit) for i in range(lax.axis_size(axis...]
  transfers between devices with their start and end apart: 19 -> 20, of which waited for: 15 -> 16; matrix products, arithmetic and copies ran while one was open for 0% -> 0% of each run, Pallas kernels for 3% -> 4%
where the time goes in v6:
time: 75.8 us; the launch traced here: 75.6 us
  waiting for transfers between devices  41.2 us (54%)
  starting transfers between devices  22.4 us (30%)
  Pallas kernels  7.51 us (10%)
  local copies, waits for them, and re-layouts  3.72 us (5%)
    ppermute x18, waiting for transfers between devices, crossed(): lax.ppermute(block, axis, [(i, i ^ bit) for i in range(lax.axis_size(axis...  37 us
    ppermute x18, starting transfers between devices, crossed(): lax.ppermute(block, axis, [(i, i ^ bit) for i in range(lax.axis_size(axis...  19.2 us
    ppermute x2, waiting for transfers between devices, paired(): return lax.ppermute(block, axis, route)  4.2 us
    unnamed x18, local copies, waits for them, and re-layouts  3.72 us
    ppermute x2, starting transfers between devices, paired(): return lax.ppermute(block, axis, route)  3.18 us
    pallas_call x1, Pallas kernels, mixer(): pl.pallas_call(body, out_shape=jax.ShapeDtypeStruct((8, count), jnp.float...  2.46 us
    pallas_call x1, Pallas kernels, products(): pl.pallas_call(ours_kernel, out_shape=[jax.ShapeDtypeStruct((count, lanes...  1.57 us
  transfers between devices with their start and end apart: 20, of which 16 were waited for; matrix products, arithmetic and copies ran while one was open for 0% of the time, Pallas kernels for 4%

profile of v6, /device:TPU:23, one launch (start us, length us, event | category | flops | bytes accessed | tf_op | source)
XLA Modules:
  0.0 75.6 jit_solution(12488743083755346291)
XLA Ops:
  0.6 0.0 copy-start.2
  0.6 1.1 %copy-done.2 = bf16[3,32,4096]{2,1,0:T(8,128)(2,1)S(1)} copy-done((bf16[3,32,4096]{2,1,0:T(8,128)(2,1)S(1)}, bf16[3,32,4096]{2,1,0:T(8,128)(2,1)}, u32[]{:S(2)}) %copy-start.2) | copy-done | bytes 786456
  1.8 0.0 copy-start.7
  1.8 0.1 panels.1
  1.9 0.3 collective-permute-start.1
  2.2 1.3 %collective-permute-start = (bf16[3,32,2048]{2,1,0:T(8,128)(2,1)S(1)}, bf16[3,32,2048]{2,1,0:T(8,128)(2,1)S(1)}, u32[]{:S(2)}, u32[]{:S(2)}) collective-permute-start(bf16[3,32,2048]{2,1,0:T(8,128)(2,1)S(1)} %get-tuple-element.34.refs_0_), channel_id=1, source_target_pairs={{0,4},{2,6},{4,0},{6,2},{8,12},{10,14},{12,8},{14,10},{1,5},{3,7},... | collective-permute-start | bytes 1179656 | tf_op jit(solution)/shard_map/ppermute | solution.py:30
  3.5 1.6 %copy-done = bf16[272,4096]{1,0:T(8,128)(2,1)S(1)} copy-done((bf16[272,4096]{1,0:T(8,128)(2,1)S(1)}, bf16[272,4096]{1,0:T(8,128)(2,1)}, u32[]{:S(2)}) %copy-start) | copy-done | bytes 2228248
  5.2 0.9 %copy-done.3 = bf16[16,4096]{1,0:T(8,128)(2,1)S(1)} copy-done((bf16[16,4096]{1,0:T(8,128)(2,1)S(1)}, bf16[16,4096]{1,0:T(8,128)(2,1)}, u32[]{:S(2)}) %copy-start.3) | copy-done | bytes 131096
  6.1 0.1 columns.1
  6.2 0.3 collective-permute-start.5
  6.5 0.1 collective-permute-start.2
  6.5 9.5 %collective-permute-done.2.refs_4_ = bf16[3,16,2048]{2,1,0:T(8,128)(2,1)S(1)} collective-permute-done((bf16[3,16,2048]{2,1,0:T(8,128)(2,1)S(1)}, bf16[3,16,2048]{2,1,0:T(8,128)(2,1)S(1)}, u32[]{:S(2)}, u32[]{:S(2)}) %collective-permute-start.2) | collective-permute-done | bytes 196640 | tf_op jit(solution)/shard_map/ppermute | solution.py:30
  16.0 0.0 collective-permute-done.1.refs_1_
  16.0 0.0 collective-permute-done.refs_2_
  16.0 1.2 %collective-permute-start.4 = (bf16[3,32,2048]{2,1,0:T(8,128)(2,1)S(1)}, bf16[3,32,2048]{2,1,0:T(8,128)(2,1)S(1)}, u32[]{:S(2)}, u32[]{:S(2)}) collective-permute-start(bf16[3,32,2048]{2,1,0:T(8,128)(2,1)S(1)} %collective-permute-done.refs_2_), channel_id=1, source_target_pairs={{0,2},{2,0},{4,6},{6,4},{8,10},{10,8},{12,14},{14,12},{1,3},{3,1},... | collective-permute-start | bytes 1179656 | tf_op jit(solution)/shard_map/ppermute | solution.py:30
  17.3 0.1 collective-permute-start.3
  17.4 0.0 copy-done.7
  17.4 0.7 bands.1
  18.1 4.7 %collective-permute-done.3.refs_5_ = bf16[3,16,2048]{2,1,0:T(8,128)(2,1)S(1)} collective-permute-done((bf16[3,16,2048]{2,1,0:T(8,128)(2,1)S(1)}, bf16[3,16,2048]{2,1,0:T(8,128)(2,1)S(1)}, u32[]{:S(2)}, u32[]{:S(2)}) %collective-permute-start.3) | collective-permute-done | bytes 196640 | tf_op jit(solution)/shard_map/ppermute | solution.py:30
  22.8 2.0 %collective-permute-done.4.refs_3_ = bf16[3,32,2048]{2,1,0:T(8,128)(2,1)S(1)} collective-permute-done((bf16[3,32,2048]{2,1,0:T(8,128)(2,1)S(1)}, bf16[3,32,2048]{2,1,0:T(8,128)(2,1)S(1)}, u32[]{:S(2)}, u32[]{:S(2)}) %collective-permute-start.4) | collective-permute-done | bytes 393248 | tf_op jit(solution)/shard_map/ppermute | solution.py:30
  24.7 1.2 %collective-permute-start.8 = (bf16[3,16,2048]{2,1,0:T(8,128)(2,1)S(1)}, bf16[3,16,2048]{2,1,0:T(8,128)(2,1)S(1)}, u32[]{:S(2)}, u32[]{:S(2)}) collective-permute-start(bf16[3,16,2048]{2,1,0:T(8,128)(2,1)S(1)} %collective-permute-done.2.refs_4_), channel_id=1, source_target_pairs={{0,2},{2,0},{4,6},{6,4},{8,10},{10,8},{12,14},{14,12},{1,3},{3,1},... | collective-permute-start | bytes 589832 | tf_op jit(solution)/shard_map/ppermute | solution.py:30
  25.9 4.1 %collective-permute-start.6 = (bf16[3,16,2048]{2,1,0:T(8,128)(2,1)S(1)}, bf16[3,16,2048]{2,1,0:T(8,128)(2,1)S(1)}, u32[]{:S(2)}, u32[]{:S(2)}) collective-permute-start(bf16[3,16,2048]{2,1,0:T(8,128)(2,1)S(1)} %collective-permute-done.2.refs_4_), channel_id=1, source_target_pairs={{0,4},{2,6},{4,0},{6,2},{8,12},{10,14},{12,8},{14,10},{1,5},{3,7},... | collective-permute-start | bytes 589832 | tf_op jit(solution)/shard_map/ppermute | solution.py:30
  30.0 1.2 %collective-permute-start.9 = (bf16[3,16,2048]{2,1,0:T(8,128)(2,1)S(1)}, bf16[3,16,2048]{2,1,0:T(8,128)(2,1)S(1)}, u32[]{:S(2)}, u32[]{:S(2)}) collective-permute-start(bf16[3,16,2048]{2,1,0:T(8,128)(2,1)S(1)} %collective-permute-done.3.refs_5_), channel_id=1, source_target_pairs={{0,2},{2,0},{4,6},{6,4},{8,10},{10,8},{12,14},{14,12},{1,3},{3,1},... | collective-permute-start | bytes 589832 | tf_op jit(solution)/shard_map/ppermute | solution.py:30
  31.2 0.0 collective-permute-start.7
  31.2 0.0 collective-permute-done.8.refs_6_
  31.2 2.6 %collective-permute-done.6.refs_8_ = bf16[3,16,2048]{2,1,0:T(8,128)(2,1)S(1)} collective-permute-done((bf16[3,16,2048]{2,1,0:T(8,128)(2,1)S(1)}, bf16[3,16,2048]{2,1,0:T(8,128)(2,1)S(1)}, u32[]{:S(2)}, u32[]{:S(2)}) %collective-permute-start.6) | collective-permute-done | bytes 196640 | tf_op jit(solution)/shard_map/ppermute | solution.py:30
  33.8 1.2 %collective-permute-done.9.refs_7_ = bf16[3,16,2048]{2,1,0:T(8,128)(2,1)S(1)} collective-permute-done((bf16[3,16,2048]{2,1,0:T(8,128)(2,1)S(1)}, bf16[3,16,2048]{2,1,0:T(8,128)(2,1)S(1)}, u32[]{:S(2)}, u32[]{:S(2)}) %collective-permute-start.9) | collective-permute-done | bytes 196640 | tf_op jit(solution)/shard_map/ppermute | solution.py:30
  35.0 3.2 %collective-permute-done.7.refs_9_ = bf16[3,16,2048]{2,1,0:T(8,128)(2,1)S(1)} collective-permute-done((bf16[3,16,2048]{2,1,0:T(8,128)(2,1)S(1)}, bf16[3,16,2048]{2,1,0:T(8,128)(2,1)S(1)}, u32[]{:S(2)}, u32[]{:S(2)}) %collective-permute-start.7) | collective-permute-done | bytes 196640 | tf_op jit(solution)/shard_map/ppermute | solution.py:30
  38.2 1.1 %collective-permute-start.11 = (bf16[3,16,2048]{2,1,0:T(8,128)(2,1)S(1)}, bf16[3,16,2048]{2,1,0:T(8,128)(2,1)S(1)}, u32[]{:S(2)}, u32[]{:S(2)}) collective-permute-start(bf16[3,16,2048]{2,1,0:T(8,128)(2,1)S(1)} %collective-permute-done.9.refs_7_), channel_id=1, source_target_pairs={{0,4},{2,6},{4,0},{6,2},{8,12},{10,14},{12,8},{14,10},{1,5},{3,7},... | collective-permute-start | bytes 589832 | tf_op jit(solution)/shard_map/ppermute | solution.py:30
  39.2 1.2 %collective-permute-start.10 = (bf16[3,16,2048]{2,1,0:T(8,128)(2,1)S(1)}, bf16[3,16,2048]{2,1,0:T(8,128)(2,1)S(1)}, u32[]{:S(2)}, u32[]{:S(2)}) collective-permute-start(bf16[3,16,2048]{2,1,0:T(8,128)(2,1)S(1)} %collective-permute-done.6.refs_8_), channel_id=1, source_target_pairs={{0,2},{2,0},{4,6},{6,4},{8,10},{10,8},{12,14},{14,12},{1,3},{3,1},... | collective-permute-start | bytes 589832 | tf_op jit(solution)/shard_map/ppermute | solution.py:30
  40.4 0.0 collective-permute-done.5.theirs
  40.4 2.2 %collective-permute-done.11.refs_11_ = bf16[3,16,2048]{2,1,0:T(8,128)(2,1)S(1)} collective-permute-done((bf16[3,16,2048]{2,1,0:T(8,128)(2,1)S(1)}, bf16[3,16,2048]{2,1,0:T(8,128)(2,1)S(1)}, u32[]{:S(2)}, u32[]{:S(2)}) %collective-permute-start.11) | collective-permute-done | bytes 196640 | tf_op jit(solution)/shard_map/ppermute | solution.py:30
  42.7 1.4 %collective-permute-done.10.refs_10_ = bf16[3,16,2048]{2,1,0:T(8,128)(2,1)S(1)} collective-permute-done((bf16[3,16,2048]{2,1,0:T(8,128)(2,1)S(1)}, bf16[3,16,2048]{2,1,0:T(8,128)(2,1)S(1)}, u32[]{:S(2)}, u32[]{:S(2)}) %collective-permute-start.10) | collective-permute-done | bytes 196640 | tf_op jit(solution)/shard_map/ppermute | solution.py:30
  44.1 1.0 %theirs.1 = (f32[3,288,128]{2,1,0:T(8,128)S(1)}, bf16[768,2048]{1,0:T(8,128)(2,1)S(1)}) custom-call(bf16[288,2048]{1,0:T(8,128)(2,1)S(1)} %collective-permute-done.5.theirs, bf16[3,32,2048]{2,1,0:T(8,128)(2,1)S(1)} %get-tuple-element.34.refs_0_, bf16[3,32,2048]{2,1,0:T(8,128)(2,1)S(1)} %collective-permute-done.1.refs_1_, ...), custom_call_target="tpu_custom_call" | custom-call | flops 905969664 | bytes 5210112 | tf_op jit(solution)/shard_map/theirs/pallas_call | solution.py:168
  45.1 3.5 %collective-permute-start.12 = (f32[3,288,128]{2,1,0:T(8,128)S(1)}, f32[3,288,128]{2,1,0:T(8,128)S(1)}, u32[]{:S(2)}, u32[]{:S(2)}) collective-permute-start(f32[3,288,128]{2,1,0:T(8,128)S(1)} %get-tuple-element.55), channel_id=1, source_target_pairs={{0,1},{1,0},{2,3},{3,2},{4,5},{5,4},{6,7},{7,6},{8,9},{9,8},{10,11... | collective-permute-start | bytes 1327112 | tf_op jit(solution)/shard_map/ppermute | solution.py:30
  48.6 0.8 %keep.1 = f32[3,288,128]{2,1,0:T(8,128)S(1)} custom-call(bf16[288,2048]{1,0:T(8,128)(2,1)S(1)} %collective-permute-done.5.theirs, bf16[768,2048]{1,0:T(8,128)(2,1)S(1)} %get-tuple-element.53.panel), custom_call_target="tpu_custom_call" | custom-call | flops 905969664 | bytes 5210112 | tf_op jit(solution)/shard_map/keep/pallas_call | solution.py:177
  49.4 0.6 collective-permute-done.12
  50.0 0.1 add.3
  50.1 0.0 copy-start.5
  50.1 0.0 copy-start.6
  50.1 0.0 copy-start.8
  50.1 0.1 collective-permute-start.13
  50.2 0.0 copy-done.1
  50.2 0.0 copy-done.4
  50.2 1.6 %ours.1 = (f32[288,128]{1,0:T(8,128)S(1)}, f32[288,128]{1,0:T(8,128)S(1)}, f32[288,128]{1,0:T(8,128)S(1)}, f32[3,288,128]{2,1,0:T(8,128)S(1)}) custom-call(bf16[272,4096]{1,0:T(8,128)(2,1)S(1)} %copy-done.1, bf16[16,4096]{1,0:T(8,128)(2,1)S(1)} %copy-done.4, bf16[768,2048]{1,0:T(8,128)(2,1)S(1)} %get-tuple-element.53.panel), custom_call_target="tpu_custom_call" | custom-call | flops 905969664 | bytes 5210112 | tf_op jit(solution)/shard_map/ours/pallas_call | solution.py:186
  51.8 0.4 collective-permute-start.14
  52.2 0.1 collective-permute-start.15
  52.4 0.4 collective-permute-start.16
  52.7 0.5 collective-permute-done.14.refs_2_
  53.2 0.4 collective-permute-done.15.refs_3_
  53.6 0.2 collective-permute-done.16.refs_4_
  53.8 7.7 %collective-permute-done.13.refs_1_ = f32[3,288,128]{2,1,0:T(8,128)S(1)} collective-permute-done((f32[3,288,128]{2,1,0:T(8,128)S(1)}, f32[3,288,128]{2,1,0:T(8,128)S(1)}, u32[]{:S(2)}, u32[]{:S(2)}) %collective-permute-start.13) | collective-permute-done | bytes 442400 | tf_op jit(solution)/shard_map/ppermute | solution.py:30
  61.5 0.0 copy-done.5
  61.5 0.0 copy-done.6
  61.5 0.1 edges.1
  61.7 1.3 %collective-permute-start.17 = (f32[168,128]{1,0:T(8,128)S(1)}, f32[168,128]{1,0:T(8,128)S(1)}, u32[]{:S(2)}, u32[]{:S(2)}) collective-permute-start(f32[168,128]{1,0:T(8,128)S(1)} %get-tuple-element.60), channel_id=1, source_target_pairs={{0,2},{2,0},{4,6},{6,4},{8,10},{10,8},{12,14},{14,12},{1,3},{3,1},... | collective-permute-start | bytes 258056 | tf_op jit(solution)/shard_map/ppermute | solution.py:26
  63.0 1.9 %collective-permute-start.18 = (f32[168,128]{1,0:T(8,128)S(1)}, f32[168,128]{1,0:T(8,128)S(1)}, u32[]{:S(2)}, u32[]{:S(2)}) collective-permute-start(f32[168,128]{1,0:T(8,128)S(1)} %get-tuple-element.61), channel_id=1, source_target_pairs={{2,4},{4,2},{6,8},{8,6},{10,12},{12,10},{3,5},{5,3},{7,9},{9,7},{1... | collective-permute-start | bytes 258056 | tf_op jit(solution)/shard_map/ppermute | solution.py:26
  64.9 0.2 collective-permute-done.17.refs_2_
  65.1 4.0 %collective-permute-done.18.refs_3_ = f32[168,128]{1,0:T(8,128)S(1)} collective-permute-done((f32[168,128]{1,0:T(8,128)S(1)}, f32[168,128]{1,0:T(8,128)S(1)}, u32[]{:S(2)}, u32[]{:S(2)}) %collective-permute-start.18) | collective-permute-done | bytes 86048 | tf_op jit(solution)/shard_map/ppermute | solution.py:26
  69.1 0.0 copy-done.8
  69.1 2.5 %mixer.1.mine = f32[8,288]{1,0:T(8,128)S(1)} custom-call(s32[16]{0:T(128)S(1)} %copy-done.8, f32[3,288,128]{2,1,0:T(8,128)S(1)} %get-tuple-element.59.refs_1_, f32[168,128]{1,0:T(8,128)S(1)} %collective-permute-done.17.refs_2_, f32[168,128]{1,0:T(8,128)S(1)} %collective-permute-done.18.refs_3_, bf16[272,128]{1,0:T(8,128)(2,1)S(1)} %copy-done.5, ...), custom_call_target="tpu_custom_call" | custom-call | tf_op jit(solution)/shard_map/mixer/pallas_call | solution.py:382
  71.5 2.7 %collective-permute-start.19 = (f32[8,288]{1,0:T(8,128)S(1)}, f32[8,288]{1,0:T(8,128)S(1)}, u32[]{:S(2)}, u32[]{:S(2)}) collective-permute-start(f32[8,288]{1,0:T(8,128)S(1)} %mixer.1.mine), channel_id=1, source_target_pairs={{0,1},{1,0},{2,3},{3,2},{4,5},{5,4},{6,7},{7,6},{8,9},{9,8},{10,11... | collective-permute-start | bytes 27656 | tf_op jit(solution)/shard_map/ppermute | solution.py:30
  74.2 0.8 %collective-permute-done.19.other = f32[8,288]{1,0:T(8,128)S(1)} collective-permute-done((f32[8,288]{1,0:T(8,128)S(1)}, f32[8,288]{1,0:T(8,128)S(1)}, u32[]{:S(2)}, u32[]{:S(2)}) %collective-permute-start.19) | collective-permute-done | bytes 9248 | tf_op jit(solution)/shard_map/ppermute | solution.py:30
  75.0 0.6 total.1
  (4 shorter events, 0.0 us)
Async XLA Ops:
  0.6 1.1 %copy-start.2 = (bf16[3,32,4096]{2,1,0:T(8,128)(2,1)S(1)}, bf16[3,32,4096]{2,1,0:T(8,128)(2,1)}, u32[]{:S(2)}) copy-start(bf16[3,32,4096]{2,1,0:T(8,128)(2,1)} %proj.1) | copy-start | bytes 2359300
  1.8 15.6 %copy-start.7 = (f32[8,128]{1,0:T(8,128)S(1)}, f32[8,128]{1,0:T(8,128)}, u32[]{:S(2)}) copy-start(f32[8,128]{1,0:T(8,128)} %filters.1) | copy-start | bytes 12292
  1.9 14.1 %collective-permute-start.1 = (bf16[3,32,2048]{2,1,0:T(8,128)(2,1)S(1)}, bf16[3,32,2048]{2,1,0:T(8,128)(2,1)S(1)}, u32[]{:S(2)}, u32[]{:S(2)}) collective-permute-start(bf16[3,32,2048]{2,1,0:T(8,128)(2,1)S(1)} %get-tuple-element.34.refs_0_), channel_id=1, source_target_pairs={{0,2},{2,0},{4,6},{6,4},{8,10},{10,8},{12,14},{14,12},{1,3},{3,1},... | collective-permute-start | bytes 1179656 | tf_op jit(solution)/shard_map/ppermute | solution.py:30
  2.2 13.8 %collective-permute-start = (bf16[3,32,2048]{2,1,0:T(8,128)(2,1)S(1)}, bf16[3,32,2048]{2,1,0:T(8,128)(2,1)S(1)}, u32[]{:S(2)}, u32[]{:S(2)}) collective-permute-start(bf16[3,32,2048]{2,1,0:T(8,128)(2,1)S(1)} %get-tuple-element.34.refs_0_), channel_id=1, source_target_pairs={{0,4},{2,6},{4,0},{6,2},{8,12},{10,14},{12,8},{14,10},{1,5},{3,7},... | collective-permute-start | bytes 1179656 | tf_op jit(solution)/shard_map/ppermute | solution.py:30
  3.5 1.6 %copy-start = (bf16[272,4096]{1,0:T(8,128)(2,1)S(1)}, bf16[272,4096]{1,0:T(8,128)(2,1)}, u32[]{:S(2)}) copy-start(bf16[272,4096]{1,0:T(8,128)(2,1)} %tokens.3) | copy-start | bytes 6684676
  5.2 0.9 %copy-start.3 = (bf16[16,4096]{1,0:T(8,128)(2,1)S(1)}, bf16[16,4096]{1,0:T(8,128)(2,1)}, u32[]{:S(2)}) copy-start(bf16[16,4096]{1,0:T(8,128)(2,1)} %alternates.3) | copy-start | bytes 393220
  6.2 34.2 %collective-permute-start.5 = (bf16[288,2048]{1,0:T(8,128)(2,1)S(1)}, bf16[288,2048]{1,0:T(8,128)(2,1)S(1)}, u32[]{:S(2)}, u32[]{:S(2)}) collective-permute-start(bf16[288,2048]{1,0:T(8,128)(2,1)S(1)} %columns.1), channel_id=1, source_target_pairs={{0,16},{16,0},{1,17},{17,1},{2,18},{18,2},{3,19},{19,3},{4,20},{20... | collective-permute-start | bytes 3538952 | tf_op jit(solution)/shard_map/ppermute | solution.py:30
  6.5 9.5 %collective-permute-start.2 = (bf16[3,16,2048]{2,1,0:T(8,128)(2,1)S(1)}, bf16[3,16,2048]{2,1,0:T(8,128)(2,1)S(1)}, u32[]{:S(2)}, u32[]{:S(2)}) collective-permute-start(bf16[3,16,2048]{2,1,0:T(8,128)(2,1)S(1)} %get-tuple-element.35), channel_id=1, source_target_pairs={{0,8},{2,10},{4,12},{6,14},{8,0},{10,2},{12,4},{14,6},{1,9},{3,11}... | collective-permute-start | bytes 589832 | tf_op jit(solution)/shard_map/ppermute | solution.py:30
  16.0 8.7 %collective-permute-start.4 = (bf16[3,32,2048]{2,1,0:T(8,128)(2,1)S(1)}, bf16[3,32,2048]{2,1,0:T(8,128)(2,1)S(1)}, u32[]{:S(2)}, u32[]{:S(2)}) collective-permute-start(bf16[3,32,2048]{2,1,0:T(8,128)(2,1)S(1)} %collective-permute-done.refs_2_), channel_id=1, source_target_pairs={{0,2},{2,0},{4,6},{6,4},{8,10},{10,8},{12,14},{14,12},{1,3},{3,1},... | collective-permute-start | bytes 1179656 | tf_op jit(solution)/shard_map/ppermute | solution.py:30
  17.3 5.5 %collective-permute-start.3 = (bf16[3,16,2048]{2,1,0:T(8,128)(2,1)S(1)}, bf16[3,16,2048]{2,1,0:T(8,128)(2,1)S(1)}, u32[]{:S(2)}, u32[]{:S(2)}) collective-permute-start(bf16[3,16,2048]{2,1,0:T(8,128)(2,1)S(1)} %get-tuple-element.37), channel_id=1, source_target_pairs={{0,8},{2,10},{4,12},{6,14},{8,0},{10,2},{12,4},{14,6},{1,9},{3,11}... | collective-permute-start | bytes 589832 | tf_op jit(solution)/shard_map/ppermute | solution.py:30
  24.7 6.5 %collective-permute-start.8 = (bf16[3,16,2048]{2,1,0:T(8,128)(2,1)S(1)}, bf16[3,16,2048]{2,1,0:T(8,128)(2,1)S(1)}, u32[]{:S(2)}, u32[]{:S(2)}) collective-permute-start(bf16[3,16,2048]{2,1,0:T(8,128)(2,1)S(1)} %collective-permute-done.2.refs_4_), channel_id=1, source_target_pairs={{0,2},{2,0},{4,6},{6,4},{8,10},{10,8},{12,14},{14,12},{1,3},{3,1},... | collective-permute-start | bytes 589832 | tf_op jit(solution)/shard_map/ppermute | solution.py:30
  25.9 7.9 %collective-permute-start.6 = (bf16[3,16,2048]{2,1,0:T(8,128)(2,1)S(1)}, bf16[3,16,2048]{2,1,0:T(8,128)(2,1)S(1)}, u32[]{:S(2)}, u32[]{:S(2)}) collective-permute-start(bf16[3,16,2048]{2,1,0:T(8,128)(2,1)S(1)} %collective-permute-done.2.refs_4_), channel_id=1, source_target_pairs={{0,4},{2,6},{4,0},{6,2},{8,12},{10,14},{12,8},{14,10},{1,5},{3,7},... | collective-permute-start | bytes 589832 | tf_op jit(solution)/shard_map/ppermute | solution.py:30
  30.0 5.0 %collective-permute-start.9 = (bf16[3,16,2048]{2,1,0:T(8,128)(2,1)S(1)}, bf16[3,16,2048]{2,1,0:T(8,128)(2,1)S(1)}, u32[]{:S(2)}, u32[]{:S(2)}) collective-permute-start(bf16[3,16,2048]{2,1,0:T(8,128)(2,1)S(1)} %collective-permute-done.3.refs_5_), channel_id=1, source_target_pairs={{0,2},{2,0},{4,6},{6,4},{8,10},{10,8},{12,14},{14,12},{1,3},{3,1},... | collective-permute-start | bytes 589832 | tf_op jit(solution)/shard_map/ppermute | solution.py:30
  31.2 6.9 %collective-permute-start.7 = (bf16[3,16,2048]{2,1,0:T(8,128)(2,1)S(1)}, bf16[3,16,2048]{2,1,0:T(8,128)(2,1)S(1)}, u32[]{:S(2)}, u32[]{:S(2)}) collective-permute-start(bf16[3,16,2048]{2,1,0:T(8,128)(2,1)S(1)} %collective-permute-done.3.refs_5_), channel_id=1, source_target_pairs={{0,4},{2,6},{4,0},{6,2},{8,12},{10,14},{12,8},{14,10},{1,5},{3,7},... | collective-permute-start | bytes 589832 | tf_op jit(solution)/shard_map/ppermute | solution.py:30
  38.2 4.5 %collective-permute-start.11 = (bf16[3,16,2048]{2,1,0:T(8,128)(2,1)S(1)}, bf16[3,16,2048]{2,1,0:T(8,128)(2,1)S(1)}, u32[]{:S(2)}, u32[]{:S(2)}) collective-permute-start(bf16[3,16,2048]{2,1,0:T(8,128)(2,1)S(1)} %collective-permute-done.9.refs_7_), channel_id=1, source_target_pairs={{0,4},{2,6},{4,0},{6,2},{8,12},{10,14},{12,8},{14,10},{1,5},{3,7},... | collective-permute-start | bytes 589832 | tf_op jit(solution)/shard_map/ppermute | solution.py:30
  39.2 4.8 %collective-permute-start.10 = (bf16[3,16,2048]{2,1,0:T(8,128)(2,1)S(1)}, bf16[3,16,2048]{2,1,0:T(8,128)(2,1)S(1)}, u32[]{:S(2)}, u32[]{:S(2)}) collective-permute-start(bf16[3,16,2048]{2,1,0:T(8,128)(2,1)S(1)} %collective-permute-done.6.refs_8_), channel_id=1, source_target_pairs={{0,2},{2,0},{4,6},{6,4},{8,10},{10,8},{12,14},{14,12},{1,3},{3,1},... | collective-permute-start | bytes 589832 | tf_op jit(solution)/shard_map/ppermute | solution.py:30
  45.1 4.9 %collective-permute-start.12 = (f32[3,288,128]{2,1,0:T(8,128)S(1)}, f32[3,288,128]{2,1,0:T(8,128)S(1)}, u32[]{:S(2)}, u32[]{:S(2)}) collective-permute-start(f32[3,288,128]{2,1,0:T(8,128)S(1)} %get-tuple-element.55), channel_id=1, source_target_pairs={{0,1},{1,0},{2,3},{3,2},{4,5},{5,4},{6,7},{7,6},{8,9},{9,8},{10,11... | collective-permute-start | bytes 1327112 | tf_op jit(solution)/shard_map/ppermute | solution.py:30
  48.6 1.6 %copy-start.1 = (bf16[272,4096]{1,0:T(8,128)(2,1)S(1)}, bf16[272,4096]{1,0:T(8,128)(2,1)}, u32[]{:S(2)}) copy-start(bf16[272,4096]{1,0:T(8,128)(2,1)} %tokens.3) | copy-start | bytes 6684676
  48.6 1.6 %copy-start.4 = (bf16[16,4096]{1,0:T(8,128)(2,1)S(1)}, bf16[16,4096]{1,0:T(8,128)(2,1)}, u32[]{:S(2)}) copy-start(bf16[16,4096]{1,0:T(8,128)(2,1)} %alternates.3) | copy-start | bytes 393220
  50.1 11.5 %copy-start.5 = (bf16[272,128]{1,0:T(8,128)(2,1)S(1)}, bf16[272,128]{1,0:T(8,128)(2,1)}, u32[]{:S(2)}) copy-start(bf16[272,128]{1,0:T(8,128)(2,1)} %refs_4_.1) | copy-start | bytes 208900
  50.1 11.5 %copy-start.6 = (f32[3,3,128]{2,1,0:T(4,128)S(1)}, f32[3,3,128]{2,1,0:T(4,128)}, u32[]{:S(2)}) copy-start(f32[3,3,128]{2,1,0:T(4,128)} %refs_5_) | copy-start | bytes 13828
  50.1 19.0 %copy-start.8 = (s32[16]{0:T(128)S(1)}, s32[16]{0:T(128)}, u32[]{:S(2)}) copy-start(s32[16]{0:T(128)} %refs_0_) | copy-start | bytes 196
  50.1 11.4 %collective-permute-start.13 = (f32[3,288,128]{2,1,0:T(8,128)S(1)}, f32[3,288,128]{2,1,0:T(8,128)S(1)}, u32[]{:S(2)}, u32[]{:S(2)}) collective-permute-start(f32[3,288,128]{2,1,0:T(8,128)S(1)} %add.3), channel_id=1, source_target_pairs={{0,16},{16,0},{1,17},{17,1},{2,18},{18,2},{3,19},{19,3},{4,20},{20... | collective-permute-start | bytes 1327112 | tf_op jit(solution)/shard_map/ppermute | solution.py:30
  51.8 1.4 %collective-permute-start.14 = (f32[288,128]{1,0:T(8,128)S(1)}, f32[288,128]{1,0:T(8,128)S(1)}, u32[]{:S(2)}, u32[]{:S(2)}) collective-permute-start(f32[288,128]{1,0:T(8,128)S(1)} %get-tuple-element.56), channel_id=1, source_target_pairs={{0,1},{1,0},{2,3},{3,2},{4,5},{5,4},{6,7},{7,6},{8,9},{9,8},{10,11... | collective-permute-start | bytes 442376 | tf_op jit(solution)/shard_map/ppermute | solution.py:30
  52.2 1.4 %collective-permute-start.15 = (f32[288,128]{1,0:T(8,128)S(1)}, f32[288,128]{1,0:T(8,128)S(1)}, u32[]{:S(2)}, u32[]{:S(2)}) collective-permute-start(f32[288,128]{1,0:T(8,128)S(1)} %get-tuple-element.57), channel_id=1, source_target_pairs={{0,1},{1,0},{2,3},{3,2},{4,5},{5,4},{6,7},{7,6},{8,9},{9,8},{10,11... | collective-permute-start | bytes 442376 | tf_op jit(solution)/shard_map/ppermute | solution.py:30
  52.4 1.4 %collective-permute-start.16 = (f32[288,128]{1,0:T(8,128)S(1)}, f32[288,128]{1,0:T(8,128)S(1)}, u32[]{:S(2)}, u32[]{:S(2)}) collective-permute-start(f32[288,128]{1,0:T(8,128)S(1)} %get-tuple-element.58), channel_id=1, source_target_pairs={{0,1},{1,0},{2,3},{3,2},{4,5},{5,4},{6,7},{7,6},{8,9},{9,8},{10,11... | collective-permute-start | bytes 442376 | tf_op jit(solution)/shard_map/ppermute | solution.py:30
  61.7 3.4 %collective-permute-start.17 = (f32[168,128]{1,0:T(8,128)S(1)}, f32[168,128]{1,0:T(8,128)S(1)}, u32[]{:S(2)}, u32[]{:S(2)}) collective-permute-start(f32[168,128]{1,0:T(8,128)S(1)} %get-tuple-element.60), channel_id=1, source_target_pairs={{0,2},{2,0},{4,6},{6,4},{8,10},{10,8},{12,14},{14,12},{1,3},{3,1},... | collective-permute-start | bytes 258056 | tf_op jit(solution)/shard_map/ppermute | solution.py:26
  63.0 6.1 %collective-permute-start.18 = (f32[168,128]{1,0:T(8,128)S(1)}, f32[168,128]{1,0:T(8,128)S(1)}, u32[]{:S(2)}, u32[]{:S(2)}) collective-permute-start(f32[168,128]{1,0:T(8,128)S(1)} %get-tuple-element.61), channel_id=1, source_target_pairs={{2,4},{4,2},{6,8},{8,6},{10,12},{12,10},{3,5},{5,3},{7,9},{9,7},{1... | collective-permute-start | bytes 258056 | tf_op jit(solution)/shard_map/ppermute | solution.py:26
  71.5 3.5 %collective-permute-start.19 = (f32[8,288]{1,0:T(8,128)S(1)}, f32[8,288]{1,0:T(8,128)S(1)}, u32[]{:S(2)}, u32[]{:S(2)}) collective-permute-start(f32[8,288]{1,0:T(8,128)S(1)} %mixer.1.mine), channel_id=1, source_target_pairs={{0,1},{1,0},{2,3},{3,2},{4,5},{5,4},{6,7},{7,6},{8,9},{9,8},{10,11... | collective-permute-start | bytes 27656 | tf_op jit(solution)/shard_map/ppermute | solution.py:30

commit v7 on v6

--- a/solution.py
+++ b/solution.py
@@ -120,21 +120,28 @@
     return [out.at[kind] for kind in range(out.shape[0])]
 
 
-def theirs_kernel(theirs, *refs):
-    blocks, (give, panel) = refs[:-2], refs[-2:]
-    kinds, _, lanes = give.shape
+def fill(panel, blocks, lanes, done):
     quarter = lanes // 4
     seq = lax.axis_index("seq")
     swap = lax.axis_index("grp") ^ (seq // 4)
-    done = 0
     for block in blocks:
-        height = block.shape[1]
+        kinds, height, _ = block.shape
         order = done // quarter
         side = ((order // 4) ^ swap) * kinds * lanes
         at = ((seq % 4) ^ (order % 4)) * quarter + done % quarter
         for kind in range(kinds):
             panel[pl.ds(pl.multiple_of(side + kind * lanes + at, 16), height), :] = block[kind]
         done += height
+
+
+def panel_kernel(lanes, *refs):
+    fill(refs[-1], refs[:-1], lanes, 0)
+
+
+def theirs_kernel(theirs, begun, *refs):
+    blocks, (give, panel) = refs[:-2], refs[-2:]
+    lanes = give.shape[2]
+    fill(panel, blocks, lanes, 2 * lanes - sum(block.shape[1] for block in blocks))
     dots(theirs, panel, 1, kinds_of(give))
 
 
@@ -165,15 +172,26 @@
         bytes_accessed=2 * width * (count + 2 * kinds * lanes) + 8 * kinds * count * lanes,
         transcendentals=0,
     )
+    whole = jax.ShapeDtypeStruct((2 * kinds * lanes, width), theirs.dtype)
+    first, last = blocks[:-2], blocks[-2:]
+    begun = pl.pallas_call(
+        functools.partial(panel_kernel, lanes),
+        out_shape=whole,
+        in_specs=[VMEM] * len(first),
+        out_specs=VMEM,
+        compiler_params=params,
+        name="panel",
+    )(*first)
     give_other, panel = pl.pallas_call(
         theirs_kernel,
-        out_shape=[half, jax.ShapeDtypeStruct((2 * kinds * lanes, width), theirs.dtype)],
-        in_specs=[VMEM] * (1 + len(blocks)),
+        out_shape=[half, whole],
+        in_specs=[VMEM] * (2 + len(last)),
         out_specs=[VMEM] * 2,
+        input_output_aliases={1: 1},
         compiler_params=params,
         cost_estimate=cost,
         name="theirs",
-    )(theirs, *blocks)
+    )(theirs, begun, *last)
     keep_other = pl.pallas_call(
         keep_kernel,
         out_shape=half,

time: 75.8 us -> 75.7 us (level)
  no operation moved by 1% of the time
where the time goes in v7:
time: 75.7 us; the launch traced here: 75.4 us
  waiting for transfers between devices  40.9 us (54%)
  starting transfers between devices  22.4 us (30%)
  Pallas kernels  7.53 us (10%)
  local copies, waits for them, and re-layouts  3.73 us (5%)
  between operations  0.76 us (1%)
    ppermute x18, waiting for transfers between devices, crossed(): lax.ppermute(block, axis, [(i, i ^ bit) for i in range(lax.axis_size(axis...  36.7 us
    ppermute x18, starting transfers between devices, crossed(): lax.ppermute(block, axis, [(i, i ^ bit) for i in range(lax.axis_size(axis...  19.2 us
    ppermute x2, waiting for transfers between devices, paired(): return lax.ppermute(block, axis, route)  4.2 us
    unnamed x18, local copies, waits for them, and re-layouts  3.73 us
    ppermute x2, starting transfers between devices, paired(): return lax.ppermute(block, axis, route)  3.19 us
    pallas_call x1, Pallas kernels, mixer(): pl.pallas_call(body, out_shape=jax.ShapeDtypeStruct((8, count), jnp.float...  2.46 us
    pallas_call x1, Pallas kernels, products(): pl.pallas_call(ours_kernel, out_shape=[jax.ShapeDtypeStruct((count, lanes...  1.57 us
  transfers between devices with their start and end apart: 20, of which 16 were waited for; matrix products, arithmetic and copies ran while one was open for 0% of the time, Pallas kernels for 4%

profile of v7, /device:TPU:23, one launch (start us, length us, event | category | flops | bytes accessed | tf_op | source)
XLA Modules:
  0.0 75.4 jit_solution(8204263565387451654)
XLA Ops:
  0.6 0.0 copy-start.2
  0.6 1.1 %copy-done.2 = bf16[3,32,4096]{2,1,0:T(8,128)(2,1)S(1)} copy-done((bf16[3,32,4096]{2,1,0:T(8,128)(2,1)S(1)}, bf16[3,32,4096]{2,1,0:T(8,128)(2,1)}, u32[]{:S(2)}) %copy-start.2) | copy-done | bytes 786456
  1.8 0.0 copy-start.7
  1.8 0.1 panels.1
  1.9 0.3 collective-permute-start.1
  2.2 1.3 %collective-permute-start = (bf16[3,32,2048]{2,1,0:T(8,128)(2,1)S(1)}, bf16[3,32,2048]{2,1,0:T(8,128)(2,1)S(1)}, u32[]{:S(2)}, u32[]{:S(2)}) collective-permute-start(bf16[3,32,2048]{2,1,0:T(8,128)(2,1)S(1)} %get-tuple-element.34.refs_0_), channel_id=1, source_target_pairs={{0,4},{2,6},{4,0},{6,2},{8,12},{10,14},{12,8},{14,10},{1,5},{3,7},... | collective-permute-start | bytes 1179656 | tf_op jit(solution)/shard_map/ppermute | solution.py:30
  3.5 1.6 %copy-done = bf16[272,4096]{1,0:T(8,128)(2,1)S(1)} copy-done((bf16[272,4096]{1,0:T(8,128)(2,1)S(1)}, bf16[272,4096]{1,0:T(8,128)(2,1)}, u32[]{:S(2)}) %copy-start) | copy-done | bytes 2228248
  5.2 0.9 %copy-done.3 = bf16[16,4096]{1,0:T(8,128)(2,1)S(1)} copy-done((bf16[16,4096]{1,0:T(8,128)(2,1)S(1)}, bf16[16,4096]{1,0:T(8,128)(2,1)}, u32[]{:S(2)}) %copy-start.3) | copy-done | bytes 131096
  6.1 0.1 columns.1
  6.2 0.3 collective-permute-start.5
  6.5 0.1 collective-permute-start.2
  6.5 9.5 %collective-permute-done.2.refs_4_ = bf16[3,16,2048]{2,1,0:T(8,128)(2,1)S(1)} collective-permute-done((bf16[3,16,2048]{2,1,0:T(8,128)(2,1)S(1)}, bf16[3,16,2048]{2,1,0:T(8,128)(2,1)S(1)}, u32[]{:S(2)}, u32[]{:S(2)}) %collective-permute-start.2) | collective-permute-done | bytes 196640 | tf_op jit(solution)/shard_map/ppermute | solution.py:30
  16.0 0.0 collective-permute-done.1.refs_1_
  16.0 0.0 collective-permute-done.refs_2_
  16.0 1.2 %collective-permute-start.4 = (bf16[3,32,2048]{2,1,0:T(8,128)(2,1)S(1)}, bf16[3,32,2048]{2,1,0:T(8,128)(2,1)S(1)}, u32[]{:S(2)}, u32[]{:S(2)}) collective-permute-start(bf16[3,32,2048]{2,1,0:T(8,128)(2,1)S(1)} %collective-permute-done.refs_2_), channel_id=1, source_target_pairs={{0,2},{2,0},{4,6},{6,4},{8,10},{10,8},{12,14},{14,12},{1,3},{3,1},... | collective-permute-start | bytes 1179656 | tf_op jit(solution)/shard_map/ppermute | solution.py:30
  17.3 0.1 collective-permute-start.3
  17.4 0.0 copy-done.7
  17.4 0.7 bands.1
  18.1 4.7 %collective-permute-done.3.refs_5_ = bf16[3,16,2048]{2,1,0:T(8,128)(2,1)S(1)} collective-permute-done((bf16[3,16,2048]{2,1,0:T(8,128)(2,1)S(1)}, bf16[3,16,2048]{2,1,0:T(8,128)(2,1)S(1)}, u32[]{:S(2)}, u32[]{:S(2)}) %collective-permute-start.3) | collective-permute-done | bytes 196640 | tf_op jit(solution)/shard_map/ppermute | solution.py:30
  22.8 2.0 %collective-permute-done.4.refs_3_ = bf16[3,32,2048]{2,1,0:T(8,128)(2,1)S(1)} collective-permute-done((bf16[3,32,2048]{2,1,0:T(8,128)(2,1)S(1)}, bf16[3,32,2048]{2,1,0:T(8,128)(2,1)S(1)}, u32[]{:S(2)}, u32[]{:S(2)}) %collective-permute-start.4) | collective-permute-done | bytes 393248 | tf_op jit(solution)/shard_map/ppermute | solution.py:30
  24.7 1.2 %collective-permute-start.8 = (bf16[3,16,2048]{2,1,0:T(8,128)(2,1)S(1)}, bf16[3,16,2048]{2,1,0:T(8,128)(2,1)S(1)}, u32[]{:S(2)}, u32[]{:S(2)}) collective-permute-start(bf16[3,16,2048]{2,1,0:T(8,128)(2,1)S(1)} %collective-permute-done.2.refs_4_), channel_id=1, source_target_pairs={{0,2},{2,0},{4,6},{6,4},{8,10},{10,8},{12,14},{14,12},{1,3},{3,1},... | collective-permute-start | bytes 589832 | tf_op jit(solution)/shard_map/ppermute | solution.py:30
  25.9 4.1 %collective-permute-start.6 = (bf16[3,16,2048]{2,1,0:T(8,128)(2,1)S(1)}, bf16[3,16,2048]{2,1,0:T(8,128)(2,1)S(1)}, u32[]{:S(2)}, u32[]{:S(2)}) collective-permute-start(bf16[3,16,2048]{2,1,0:T(8,128)(2,1)S(1)} %collective-permute-done.2.refs_4_), channel_id=1, source_target_pairs={{0,4},{2,6},{4,0},{6,2},{8,12},{10,14},{12,8},{14,10},{1,5},{3,7},... | collective-permute-start | bytes 589832 | tf_op jit(solution)/shard_map/ppermute | solution.py:30
  30.0 1.2 %collective-permute-start.9 = (bf16[3,16,2048]{2,1,0:T(8,128)(2,1)S(1)}, bf16[3,16,2048]{2,1,0:T(8,128)(2,1)S(1)}, u32[]{:S(2)}, u32[]{:S(2)}) collective-permute-start(bf16[3,16,2048]{2,1,0:T(8,128)(2,1)S(1)} %collective-permute-done.3.refs_5_), channel_id=1, source_target_pairs={{0,2},{2,0},{4,6},{6,4},{8,10},{10,8},{12,14},{14,12},{1,3},{3,1},... | collective-permute-start | bytes 589832 | tf_op jit(solution)/shard_map/ppermute | solution.py:30
  31.2 0.0 collective-permute-start.7
  31.2 0.0 collective-permute-done.8.refs_6_
  31.2 2.6 %collective-permute-done.6.refs_8_ = bf16[3,16,2048]{2,1,0:T(8,128)(2,1)S(1)} collective-permute-done((bf16[3,16,2048]{2,1,0:T(8,128)(2,1)S(1)}, bf16[3,16,2048]{2,1,0:T(8,128)(2,1)S(1)}, u32[]{:S(2)}, u32[]{:S(2)}) %collective-permute-start.6) | collective-permute-done | bytes 196640 | tf_op jit(solution)/shard_map/ppermute | solution.py:30
  33.8 1.2 %collective-permute-done.9.refs_7_ = bf16[3,16,2048]{2,1,0:T(8,128)(2,1)S(1)} collective-permute-done((bf16[3,16,2048]{2,1,0:T(8,128)(2,1)S(1)}, bf16[3,16,2048]{2,1,0:T(8,128)(2,1)S(1)}, u32[]{:S(2)}, u32[]{:S(2)}) %collective-permute-start.9) | collective-permute-done | bytes 196640 | tf_op jit(solution)/shard_map/ppermute | solution.py:30
  35.0 3.2 %collective-permute-done.7.refs_9_ = bf16[3,16,2048]{2,1,0:T(8,128)(2,1)S(1)} collective-permute-done((bf16[3,16,2048]{2,1,0:T(8,128)(2,1)S(1)}, bf16[3,16,2048]{2,1,0:T(8,128)(2,1)S(1)}, u32[]{:S(2)}, u32[]{:S(2)}) %collective-permute-start.7) | collective-permute-done | bytes 196640 | tf_op jit(solution)/shard_map/ppermute | solution.py:30
  38.2 1.1 %collective-permute-start.11 = (bf16[3,16,2048]{2,1,0:T(8,128)(2,1)S(1)}, bf16[3,16,2048]{2,1,0:T(8,128)(2,1)S(1)}, u32[]{:S(2)}, u32[]{:S(2)}) collective-permute-start(bf16[3,16,2048]{2,1,0:T(8,128)(2,1)S(1)} %collective-permute-done.9.refs_7_), channel_id=1, source_target_pairs={{0,4},{2,6},{4,0},{6,2},{8,12},{10,14},{12,8},{14,10},{1,5},{3,7},... | collective-permute-start | bytes 589832 | tf_op jit(solution)/shard_map/ppermute | solution.py:30
  39.2 1.2 %collective-permute-start.10 = (bf16[3,16,2048]{2,1,0:T(8,128)(2,1)S(1)}, bf16[3,16,2048]{2,1,0:T(8,128)(2,1)S(1)}, u32[]{:S(2)}, u32[]{:S(2)}) collective-permute-start(bf16[3,16,2048]{2,1,0:T(8,128)(2,1)S(1)} %collective-permute-done.6.refs_8_), channel_id=1, source_target_pairs={{0,2},{2,0},{4,6},{6,4},{8,10},{10,8},{12,14},{14,12},{1,3},{3,1},... | collective-permute-start | bytes 589832 | tf_op jit(solution)/shard_map/ppermute | solution.py:30
  40.4 0.2 panel.1.begun
  40.6 0.0 collective-permute-done.5.theirs
  40.6 2.0 %collective-permute-done.11.refs_1_ = bf16[3,16,2048]{2,1,0:T(8,128)(2,1)S(1)} collective-permute-done((bf16[3,16,2048]{2,1,0:T(8,128)(2,1)S(1)}, bf16[3,16,2048]{2,1,0:T(8,128)(2,1)S(1)}, u32[]{:S(2)}, u32[]{:S(2)}) %collective-permute-start.11) | collective-permute-done | bytes 196640 | tf_op jit(solution)/shard_map/ppermute | solution.py:30
  42.7 1.4 %collective-permute-done.10.refs_0_ = bf16[3,16,2048]{2,1,0:T(8,128)(2,1)S(1)} collective-permute-done((bf16[3,16,2048]{2,1,0:T(8,128)(2,1)S(1)}, bf16[3,16,2048]{2,1,0:T(8,128)(2,1)S(1)}, u32[]{:S(2)}, u32[]{:S(2)}) %collective-permute-start.10) | collective-permute-done | bytes 196640 | tf_op jit(solution)/shard_map/ppermute | solution.py:30
  44.1 0.8 %theirs.1 = (f32[3,288,128]{2,1,0:T(8,128)S(1)}, bf16[768,2048]{1,0:T(8,128)(2,1)S(1)}) custom-call(bf16[288,2048]{1,0:T(8,128)(2,1)S(1)} %collective-permute-done.5.theirs, bf16[768,2048]{1,0:T(8,128)(2,1)S(1)} %panel.1.begun, bf16[3,16,2048]{2,1,0:T(8,128)(2,1)S(1)} %collective-permute-done.10.refs_0_, ...), custom_call_target="tpu_custom_call", output_to_operand_aliasing={{1}: (1, {})} | custom-call | flops 905969664 | bytes 5210112 | tf_op jit(solution)/shard_map/theirs/pallas_call | solution.py:185
  44.9 3.5 %collective-permute-start.12 = (f32[3,288,128]{2,1,0:T(8,128)S(1)}, f32[3,288,128]{2,1,0:T(8,128)S(1)}, u32[]{:S(2)}, u32[]{:S(2)}) collective-permute-start(f32[3,288,128]{2,1,0:T(8,128)S(1)} %get-tuple-element.55), channel_id=1, source_target_pairs={{0,1},{1,0},{2,3},{3,2},{4,5},{5,4},{6,7},{7,6},{8,9},{9,8},{10,11... | collective-permute-start | bytes 1327112 | tf_op jit(solution)/shard_map/ppermute | solution.py:30
  48.4 0.8 %keep.1 = f32[3,288,128]{2,1,0:T(8,128)S(1)} custom-call(bf16[288,2048]{1,0:T(8,128)(2,1)S(1)} %collective-permute-done.5.theirs, bf16[768,2048]{1,0:T(8,128)(2,1)S(1)} %get-tuple-element.53.panel), custom_call_target="tpu_custom_call" | custom-call | flops 905969664 | bytes 5210112 | tf_op jit(solution)/shard_map/keep/pallas_call | solution.py:195
  49.2 0.6 collective-permute-done.12
  49.9 0.0 copy-start.5
  49.9 0.0 copy-start.6
  49.9 0.0 copy-start.8
  49.9 0.1 collective-permute-start.13
  50.0 0.0 copy-done.1
  50.0 0.0 copy-done.4
  50.0 1.6 %ours.1 = (f32[288,128]{1,0:T(8,128)S(1)}, f32[288,128]{1,0:T(8,128)S(1)}, f32[288,128]{1,0:T(8,128)S(1)}, f32[3,288,128]{2,1,0:T(8,128)S(1)}) custom-call(bf16[272,4096]{1,0:T(8,128)(2,1)S(1)} %copy-done.1, bf16[16,4096]{1,0:T(8,128)(2,1)S(1)} %copy-done.4, bf16[768,2048]{1,0:T(8,128)(2,1)S(1)} %get-tuple-element.53.panel), custom_call_target="tpu_custom_call" | custom-call | flops 905969664 | bytes 5210112 | tf_op jit(solution)/shard_map/ours/pallas_call | solution.py:204
  51.6 0.4 collective-permute-start.14
  52.0 0.1 collective-permute-start.15
  52.2 0.4 collective-permute-start.16
  52.5 0.5 collective-permute-done.14.refs_2_
  53.0 0.4 collective-permute-done.15.refs_3_
  53.4 0.2 collective-permute-done.16.refs_4_
  53.6 7.7 %collective-permute-done.13.refs_1_ = f32[3,288,128]{2,1,0:T(8,128)S(1)} collective-permute-done((f32[3,288,128]{2,1,0:T(8,128)S(1)}, f32[3,288,128]{2,1,0:T(8,128)S(1)}, u32[]{:S(2)}, u32[]{:S(2)}) %collective-permute-start.13) | collective-permute-done | bytes 442400 | tf_op jit(solution)/shard_map/ppermute | solution.py:30
  61.3 0.0 copy-done.5
  61.3 0.0 copy-done.6
  61.3 0.1 edges.1
  61.5 1.3 %collective-permute-start.17 = (f32[168,128]{1,0:T(8,128)S(1)}, f32[168,128]{1,0:T(8,128)S(1)}, u32[]{:S(2)}, u32[]{:S(2)}) collective-permute-start(f32[168,128]{1,0:T(8,128)S(1)} %get-tuple-element.60), channel_id=1, source_target_pairs={{0,2},{2,0},{4,6},{6,4},{8,10},{10,8},{12,14},{14,12},{1,3},{3,1},... | collective-permute-start | bytes 258056 | tf_op jit(solution)/shard_map/ppermute | solution.py:26
  62.8 1.9 %collective-permute-start.18 = (f32[168,128]{1,0:T(8,128)S(1)}, f32[168,128]{1,0:T(8,128)S(1)}, u32[]{:S(2)}, u32[]{:S(2)}) collective-permute-start(f32[168,128]{1,0:T(8,128)S(1)} %get-tuple-element.61), channel_id=1, source_target_pairs={{2,4},{4,2},{6,8},{8,6},{10,12},{12,10},{3,5},{5,3},{7,9},{9,7},{1... | collective-permute-start | bytes 258056 | tf_op jit(solution)/shard_map/ppermute | solution.py:26
  64.7 0.2 collective-permute-done.17.refs_2_
  64.9 4.0 %collective-permute-done.18.refs_3_ = f32[168,128]{1,0:T(8,128)S(1)} collective-permute-done((f32[168,128]{1,0:T(8,128)S(1)}, f32[168,128]{1,0:T(8,128)S(1)}, u32[]{:S(2)}, u32[]{:S(2)}) %collective-permute-start.18) | collective-permute-done | bytes 86048 | tf_op jit(solution)/shard_map/ppermute | solution.py:26
  68.9 0.0 copy-done.8
  68.9 2.5 %mixer.1.mine = f32[8,288]{1,0:T(8,128)S(1)} custom-call(s32[16]{0:T(128)S(1)} %copy-done.8, f32[3,288,128]{2,1,0:T(8,128)S(1)} %get-tuple-element.59.refs_1_, f32[168,128]{1,0:T(8,128)S(1)} %collective-permute-done.17.refs_2_, f32[168,128]{1,0:T(8,128)S(1)} %collective-permute-done.18.refs_3_, bf16[272,128]{1,0:T(8,128)(2,1)S(1)} %copy-done.5, ...), custom_call_target="tpu_custom_call" | custom-call | tf_op jit(solution)/shard_map/mixer/pallas_call | solution.py:400
  71.3 2.7 %collective-permute-start.19 = (f32[8,288]{1,0:T(8,128)S(1)}, f32[8,288]{1,0:T(8,128)S(1)}, u32[]{:S(2)}, u32[]{:S(2)}) collective-permute-start(f32[8,288]{1,0:T(8,128)S(1)} %mixer.1.mine), channel_id=1, source_target_pairs={{0,1},{1,0},{2,3},{3,2},{4,5},{5,4},{6,7},{7,6},{8,9},{9,8},{10,11... | collective-permute-start | bytes 27656 | tf_op jit(solution)/shard_map/ppermute | solution.py:30
  74.0 0.8 %collective-permute-done.19.other = f32[8,288]{1,0:T(8,128)S(1)} collective-permute-done((f32[8,288]{1,0:T(8,128)S(1)}, f32[8,288]{1,0:T(8,128)S(1)}, u32[]{:S(2)}, u32[]{:S(2)}) %collective-permute-start.19) | collective-permute-done | bytes 9248 | tf_op jit(solution)/shard_map/ppermute | solution.py:30
  74.8 0.6 total.1
  (5 shorter events, 0.1 us)
Async XLA Ops:
  0.6 1.1 %copy-start.2 = (bf16[3,32,4096]{2,1,0:T(8,128)(2,1)S(1)}, bf16[3,32,4096]{2,1,0:T(8,128)(2,1)}, u32[]{:S(2)}) copy-start(bf16[3,32,4096]{2,1,0:T(8,128)(2,1)} %proj.1) | copy-start | bytes 2359300
  1.8 15.6 %copy-start.7 = (f32[8,128]{1,0:T(8,128)S(1)}, f32[8,128]{1,0:T(8,128)}, u32[]{:S(2)}) copy-start(f32[8,128]{1,0:T(8,128)} %filters.1) | copy-start | bytes 12292
  1.9 14.1 %collective-permute-start.1 = (bf16[3,32,2048]{2,1,0:T(8,128)(2,1)S(1)}, bf16[3,32,2048]{2,1,0:T(8,128)(2,1)S(1)}, u32[]{:S(2)}, u32[]{:S(2)}) collective-permute-start(bf16[3,32,2048]{2,1,0:T(8,128)(2,1)S(1)} %get-tuple-element.34.refs_0_), channel_id=1, source_target_pairs={{0,2},{2,0},{4,6},{6,4},{8,10},{10,8},{12,14},{14,12},{1,3},{3,1},... | collective-permute-start | bytes 1179656 | tf_op jit(solution)/shard_map/ppermute | solution.py:30
  2.2 13.8 %collective-permute-start = (bf16[3,32,2048]{2,1,0:T(8,128)(2,1)S(1)}, bf16[3,32,2048]{2,1,0:T(8,128)(2,1)S(1)}, u32[]{:S(2)}, u32[]{:S(2)}) collective-permute-start(bf16[3,32,2048]{2,1,0:T(8,128)(2,1)S(1)} %get-tuple-element.34.refs_0_), channel_id=1, source_target_pairs={{0,4},{2,6},{4,0},{6,2},{8,12},{10,14},{12,8},{14,10},{1,5},{3,7},... | collective-permute-start | bytes 1179656 | tf_op jit(solution)/shard_map/ppermute | solution.py:30
  3.5 1.6 %copy-start = (bf16[272,4096]{1,0:T(8,128)(2,1)S(1)}, bf16[272,4096]{1,0:T(8,128)(2,1)}, u32[]{:S(2)}) copy-start(bf16[272,4096]{1,0:T(8,128)(2,1)} %tokens.3) | copy-start | bytes 6684676
  5.2 0.9 %copy-start.3 = (bf16[16,4096]{1,0:T(8,128)(2,1)S(1)}, bf16[16,4096]{1,0:T(8,128)(2,1)}, u32[]{:S(2)}) copy-start(bf16[16,4096]{1,0:T(8,128)(2,1)} %alternates.3) | copy-start | bytes 393220
  6.2 34.4 %collective-permute-start.5 = (bf16[288,2048]{1,0:T(8,128)(2,1)S(1)}, bf16[288,2048]{1,0:T(8,128)(2,1)S(1)}, u32[]{:S(2)}, u32[]{:S(2)}) collective-permute-start(bf16[288,2048]{1,0:T(8,128)(2,1)S(1)} %columns.1), channel_id=1, source_target_pairs={{0,16},{16,0},{1,17},{17,1},{2,18},{18,2},{3,19},{19,3},{4,20},{20... | collective-permute-start | bytes 3538952 | tf_op jit(solution)/shard_map/ppermute | solution.py:30
  6.5 9.5 %collective-permute-start.2 = (bf16[3,16,2048]{2,1,0:T(8,128)(2,1)S(1)}, bf16[3,16,2048]{2,1,0:T(8,128)(2,1)S(1)}, u32[]{:S(2)}, u32[]{:S(2)}) collective-permute-start(bf16[3,16,2048]{2,1,0:T(8,128)(2,1)S(1)} %get-tuple-element.35), channel_id=1, source_target_pairs={{0,8},{2,10},{4,12},{6,14},{8,0},{10,2},{12,4},{14,6},{1,9},{3,11}... | collective-permute-start | bytes 589832 | tf_op jit(solution)/shard_map/ppermute | solution.py:30
  16.0 8.7 %collective-permute-start.4 = (bf16[3,32,2048]{2,1,0:T(8,128)(2,1)S(1)}, bf16[3,32,2048]{2,1,0:T(8,128)(2,1)S(1)}, u32[]{:S(2)}, u32[]{:S(2)}) collective-permute-start(bf16[3,32,2048]{2,1,0:T(8,128)(2,1)S(1)} %collective-permute-done.refs_2_), channel_id=1, source_target_pairs={{0,2},{2,0},{4,6},{6,4},{8,10},{10,8},{12,14},{14,12},{1,3},{3,1},... | collective-permute-start | bytes 1179656 | tf_op jit(solution)/shard_map/ppermute | solution.py:30
  17.3 5.5 %collective-permute-start.3 = (bf16[3,16,2048]{2,1,0:T(8,128)(2,1)S(1)}, bf16[3,16,2048]{2,1,0:T(8,128)(2,1)S(1)}, u32[]{:S(2)}, u32[]{:S(2)}) collective-permute-start(bf16[3,16,2048]{2,1,0:T(8,128)(2,1)S(1)} %get-tuple-element.37), channel_id=1, source_target_pairs={{0,8},{2,10},{4,12},{6,14},{8,0},{10,2},{12,4},{14,6},{1,9},{3,11}... | collective-permute-start | bytes 589832 | tf_op jit(solution)/shard_map/ppermute | solution.py:30
  24.7 6.5 %collective-permute-start.8 = (bf16[3,16,2048]{2,1,0:T(8,128)(2,1)S(1)}, bf16[3,16,2048]{2,1,0:T(8,128)(2,1)S(1)}, u32[]{:S(2)}, u32[]{:S(2)}) collective-permute-start(bf16[3,16,2048]{2,1,0:T(8,128)(2,1)S(1)} %collective-permute-done.2.refs_4_), channel_id=1, source_target_pairs={{0,2},{2,0},{4,6},{6,4},{8,10},{10,8},{12,14},{14,12},{1,3},{3,1},... | collective-permute-start | bytes 589832 | tf_op jit(solution)/shard_map/ppermute | solution.py:30
  25.9 7.9 %collective-permute-start.6 = (bf16[3,16,2048]{2,1,0:T(8,128)(2,1)S(1)}, bf16[3,16,2048]{2,1,0:T(8,128)(2,1)S(1)}, u32[]{:S(2)}, u32[]{:S(2)}) collective-permute-start(bf16[3,16,2048]{2,1,0:T(8,128)(2,1)S(1)} %collective-permute-done.2.refs_4_), channel_id=1, source_target_pairs={{0,4},{2,6},{4,0},{6,2},{8,12},{10,14},{12,8},{14,10},{1,5},{3,7},... | collective-permute-start | bytes 589832 | tf_op jit(solution)/shard_map/ppermute | solution.py:30
  30.0 5.0 %collective-permute-start.9 = (bf16[3,16,2048]{2,1,0:T(8,128)(2,1)S(1)}, bf16[3,16,2048]{2,1,0:T(8,128)(2,1)S(1)}, u32[]{:S(2)}, u32[]{:S(2)}) collective-permute-start(bf16[3,16,2048]{2,1,0:T(8,128)(2,1)S(1)} %collective-permute-done.3.refs_5_), channel_id=1, source_target_pairs={{0,2},{2,0},{4,6},{6,4},{8,10},{10,8},{12,14},{14,12},{1,3},{3,1},... | collective-permute-start | bytes 589832 | tf_op jit(solution)/shard_map/ppermute | solution.py:30
  31.2 6.9 %collective-permute-start.7 = (bf16[3,16,2048]{2,1,0:T(8,128)(2,1)S(1)}, bf16[3,16,2048]{2,1,0:T(8,128)(2,1)S(1)}, u32[]{:S(2)}, u32[]{:S(2)}) collective-permute-start(bf16[3,16,2048]{2,1,0:T(8,128)(2,1)S(1)} %collective-permute-done.3.refs_5_), channel_id=1, source_target_pairs={{0,4},{2,6},{4,0},{6,2},{8,12},{10,14},{12,8},{14,10},{1,5},{3,7},... | collective-permute-start | bytes 589832 | tf_op jit(solution)/shard_map/ppermute | solution.py:30
  38.2 4.5 %collective-permute-start.11 = (bf16[3,16,2048]{2,1,0:T(8,128)(2,1)S(1)}, bf16[3,16,2048]{2,1,0:T(8,128)(2,1)S(1)}, u32[]{:S(2)}, u32[]{:S(2)}) collective-permute-start(bf16[3,16,2048]{2,1,0:T(8,128)(2,1)S(1)} %collective-permute-done.9.refs_7_), channel_id=1, source_target_pairs={{0,4},{2,6},{4,0},{6,2},{8,12},{10,14},{12,8},{14,10},{1,5},{3,7},... | collective-permute-start | bytes 589832 | tf_op jit(solution)/shard_map/ppermute | solution.py:30
  39.2 4.8 %collective-permute-start.10 = (bf16[3,16,2048]{2,1,0:T(8,128)(2,1)S(1)}, bf16[3,16,2048]{2,1,0:T(8,128)(2,1)S(1)}, u32[]{:S(2)}, u32[]{:S(2)}) collective-permute-start(bf16[3,16,2048]{2,1,0:T(8,128)(2,1)S(1)} %collective-permute-done.6.refs_8_), channel_id=1, source_target_pairs={{0,2},{2,0},{4,6},{6,4},{8,10},{10,8},{12,14},{14,12},{1,3},{3,1},... | collective-permute-start | bytes 589832 | tf_op jit(solution)/shard_map/ppermute | solution.py:30
  44.9 4.9 %collective-permute-start.12 = (f32[3,288,128]{2,1,0:T(8,128)S(1)}, f32[3,288,128]{2,1,0:T(8,128)S(1)}, u32[]{:S(2)}, u32[]{:S(2)}) collective-permute-start(f32[3,288,128]{2,1,0:T(8,128)S(1)} %get-tuple-element.55), channel_id=1, source_target_pairs={{0,1},{1,0},{2,3},{3,2},{4,5},{5,4},{6,7},{7,6},{8,9},{9,8},{10,11... | collective-permute-start | bytes 1327112 | tf_op jit(solution)/shard_map/ppermute | solution.py:30
  48.4 1.6 %copy-start.1 = (bf16[272,4096]{1,0:T(8,128)(2,1)S(1)}, bf16[272,4096]{1,0:T(8,128)(2,1)}, u32[]{:S(2)}) copy-start(bf16[272,4096]{1,0:T(8,128)(2,1)} %tokens.3) | copy-start | bytes 6684676
  48.4 1.6 %copy-start.4 = (bf16[16,4096]{1,0:T(8,128)(2,1)S(1)}, bf16[16,4096]{1,0:T(8,128)(2,1)}, u32[]{:S(2)}) copy-start(bf16[16,4096]{1,0:T(8,128)(2,1)} %alternates.3) | copy-start | bytes 393220
  49.9 11.5 %copy-start.5 = (bf16[272,128]{1,0:T(8,128)(2,1)S(1)}, bf16[272,128]{1,0:T(8,128)(2,1)}, u32[]{:S(2)}) copy-start(bf16[272,128]{1,0:T(8,128)(2,1)} %refs_4_.1) | copy-start | bytes 208900
  49.9 11.5 %copy-start.6 = (f32[3,3,128]{2,1,0:T(4,128)S(1)}, f32[3,3,128]{2,1,0:T(4,128)}, u32[]{:S(2)}) copy-start(f32[3,3,128]{2,1,0:T(4,128)} %refs_5_) | copy-start | bytes 13828
  49.9 19.0 %copy-start.8 = (s32[16]{0:T(128)S(1)}, s32[16]{0:T(128)}, u32[]{:S(2)}) copy-start(s32[16]{0:T(128)} %refs_0_) | copy-start | bytes 196
  49.9 11.4 %collective-permute-start.13 = (f32[3,288,128]{2,1,0:T(8,128)S(1)}, f32[3,288,128]{2,1,0:T(8,128)S(1)}, u32[]{:S(2)}, u32[]{:S(2)}) collective-permute-start(f32[3,288,128]{2,1,0:T(8,128)S(1)} %add.3), channel_id=1, source_target_pairs={{0,16},{16,0},{1,17},{17,1},{2,18},{18,2},{3,19},{19,3},{4,20},{20... | collective-permute-start | bytes 1327112 | tf_op jit(solution)/shard_map/ppermute | solution.py:30
  51.6 1.4 %collective-permute-start.14 = (f32[288,128]{1,0:T(8,128)S(1)}, f32[288,128]{1,0:T(8,128)S(1)}, u32[]{:S(2)}, u32[]{:S(2)}) collective-permute-start(f32[288,128]{1,0:T(8,128)S(1)} %get-tuple-element.56), channel_id=1, source_target_pairs={{0,1},{1,0},{2,3},{3,2},{4,5},{5,4},{6,7},{7,6},{8,9},{9,8},{10,11... | collective-permute-start | bytes 442376 | tf_op jit(solution)/shard_map/ppermute | solution.py:30
  52.0 1.4 %collective-permute-start.15 = (f32[288,128]{1,0:T(8,128)S(1)}, f32[288,128]{1,0:T(8,128)S(1)}, u32[]{:S(2)}, u32[]{:S(2)}) collective-permute-start(f32[288,128]{1,0:T(8,128)S(1)} %get-tuple-element.57), channel_id=1, source_target_pairs={{0,1},{1,0},{2,3},{3,2},{4,5},{5,4},{6,7},{7,6},{8,9},{9,8},{10,11... | collective-permute-start | bytes 442376 | tf_op jit(solution)/shard_map/ppermute | solution.py:30
  52.2 1.4 %collective-permute-start.16 = (f32[288,128]{1,0:T(8,128)S(1)}, f32[288,128]{1,0:T(8,128)S(1)}, u32[]{:S(2)}, u32[]{:S(2)}) collective-permute-start(f32[288,128]{1,0:T(8,128)S(1)} %get-tuple-element.58), channel_id=1, source_target_pairs={{0,1},{1,0},{2,3},{3,2},{4,5},{5,4},{6,7},{7,6},{8,9},{9,8},{10,11... | collective-permute-start | bytes 442376 | tf_op jit(solution)/shard_map/ppermute | solution.py:30
  61.5 3.4 %collective-permute-start.17 = (f32[168,128]{1,0:T(8,128)S(1)}, f32[168,128]{1,0:T(8,128)S(1)}, u32[]{:S(2)}, u32[]{:S(2)}) collective-permute-start(f32[168,128]{1,0:T(8,128)S(1)} %get-tuple-element.60), channel_id=1, source_target_pairs={{0,2},{2,0},{4,6},{6,4},{8,10},{10,8},{12,14},{14,12},{1,3},{3,1},... | collective-permute-start | bytes 258056 | tf_op jit(solution)/shard_map/ppermute | solution.py:26
  62.8 6.1 %collective-permute-start.18 = (f32[168,128]{1,0:T(8,128)S(1)}, f32[168,128]{1,0:T(8,128)S(1)}, u32[]{:S(2)}, u32[]{:S(2)}) collective-permute-start(f32[168,128]{1,0:T(8,128)S(1)} %get-tuple-element.61), channel_id=1, source_target_pairs={{2,4},{4,2},{6,8},{8,6},{10,12},{12,10},{3,5},{5,3},{7,9},{9,7},{1... | collective-permute-start | bytes 258056 | tf_op jit(solution)/shard_map/ppermute | solution.py:26
  71.3 3.5 %collective-permute-start.19 = (f32[8,288]{1,0:T(8,128)S(1)}, f32[8,288]{1,0:T(8,128)S(1)}, u32[]{:S(2)}, u32[]{:S(2)}) collective-permute-start(f32[8,288]{1,0:T(8,128)S(1)} %mixer.1.mine), channel_id=1, source_target_pairs={{0,1},{1,0},{2,3},{3,2},{4,5},{5,4},{6,7},{7,6},{8,9},{9,8},{10,11... | collective-permute-start | bytes 27656 | tf_op jit(solution)/shard_map/ppermute | solution.py:30
